TPU v7x, 32 devices: a whole 2x2x4 slice. The times are simulated.
32 devices in a mesh: dp: 8 (over z, x), feat: 4 (over y, core).
Axes of the slice: x: 2, y: 2, z: 4, core: 2. Of those that a mesh axis runs over, the one named last changes fastest.
Arguments:
- member_feats: bfloat16 [32768, 256], P(('dp', 'feat')), may hold values from -6 to 6
- labels: int32 [32768], P(('dp', 'feat')), may hold values 0 or 1
- fixed_values: bfloat16 [32768, 2048], P('dp', 'feat'), may hold values from -6 to 6
- fixed_blocks: int32 [32768, 4], P('dp', 'feat'), may hold values from 0 to 511
- fixed_coef: float32 [2048, 512], P('feat'), may hold values from -0.12 to 0.12
- member_coef: float32 [128, 256], P(('dp', 'feat')), may hold values from -0.36 to 0.36
- row_slot: int32 [32768], P(('dp', 'feat')), may hold values from 0 to 2047, as said below
- tile_source: int32 [77824], P(('dp', 'feat')), may hold values from 0 to 2048, as said below
- member_tiles: int32 [128], P(('dp', 'feat')), may hold values from 1 to 16, as said below
Outputs:
- margin: float32 [32768], P(('dp', 'feat'))
- updated_coef: float32 [128, 256], P(('dp', 'feat'))
- fixed_grad: float32 [2048, 512], P('feat')
Inputs may be any that keep to these rules, and one draw needn't show every extreme that they name: `row_slot`: each owner receives the same number of rows, 256, 128 or 64, from every device of its feat column; some owner receives 256 from every device. The rows one device sends to one owner take that owner's slots 0, 1, 2 and so on, each slot once. `tile_source`: every received row appears at exactly one position. An owner's members, in order, take consecutive runs of tiles; a member's rows fill its tiles from the first position on, and the rest of its last tile is padding, as are the tiles past all members. `member_tiles`: A member's tiles are its received rows divided by 128, rounded up; a device's members use at most 19 tiles in all, exactly 19 on the owners that receive 256 rows from every device.
All inputs are finite; a program needn't handle non-finite values. No bound on the sum of `labels` on one device may be relied on, other than what follows from the above.
Results may differ from a plain program's by a relative error of at most 0.0013.
Values may be sent and summed in bfloat16 or wider, within the bound.
No kernel may reach another device: no remote copies, remote signals or barrier semaphores. Data moves between devices by JAX's collectives and lax.ppermute only.
A program may use at most 64 MiB of HBM per device.

v0:
```python
import jax
import jax.numpy as jnp
from jax import lax
from jax.sharding import PartitionSpec as P

CG_ITERS = 2
TILE = 128


ridge_member = 1.0
ridge_fixed = 1.0
highest = lax.Precision.HIGHEST


def member_frame(tile_counts, tile_total, member_count):
    tile_ends = jnp.cumsum(tile_counts)
    positions = jnp.arange(tile_total, dtype=jnp.int32)
    member_index = jnp.sum((positions[:, None] >= tile_ends[None, :]).astype(jnp.int32), axis=1)
    return (member_index[:, None] == jnp.arange(member_count, dtype=jnp.int32)[None, :]).astype(
        jnp.float32
    )


def per_tile(tile_member, values):
    return jnp.dot(tile_member, values, precision=highest, preferred_element_type=jnp.float32)


def per_member(tile_member, values):
    return jnp.dot(tile_member.T, values, precision=highest, preferred_element_type=jnp.float32)


def row_dots(feats_wide, tile_vectors):
    return jnp.einsum("tri,ti->tr", feats_wide, tile_vectors, precision=highest)


def row_sums(row_weights, feats_wide):
    return jnp.einsum("tr,tri->ti", row_weights, feats_wide, precision=highest)


def body(
    member_feats,
    labels,
    fixed_values,
    fixed_blocks,
    fixed_coef,
    member_coef,
    row_slot,
    tile_source,
    member_tiles,
):
    dp_count = lax.axis_size("dp")
    rows_here = member_feats.shape[0]
    width = member_feats.shape[1]
    member_count = member_coef.shape[0]
    block_count = fixed_coef.shape[0]
    capacity = 2 * rows_here // dp_count
    slot_total = dp_count * capacity
    tile_total = tile_source.shape[0] // TILE
    block_index = fixed_blocks[:, 0]
    one_hot = (block_index[:, None] == jnp.arange(block_count, dtype=jnp.int32)[None, :]).astype(
        jnp.float32
    )
    looked_up = jnp.dot(one_hot, fixed_coef, precision=highest, preferred_element_type=jnp.float32)
    partial_value = jnp.sum(fixed_values.astype(jnp.float32) * looked_up, axis=1)
    fixed_score = lax.psum_scatter(partial_value, "feat", scatter_dimension=0, tiled=True)
    send_feats = jnp.zeros((slot_total, width), jnp.bfloat16).at[row_slot].set(member_feats)
    send_score = (
        jnp.zeros((slot_total,), jnp.bfloat16).at[row_slot].set(fixed_score.astype(jnp.bfloat16))
    )
    send_label = (
        jnp.zeros((slot_total,), jnp.bfloat16).at[row_slot].set(labels.astype(jnp.bfloat16))
    )
    got_feats, got_score, got_label = (
        lax.all_to_all(
            send_feats.reshape(dp_count, capacity, width),
            "dp",
            split_axis=0,
            concat_axis=0,
            tiled=True,
        ),
        lax.all_to_all(
            send_score.reshape(dp_count, capacity), "dp", split_axis=0, concat_axis=0, tiled=True
        ),
        lax.all_to_all(
            send_label.reshape(dp_count, capacity), "dp", split_axis=0, concat_axis=0, tiled=True
        ),
    )
    padded_feats = jnp.concatenate(
        [got_feats.reshape(slot_total, width), jnp.zeros((1, width), jnp.bfloat16)], axis=0
    )
    padded_score = jnp.concatenate(
        [got_score.reshape(slot_total), jnp.zeros((1,), jnp.bfloat16)], axis=0
    )
    padded_label = jnp.concatenate(
        [got_label.reshape(slot_total), jnp.zeros((1,), jnp.bfloat16)], axis=0
    )
    feats_wide = padded_feats[tile_source].astype(jnp.float32).reshape(tile_total, TILE, width)
    tile_fixed = padded_score[tile_source].astype(jnp.float32).reshape(tile_total, TILE)
    tile_label = padded_label[tile_source].astype(jnp.float32).reshape(tile_total, TILE)
    tile_member = member_frame(member_tiles, tile_total, member_count)
    logits = tile_fixed + row_dots(feats_wide, per_tile(tile_member, member_coef))
    probability = jax.nn.sigmoid(logits)
    weight = probability * (1.0 - probability)
    gradient = (
        per_member(tile_member, row_sums(tile_label - probability, feats_wide))
        - ridge_member * member_coef
    )
    diagonal = per_member(tile_member, row_sums(weight, feats_wide * feats_wide)) + ridge_member
    step_sum = jnp.zeros_like(member_coef)
    remain = gradient
    scaled = remain / diagonal
    search = scaled
    inner_product = jnp.sum(remain * scaled, axis=1)
    for iteration in range(CG_ITERS):
        projected = row_dots(feats_wide, per_tile(tile_member, search))
        image = (
            per_member(tile_member, row_sums(weight * projected, feats_wide))
            + ridge_member * search
        )
        alpha_step = inner_product / jnp.sum(search * image, axis=1)
        step_sum = step_sum + alpha_step[:, None] * search
        if iteration + 1 < CG_ITERS:
            remain = remain - alpha_step[:, None] * image
            scaled = remain / diagonal
            inner_next = jnp.sum(remain * scaled, axis=1)
            search = scaled + (inner_next / inner_product)[:, None] * search
            inner_product = inner_next
    updated_coef = member_coef + step_sum
    new_scores = row_dots(feats_wide, per_tile(tile_member, updated_coef)).reshape(-1)
    back_scores = (
        jnp.zeros((slot_total + 1,), jnp.float32).at[tile_source].set(new_scores)[:slot_total]
    )
    returned = lax.all_to_all(
        back_scores.reshape(dp_count, capacity), "dp", split_axis=0, concat_axis=0, tiled=True
    )
    member_score = returned.reshape(slot_total)[row_slot]
    margin = fixed_score + member_score
    residual = labels.astype(jnp.float32) - jax.nn.sigmoid(margin)
    group_residual = lax.all_gather(residual, "feat", axis=0, tiled=True)
    weighted_hot = one_hot * group_residual[:, None]
    contribution = jnp.dot(
        weighted_hot.T,
        fixed_values.astype(jnp.float32),
        precision=highest,
        preferred_element_type=jnp.float32,
    )
    summed = lax.psum(contribution, "dp")
    fixed_grad = ridge_fixed * fixed_coef - summed / dp_count
    return (margin, updated_coef, fixed_grad)


def solution(mesh):
    placed = (
        P(("dp", "feat"), None),
        P(("dp", "feat")),
        P("dp", "feat"),
        P("dp", "feat"),
        P("feat", None),
        P(("dp", "feat"), None),
        P(("dp", "feat")),
        P(("dp", "feat")),
        P(("dp", "feat")),
    )
    return jax.shard_map(
        body,
        mesh=mesh,
        in_specs=placed,
        out_specs=(P(("dp", "feat")), P(("dp", "feat"), None), P("feat", None)),
        check_vma=False,
    )
```

profile of v0, /device:TPU:0, one launch (start us, length us, event | category | flops | bytes accessed | tf_op | source)
XLA Modules:
  0.0 260.8 jit_solution(10872461917790779837)
XLA Ops:
  7.2 0.7 broadcast_clamp_fusion
  7.9 6.5 %copy.17 = bf16[4096,512]{0,1:T(8,128)(2,1)} copy(bf16[4096,512]{1,0:T(8,128)(2,1)} %param.11) | data formatting | bytes 8388608 | tf_op args[2]
  14.4 10.0 %multiply_reduce_fusion = f32[4096]{0:T(1024)S(1)} fusion(bf16[4096,512]{0,1:T(8,128)(2,1)} %copy.17, f32[512,512]{1,0:T(8,128)S(1)} %copy-done, s32[4096]{0:T(1024)S(1)} %bitcast.111), kind=kOutput, calls=%fused_computation.10 | convolution fusion | flops 12893286400 | bytes 5275648 | tf_op jit(solution)/shard_map/dot_general | solution.py:63
  24.4 12.7 %all-reduce.1 = f32[4096]{0:T(1024)S(1)} all-reduce(f32[4096]{0:T(1024)S(1)} %multiply_reduce_fusion), channel_id=2, replica_groups=mesh['dp'=8,'feat'=4] {'feat'}, use_global_device_ids=true, to_apply=%region_1.0.clone | all-reduce | flops 4096 | bytes 32768
  38.4 7.6 %scatter_custom_fusion.2 = bf16[2048]{0:T(1024)(128)(2,1)S(1)} fusion(s32[1024]{0:T(1024)S(1)} %get-tuple-element.10, bf16[1024]{0:T(1024)(128)(2,1)S(1)} %dynamic-slice.4, bf16[]{:T(256)} %constant.11.clone.1), kind=kCustom, calls=%fused_computation.96 | custom fusion | bytes 4098 | tf_op jit(solution)/shard_map/scatter | solution.py:68
  46.5 0.7 reduce.2
  47.2 0.6 reshape.204
  47.8 5.8 %all-to-all-start.2 = ((bf16[8,2,128]{2,1,0:T(2,128)(2,1)}), bf16[8,2,128]{2,1,0:T(2,128)(2,1)S(1)}, u32[]{:S(2)}, u32[]{:S(2)}) async-start(bf16[8,2,128]{2,1,0:T(2,128)(2,1)} %reshape.204), calls=%async_computation.2 | async-start | bytes 8192 | tf_op jit(solution)/shard_map/all_to_all | solution.py:81
  53.6 7.6 %scatter_custom_fusion.1 = bf16[2048]{0:T(1024)(128)(2,1)S(1)} fusion(s32[1024]{0:T(1024)S(1)} %get-tuple-element.10, bf16[1024]{0:T(1024)(128)(2,1)S(1)} %convert_element_type.38, bf16[]{:T(256)} %constant.11.clone.1), kind=kCustom, calls=%fused_computation.98 | custom fusion | bytes 4098 | tf_op jit(solution)/shard_map/scatter | solution.py:71
  61.2 0.7 reduce.3
  61.9 0.6 reshape.202
  62.5 6.0 %all-to-all-start.1 = ((bf16[8,2,128]{2,1,0:T(2,128)(2,1)}), bf16[8,2,128]{2,1,0:T(2,128)(2,1)S(1)}, u32[]{:S(2)}, u32[]{:S(2)}) async-start(bf16[8,2,128]{2,1,0:T(2,128)(2,1)} %reshape.202), calls=%async_computation.1 | async-start | bytes 8192 | tf_op jit(solution)/shard_map/all_to_all | solution.py:84
  68.5 6.4 %scatter_custom_fusion = bf16[2048,256]{1,0:T(8,128)(2,1)} fusion(s32[1024]{0:T(1024)S(1)} %get-tuple-element.10, bf16[1024,256]{1,0:T(8,128)(2,1)} %param.9, bf16[]{:T(256)} %constant.11.clone.1), kind=kCustom, calls=%fused_computation.31 | custom fusion | bytes 1049088 | tf_op jit(solution)/shard_map/scatter | solution.py:66
  74.9 6.1 %all-to-all-start = ((bf16[8,256,256]{2,1,0:T(8,128)(2,1)}), bf16[8,256,256]{2,1,0:T(8,128)(2,1)S(1)}, u32[]{:S(2)}, u32[]{:S(2)}) async-start(bf16[8,256,256]{2,1,0:T(8,128)(2,1)} %bitcast.1), calls=%async_computation | async-start | bytes 2097152 | tf_op jit(solution)/shard_map/all_to_all | solution.py:74
  81.9 14.7 %gather_fusion.2 = bf16[2432]{0:T(1024)(128)(2,1)S(1)} fusion(bf16[2049]{0:T(1024)(128)(2,1)S(1)} %get-tuple-element.14, s32[3072]{0:T(1024)S(1)} %pad_clamp_fusion), kind=kCustom, calls=%fused_computation.2 | custom fusion | bytes 19456 | tf_op jit(solution)/shard_map/gather | solution.py:98
  96.6 14.7 %gather_fusion.1 = bf16[2432]{0:T(1024)(128)(2,1)S(1)} fusion(bf16[2049]{0:T(1024)(128)(2,1)S(1)} %get-tuple-element.15, s32[3072]{0:T(1024)S(1)} %pad_clamp_fusion), kind=kCustom, calls=%fused_computation.1 | custom fusion | bytes 19456 | tf_op jit(solution)/shard_map/gather | solution.py:99
  111.4 7.8 %gather_fusion = bf16[2432,256]{1,0:T(8,128)(2,1)S(1)} fusion(bf16[2049,256]{1,0:T(8,128)(2,1)S(1)} %concatenate.9, s32[3072]{0:T(1024)S(1)} %pad_clamp_fusion), kind=kCustom, calls=%fused_computation | custom fusion | bytes 2500096 | tf_op jit(solution)/shard_map/gather | solution.py:97
  119.2 1.1 fusion.28
  120.3 1.4 fusion.7
  122.0 0.6 fusion.42
  123.1 1.1 fusion.26
  124.2 0.6 fusion.39
  125.7 1.1 fusion.24
  128.1 1.1 fusion.22
  129.2 12.4 %scatter_custom_fusion.3 = f32[2049]{0:T(1024)S(1)} fusion(s32[2432]{0:T(1024)S(1)} %compare_select_fusion, f32[2432]{0:T(1024)S(1)} %bitcast.110, f32[]{:T(128)} %constant.8.clone.1), kind=kCustom, calls=%fused_computation.84 | custom fusion | bytes 8200 | tf_op jit(solution)/shard_map/scatter | solution.py:131
  141.6 12.0 %all_to_all.34 = f32[8,1,256]{2,1,0:T(1,128)S(1)} all-to-all(f32[8,1,256]{2,1,0:T(1,128)S(1)} %bitcast.105), channel_id=1, replica_groups=mesh['dp'=8,'feat'=4] {'dp'}, dimensions={0} | all-to-all | bytes 16384 | tf_op jit(solution)/shard_map/all_to_all | solution.py:133
  153.6 6.1 %gather_fusion.3 = f32[1024]{0:T(1024)S(1)} fusion(f32[2048]{0:T(1024)S(1)} %bitcast.95, s32[1024]{0:T(1024)S(1)} %get-tuple-element.9), kind=kCustom, calls=%fused_computation.3 | custom fusion | bytes 12288 | tf_op jit(solution)/shard_map/gather | solution.py:136
  159.8 0.6 divide_subtract_fusion
  160.4 5.5 %all_gather.3 = f32[4096]{0:T(1024)S(1)} all-gather(f32[1024]{0:T(1024)S(1)} %get-tuple-element.5), channel_id=1, replica_groups=mesh['dp'=8,'feat'=4] {'feat'}, dimensions={0}, use_global_device_ids=true | all-gather | bytes 20480 | tf_op jit(solution)/shard_map/all_gather | solution.py:139
  165.8 11.0 %fusion = f32[512,512]{1,0:T(8,128)} fusion(bf16[4096,512]{1,0:T(8,128)(2,1)} %param.11, f32[4096]{0:T(1024)S(1)} %all_gather.3, s32[4096]{0:T(1024)S(1)} %bitcast.112), kind=kOutput, calls=%fused_computation.8 | convolution fusion | flops 12889096192 | bytes 5275648 | tf_op jit(solution)/shard_map/dot_general | solution.py:141
  176.9 74.7 %all-reduce.4.cloned.1.call-done = f32[512,512]{1,0:T(8,128)} async-done(((f32[512,512]{1,0:T(8,128)}), f32[512,512]{1,0:T(8,128)}) %all-reduce.4.cloned.1.call-update) | async-done | bytes 1048592 | tf_op jit(solution)/shard_map/psum | solution.py:147
  251.6 2.4 multiply_subtract_fusion
  (59 shorter events, 5.1 us)
Async XLA Ops:
  7.9 6.5 %copy-start = (f32[512,512]{1,0:T(8,128)S(1)}, f32[512,512]{1,0:T(8,128)}, u32[]{:S(2)}) copy-start(f32[512,512]{1,0:T(8,128)} %param.13) | copy-start | bytes 3145732
  7.9 6.5 %copy-start.5 = (s32[4096,1]{0,1:T(1,128)S(1)}, s32[4096,1]{0,1:T(1,128)}, u32[]{:S(2)}) copy-start(s32[4096,1]{0,1:T(1,128)} %param.12) | copy-start | bytes 49156
  14.4 22.7 %copy-start.7 = (u32[32]{0:T(128)S(1)}, u32[32]{0:T(128)}, u32[]{:S(2)}) copy-start(u32[32]{0:T(128)} %constant.35) | copy-start | bytes 388
  14.4 39.2 %copy-start.1 = (s32[1024]{0:T(1024)S(1)}, s32[1024]{0:T(1024)}, u32[]{:S(2)}) copy-start(s32[1024]{0:T(1024)} %param.10) | copy-start | bytes 12292
  47.8 14.7 %all-to-all-start.2 = ((bf16[8,2,128]{2,1,0:T(2,128)(2,1)}), bf16[8,2,128]{2,1,0:T(2,128)(2,1)S(1)}, u32[]{:S(2)}, u32[]{:S(2)}) async-start(bf16[8,2,128]{2,1,0:T(2,128)(2,1)} %reshape.204), calls=%async_computation.2 | async-start | bytes 8192 | tf_op jit(solution)/shard_map/all_to_all | solution.py:81
  62.5 12.4 %all-to-all-start.1 = ((bf16[8,2,128]{2,1,0:T(2,128)(2,1)}), bf16[8,2,128]{2,1,0:T(2,128)(2,1)S(1)}, u32[]{:S(2)}, u32[]{:S(2)}) async-start(bf16[8,2,128]{2,1,0:T(2,128)(2,1)} %reshape.202), calls=%async_computation.1 | async-start | bytes 8192 | tf_op jit(solution)/shard_map/all_to_all | solution.py:84
  74.9 6.4 %copy-start.6 = (s32[4]{0:T(128)S(1)}, s32[4]{0:T(128)}, u32[]{:S(2)}) copy-start(s32[4]{0:T(128)} %param.17) | copy-start | bytes 52
  74.9 6.6 %copy-start.2 = (s32[2432]{0:T(1024)S(1)}, s32[2432]{0:T(1024)}, u32[]{:S(2)}) copy-start(s32[2432]{0:T(1024)} %param.16) | copy-start | bytes 29188
  74.9 6.7 %copy-start.3 = (f32[4,256]{1,0:T(4,128)S(1)}, f32[4,256]{1,0:T(4,128)}, u32[]{:S(2)}) copy-start(f32[4,256]{1,0:T(4,128)} %param.14) | copy-start | bytes 12292
  74.9 36.5 %all-to-all-start = ((bf16[8,256,256]{2,1,0:T(8,128)(2,1)}), bf16[8,256,256]{2,1,0:T(8,128)(2,1)S(1)}, u32[]{:S(2)}, u32[]{:S(2)}) async-start(bf16[8,256,256]{2,1,0:T(8,128)(2,1)} %bitcast.1), calls=%async_computation | async-start | bytes 2097152 | tf_op jit(solution)/shard_map/all_to_all | solution.py:74
  81.0 170.6 %all-reduce.4.cloned.1.call-start = ((), (), s32[]{:S(2)}) async-start(), calls=%async_computation.4 | async-start | bytes 2097152 | tf_op jit(solution)/shard_map/psum | solution.py:147
  127.9 31.9 %copy-start.4 = (f32[4,256]{1,0:T(4,128)}, f32[4,256]{1,0:T(4,128)S(1)}, u32[]{:S(2)}) copy-start(f32[4,256]{1,0:T(4,128)S(1)} %add_add_fusion) | copy-start | bytes 12292
Sparse Core Ops, SparseCore 0:
  177.0 74.5 all-reduce.3
where the time goes:
time: 261 us
  local copies, waits for them, and re-layouts  86.3 us (33%)
  waiting for transfers between devices  74.7 us (29%)
  matrix products  30.6 us (12%)
  blocking collectives  30.2 us (12%)
  starting transfers between devices  18.2 us (7%)
  between operations  15 us (6%)
  other arithmetic  5.88 us (2%)
    psum x1, waiting for transfers between devices, body(): summed = lax.psum(contribution, 'dp')  74.7 us
    scatter x2, local copies, waits for them, and re-layouts, body(): jnp.zeros((slot_total,), jnp.bfloat16).at[row_slot]  15.2 us
    gather x1, local copies, waits for them, and re-layouts, body(): padded_score[tile_source].astype(jnp.float32).reshape(tile_total, TILE)  14.7 us
    gather x1, local copies, waits for them, and re-layouts, body(): padded_label[tile_source].astype(jnp.float32).reshape(tile_total, TILE)  14.7 us
    unnamed x1, blocking collectives  12.7 us
    scatter x1, local copies, waits for them, and re-layouts, body(): jnp.zeros((slot_total + 1,), jnp.float32).at[tile_source].set(new_scores)  12.4 us
    all_to_all x1, blocking collectives, body(): lax.all_to_all(back_scores.reshape(dp_count, capacity), 'dp', split_axis=...  12 us
    dot_general x1, matrix products, body(): jnp.dot(weighted_hot.T, fixed_values.astype(jnp.float32), precision=highe...  11 us
  transfers between devices with their start and end apart: 4, of which 1 were waited for; matrix products, arithmetic and copies ran while one was open for 17% of the time, Pallas kernels for 0%

commit v1 on v0

v1 whole, which is shorter than its diff:
```python
import jax
import jax.numpy as jnp
from jax import lax
from jax.experimental import pallas as pl
from jax.experimental.pallas import tpu as pltpu
from jax.sharding import PartitionSpec as P

CG_ITERS = 2
TILE = 128

ridge_member = 1.0
ridge_fixed = 1.0
bf16 = jnp.bfloat16
f32 = jnp.float32
f16 = jnp.float16


def split(value, parts):
    out = []
    for _ in range(parts):
        piece = value.astype(bf16)
        out.append(piece)
        value = value - piece.astype(f32)
    return out


def dot_nt(a, b):
    return lax.dot_general(a, b, (((1,), (1,)), ((), ())), preferred_element_type=f32)


def dot_nn(a, b):
    return jnp.dot(a, b, preferred_element_type=f32)


def rows_iota(shape):
    return lax.broadcasted_iota(jnp.int32, shape, 0)


def hot(index, count):
    return rows_iota((count, index.shape[1])) == index


def sigmoid(x):
    return 1.0 / (1.0 + jnp.exp(-x))


def partial_kernel(values_ref, block_ref, coef_ref, out_ref, high_ref, low_ref):
    @pl.when(pl.program_id(0) == 0)
    def _():
        high, low = split(coef_ref[...], 2)
        high_ref[...] = high
        low_ref[...] = low

    values = values_ref[...]
    product = dot_nt(high_ref[...], values) + dot_nt(low_ref[...], values)
    mask = hot(block_ref[...], product.shape[0])
    out_ref[...] = jnp.sum(jnp.where(mask, product, 0.0), axis=0, keepdims=True)


def partial_scores(fixed_values, block_row, fixed_coef):
    rows, width = fixed_values.shape
    blocks = fixed_coef.shape[0]
    step = min(512, rows)
    return pl.pallas_call(
        partial_kernel,
        grid=(rows // step,),
        in_specs=[
            pl.BlockSpec((step, width), lambda i: (i, 0)),
            pl.BlockSpec((1, step), lambda i: (0, i)),
            pl.BlockSpec((blocks, width), lambda i: (0, 0)),
        ],
        out_specs=pl.BlockSpec((1, step), lambda i: (0, i)),
        out_shape=jax.ShapeDtypeStruct((1, rows), f32),
        scratch_shapes=[pltpu.VMEM((blocks, width), bf16)] * 2,
        cost_estimate=pl.CostEstimate(
            flops=4 * rows * blocks * width,
            bytes_accessed=2 * rows * width + 4 * blocks * width,
            transcendentals=0,
        ),
        name="partial_scores",
    )(fixed_values, block_row, fixed_coef)


def grad_kernel(values_ref, block_ref, residual_ref, out_ref):
    high, low = split(residual_ref[...], 2)
    mask = hot(block_ref[...], out_ref.shape[0])
    zero = jnp.zeros((), f32)
    left_high = jnp.where(mask, high.astype(f32), zero).astype(bf16)
    left_low = jnp.where(mask, low.astype(f32), zero).astype(bf16)
    values = values_ref[...]
    total = dot_nn(left_high, values) + dot_nn(left_low, values)

    @pl.when(pl.program_id(0) == 0)
    def _():
        out_ref[...] = total

    @pl.when(pl.program_id(0) > 0)
    def _():
        out_ref[...] += total


def gradient_partial(fixed_values, block_row, residual_row, blocks):
    rows, width = fixed_values.shape
    step = min(512, rows)
    return pl.pallas_call(
        grad_kernel,
        grid=(rows // step,),
        in_specs=[
            pl.BlockSpec((step, width), lambda i: (i, 0)),
            pl.BlockSpec((1, step), lambda i: (0, i)),
            pl.BlockSpec((1, step), lambda i: (0, i)),
        ],
        out_specs=pl.BlockSpec((blocks, width), lambda i: (0, 0)),
        out_shape=jax.ShapeDtypeStruct((blocks, width), f32),
        cost_estimate=pl.CostEstimate(
            flops=4 * rows * blocks * width,
            bytes_accessed=2 * rows * width + 4 * blocks * width,
            transcendentals=0,
        ),
        name="gradient_partial",
    )(fixed_values, block_row, residual_row)


def pack_kernel(feats_ref, slot_ref, out_ref):
    count = out_ref.shape[0]
    start = pl.program_id(0) * count
    mask = (rows_iota((count, slot_ref.shape[1])) + start) == slot_ref[...]
    one_hot = jnp.where(mask, 1.0, 0.0).astype(bf16)
    out_ref[...] = dot_nn(one_hot, feats_ref[...]).astype(bf16)


def pack_feats(member_feats, slot_row, slot_total):
    rows, width = member_feats.shape
    step = min(512, slot_total)
    return pl.pallas_call(
        pack_kernel,
        grid=(slot_total // step,),
        in_specs=[
            pl.BlockSpec((rows, width), lambda i: (0, 0)),
            pl.BlockSpec((1, rows), lambda i: (0, 0)),
        ],
        out_specs=pl.BlockSpec((step, width), lambda i: (i, 0)),
        out_shape=jax.ShapeDtypeStruct((slot_total, width), bf16),
        cost_estimate=pl.CostEstimate(
            flops=2 * rows * slot_total * width,
            bytes_accessed=2 * rows * width + 2 * slot_total * width,
            transcendentals=0,
        ),
        name="pack_feats",
    )(member_feats, slot_row)


def message_kernel(capacity, parts_refs, label_ref, slot_ref, fixed_ref, out_ref):
    fixed = parts_refs[0][...]
    for part in parts_refs[1:]:
        fixed = fixed + part[...]
    fixed_ref[...] = fixed
    destinations = out_ref.shape[1]
    slot = slot_ref[...]
    owner = slot // capacity
    owner_hot = hot(owner, destinations)
    place_hot = jnp.where(hot(slot - owner * capacity, capacity), 1.0, 0.0).astype(bf16)
    score = fixed.astype(bf16).astype(f32)
    label = label_ref[...].astype(f32)
    out_ref[0] = dot_nt(jnp.where(owner_hot, score, 0.0).astype(bf16), place_hot).astype(bf16)
    out_ref[1] = dot_nt(jnp.where(owner_hot, label, 0.0).astype(bf16), place_hot).astype(bf16)


def build_message(parts, label_row, slot_row, dp_count, capacity):
    rows = slot_row.shape[1]

    def kernel(*refs):
        message_kernel(capacity, refs[: len(parts)], *refs[len(parts) :])

    return pl.pallas_call(
        kernel,
        out_shape=(
            jax.ShapeDtypeStruct((1, rows), f32),
            jax.ShapeDtypeStruct((2, dp_count, capacity), bf16),
        ),
        name="build_message",
    )(*parts, label_row, slot_row)


def slot_member_kernel(tiles_ref, source_ref, out_ref):
    slots, capacity = out_ref.shape
    source = source_ref[...]
    position = lax.broadcasted_iota(jnp.int32, source.shape, 1) // TILE
    member = jnp.zeros(source.shape, jnp.int32)
    end = jnp.int32(0)
    for m in range(tiles_ref.shape[0]):
        end = end + tiles_ref[m]
        member = member + (position >= end).astype(jnp.int32)
    sender = source // capacity
    sender_hot = jnp.where(hot(sender, slots), member.astype(f32) + 1.0, 0.0).astype(bf16)
    place_hot = jnp.where(hot(source - sender * capacity, capacity), 1.0, 0.0).astype(bf16)
    out_ref[...] = dot_nt(sender_hot, place_hot) - 1.0


def slot_members(member_tiles, source_row, dp_count, capacity):
    return pl.pallas_call(
        slot_member_kernel,
        in_specs=[
            pl.BlockSpec(memory_space=pltpu.SMEM),
            pl.BlockSpec(memory_space=pltpu.VMEM),
        ],
        out_specs=pl.BlockSpec(memory_space=pltpu.VMEM),
        out_shape=jax.ShapeDtypeStruct((dp_count, capacity), f32),
        name="slot_members",
    )(member_tiles, source_row)


def solve_kernel(feats_ref, score_ref, label_ref, member_ref, coef_ref, updated_ref, scores_ref):
    feats = feats_ref[...]
    coef = coef_ref[...]
    count = coef.shape[0]
    slots = feats.shape[0]
    own = rows_iota((count, slots)).astype(f32) == member_ref[...]

    def pick(vectors):
        high, low = split(vectors, 2)
        both = dot_nt(jnp.concatenate([high, low], axis=0), feats)
        each = both[:count] + both[count:]
        return jnp.sum(jnp.where(own, each, 0.0), axis=0, keepdims=True)

    def spread(row_weights):
        high, low = split(jnp.where(own, row_weights, 0.0), 2)
        return jnp.concatenate([high, low], axis=0)

    def gather(row_weights):
        both = dot_nn(spread(row_weights), feats)
        return both[:count] + both[count:]

    base = pick(coef)
    logits = score_ref[...].astype(f32) + base
    probability = sigmoid(logits)
    weight = probability * (1.0 - probability)
    gradient = gather(label_ref[...].astype(f32) - probability) - ridge_member * coef
    wide = feats.astype(f32)
    square_high, square_low = split(wide * wide, 2)
    weights = spread(weight)
    both = dot_nn(weights, square_high) + dot_nn(weights, square_low)
    diagonal = both[:count] + both[count:] + ridge_member
    step_sum = jnp.zeros_like(coef)
    new_scores = base
    remain = gradient
    scaled = remain / diagonal
    search = scaled
    inner_product = jnp.sum(remain * scaled, axis=1, keepdims=True)
    for iteration in range(CG_ITERS):
        projected = pick(search)
        if iteration + 1 < CG_ITERS:
            image = gather(weight * projected) + ridge_member * search
            curvature = jnp.sum(search * image, axis=1, keepdims=True)
        else:
            row_part = jnp.where(own, weight * projected * projected, 0.0)
            curvature = jnp.sum(row_part, axis=1, keepdims=True) + ridge_member * jnp.sum(
                search * search, axis=1, keepdims=True
            )
        alpha_step = inner_product / curvature
        step_sum = step_sum + alpha_step * search
        row_alpha = jnp.sum(jnp.where(own, alpha_step, 0.0), axis=0, keepdims=True)
        new_scores = new_scores + row_alpha * projected
        if iteration + 1 < CG_ITERS:
            remain = remain - alpha_step * image
            scaled = remain / diagonal
            inner_next = jnp.sum(remain * scaled, axis=1, keepdims=True)
            search = scaled + (inner_next / inner_product) * search
            inner_product = inner_next
    updated_ref[...] = coef + step_sum
    scores_ref[...] = new_scores


def solve_members(feats, score_row, label_row, member_row, member_coef):
    slots, width = feats.shape
    return pl.pallas_call(
        solve_kernel,
        out_shape=(
            jax.ShapeDtypeStruct(member_coef.shape, f32),
            jax.ShapeDtypeStruct((1, slots), f32),
        ),
        name="solve_members",
    )(feats, score_row, label_row, member_row, member_coef)


def margin_kernel(returned_ref, slot_ref, fixed_ref, label_ref, margin_ref, residual_ref):
    owners, capacity = returned_ref.shape
    slot = slot_ref[...]
    owner = slot // capacity
    place_hot = jnp.where(hot(slot - owner * capacity, capacity), 1.0, 0.0).astype(bf16)
    looked_up = jnp.zeros((owners, slot.shape[1]), f32)
    for piece in reversed(split(returned_ref[...], 3)):
        looked_up = looked_up + dot_nn(piece, place_hot)
    score = jnp.sum(jnp.where(hot(owner, owners), looked_up, 0.0), axis=0, keepdims=True)
    margin = fixed_ref[...] + score
    margin_ref[...] = margin
    residual_ref[...] = label_ref[...].astype(f32) - sigmoid(margin)


def margins(returned, slot_row, fixed_row, label_row):
    out = jax.ShapeDtypeStruct(slot_row.shape, f32)
    return pl.pallas_call(margin_kernel, out_shape=(out, out), name="margins")(
        returned, slot_row, fixed_row, label_row
    )


def swap(value, axis, offset, count):
    return lax.ppermute(value, axis, [(i, i ^ offset) for i in range(count)])


def pick_index(value, index, axis=0):
    return lax.dynamic_index_in_dim(value, index, axis, keepdims=False)


def reduce_chunks(partial, dp_count):
    half = dp_count // 2
    if half > 4 or dp_count % 2:
        sent = lax.all_to_all(partial.astype(f16), "dp", 0, 0, tiled=True)
        return jnp.sum(sent.astype(f32), axis=0)
    me = lax.axis_index("dp")
    side = me % 2
    place = me // 2
    pairs = partial.reshape((half, 2) + partial.shape[1:])
    other = swap(pick_index(pairs, 1 - side, 1).astype(f16), "dp", 1, dp_count)
    kept = pick_index(pairs, side, 1) + other.astype(f32)
    sends = kept.astype(f16)
    total = pick_index(kept, place)
    for k in range(1, half):
        got = swap(pick_index(sends, place ^ k), "dp", 2 * k, dp_count)
        total = total + got.astype(f32)
    return total


def spread_chunks(chunk, dp_count, coef, scale):
    rows, width = chunk.shape
    half = dp_count // 2
    if half > 4 or dp_count % 2:
        whole = lax.all_gather(chunk, "dp", axis=0, tiled=True)
        return ridge_fixed * coef - whole.astype(f32) * scale
    me = lax.axis_index("dp")
    side = me % 2
    place = me // 2
    other = swap(chunk, "dp", 1, dp_count)
    pair = jnp.where(
        side == 0, jnp.concatenate([chunk, other]), jnp.concatenate([other, chunk])
    )
    out = jnp.zeros(coef.shape, f32)
    for k in range(half):
        got = pair if k == 0 else swap(pair, "dp", 2 * k, dp_count)
        at = (place ^ k) * 2 * rows
        own_coef = lax.dynamic_slice_in_dim(coef, at, 2 * rows, 0)
        out = lax.dynamic_update_slice_in_dim(
            out, ridge_fixed * own_coef - got.astype(f32) * scale, at, 0
        )
    return out


def body(
    member_feats,
    labels,
    fixed_values,
    fixed_blocks,
    fixed_coef,
    member_coef,
    row_slot,
    tile_source,
    member_tiles,
):
    dp_count = lax.axis_size("dp")
    feat_count = lax.axis_size("feat")
    feat = lax.axis_index("feat")
    rows_here = member_feats.shape[0]
    blocks, block_width = fixed_coef.shape
    capacity = 2 * rows_here // dp_count
    slot_total = dp_count * capacity
    group_rows = fixed_values.shape[0]

    slot_row = row_slot.reshape(1, rows_here)
    label_row = labels.reshape(1, rows_here)
    block_row = fixed_blocks.reshape(1, group_rows)

    send_feats = pack_feats(member_feats, slot_row, slot_total)
    got_feats = lax.all_to_all(
        send_feats.reshape(dp_count, capacity, -1), "dp", split_axis=0, concat_axis=0, tiled=True
    ).reshape(slot_total, -1)
    member_row = slot_members(
        member_tiles, tile_source.reshape(1, -1), dp_count, capacity
    ).reshape(1, slot_total)

    partial = partial_scores(fixed_values, block_row, fixed_coef)

    def rows_of(shard):
        return lax.dynamic_slice_in_dim(partial, shard * rows_here, rows_here, 1)

    parts = [rows_of(feat)] + [
        swap(rows_of(feat ^ k), "feat", k, feat_count) for k in range(1, feat_count)
    ]
    fixed_row, message = build_message(parts, label_row, slot_row, dp_count, capacity)
    got = lax.all_to_all(message, "dp", split_axis=1, concat_axis=1, tiled=True)
    score_row = got[0].reshape(1, slot_total)
    tile_label = got[1].reshape(1, slot_total)

    updated_coef, new_scores = solve_members(
        got_feats, score_row, tile_label, member_row, member_coef
    )
    returned = lax.all_to_all(
        new_scores.reshape(dp_count, capacity), "dp", split_axis=0, concat_axis=0, tiled=True
    )
    margin, residual = margins(returned, slot_row, fixed_row, label_row)

    group = jnp.zeros((feat_count, rows_here), f32)
    for k in range(feat_count):
        got_residual = residual if k == 0 else swap(residual, "feat", k, feat_count)
        group = lax.dynamic_update_slice_in_dim(group, got_residual, feat ^ k, 0)
    contribution = gradient_partial(
        fixed_values, block_row, group.reshape(1, group_rows), blocks
    )
    summed = reduce_chunks(
        contribution.reshape(dp_count, blocks // dp_count, block_width) * (1.0 / dp_count), dp_count
    )
    fixed_grad = spread_chunks(summed.astype(f16), dp_count, fixed_coef, 1.0)
    return (margin.reshape(rows_here), updated_coef, fixed_grad)


def solution(mesh):
    placed = (
        P(("dp", "feat"), None),
        P(("dp", "feat")),
        P("dp", "feat"),
        P("dp", "feat"),
        P("feat", None),
        P(("dp", "feat"), None),
        P(("dp", "feat")),
        P(("dp", "feat")),
        P(("dp", "feat")),
    )
    return jax.shard_map(
        body,
        mesh=mesh,
        in_specs=placed,
        out_specs=(P(("dp", "feat")), P(("dp", "feat"), None), P("feat", None)),
        check_vma=False,
    )
```

time: 261 us -> 129 us (0.49)
  local copies, waits for them, and re-layouts: 86.3 us -> 10 us
  Pallas kernels: 0 us -> 32 us
  matrix products: 30.6 us -> 0 us
  waiting for transfers between devices: 74.7 us -> 48.4 us
  blocking collectives: 30.2 us -> 9.93 us
  between operations: 15 us -> 0.83 us
  starting transfers between devices: 18.2 us -> 24.6 us
  other arithmetic: 5.88 us -> 1.77 us
    psum x1 -> x0, waiting for transfers between devices: 74.7 us -> none  [body(): summed = lax.psum(contribution, 'dp')]
    gather x4 -> x0, local copies, waits for them, and re-layouts: 43.3 us -> none  [the longest x1 14.7 us: body(): padded_score[tile_source].astype(jnp.float32).reshape(tile_total, TILE)]
    scatter x4 -> x0, local copies, waits for them, and re-layouts: 33.9 us -> none  [the longest x2 15.2 us: body(): jnp.zeros((slot_total,), jnp.bfloat16).at[row_slot]]
    pallas_call x0 -> x7, Pallas kernels: none -> 32 us  [the longest x1 9.32 us: gradient_partial(): pl.pallas_call(grad_kernel, grid=(rows // step,), in_specs=[pl.BlockSpec(...]
    dot_general x18 -> x0, matrix products: 30.6 us -> none  [the longest x1 11 us: body(): jnp.dot(weighted_hot.T, fixed_values.astype(jnp.float32), precision=highe...]
    ppermute x0 -> x14, waiting for transfers between devices: none -> 24.5 us  [swap(): return lax.ppermute(value, axis, [(i, i ^ offset) for i in range(count)])]
    all_to_all x3 -> x2, waiting for transfers between devices: 0.01 us -> 23.9 us  [the longest x1 21.2 us: body(): lax.all_to_all(send_feats.reshape(dp_count, capacity, -1), 'dp', split_ax...]
    ppermute x0 -> x14, starting transfers between devices: none -> 15.2 us  [swap(): return lax.ppermute(value, axis, [(i, i ^ offset) for i in range(count)])]
  transfers between devices with their start and end apart: 4 -> 16, of which waited for: 1 -> 10; matrix products, arithmetic and copies ran while one was open for 17% -> 3% of each run, Pallas kernels for 0% -> 4%
where the time goes in v1:
time: 129 us; the launch traced here: 127 us
  waiting for transfers between devices  48.4 us (38%)
  Pallas kernels  32 us (25%)
  starting transfers between devices  24.6 us (19%)
  local copies, waits for them, and re-layouts  10 us (8%)
  blocking collectives  9.93 us (8%)
  other arithmetic  1.77 us (1%)
    ppermute x14, waiting for transfers between devices, swap(): return lax.ppermute(value, axis, [(i, i ^ offset) for i in range(count)])  24.5 us
    all_to_all x1, waiting for transfers between devices, body(): lax.all_to_all(send_feats.reshape(dp_count, capacity, -1), 'dp', split_ax...  21.2 us
    ppermute x14, starting transfers between devices, swap(): return lax.ppermute(value, axis, [(i, i ^ offset) for i in range(count)])  15.2 us
    all_to_all x1, blocking collectives, body(): lax.all_to_all(new_scores.reshape(dp_count, capacity), 'dp', split_axis=0...  9.93 us
    pallas_call x1, Pallas kernels, gradient_partial(): pl.pallas_call(grad_kernel, grid=(rows // step,), in_specs=[pl.BlockSpec(...  9.32 us
    pallas_call x1, Pallas kernels, partial_scores(): pl.pallas_call(partial_kernel, grid=(rows // step,), in_specs=[pl.BlockSp...  9.23 us
    all_to_all x1, starting transfers between devices, body(): got = lax.all_to_all(message, 'dp', split_axis=1, concat_axis=1, tiled=True)  5.8 us
    unnamed x17, local copies, waits for them, and re-layouts  5.05 us
  transfers between devices with their start and end apart: 16, of which 10 were waited for; matrix products, arithmetic and copies ran while one was open for 3% of the time, Pallas kernels for 4%

profile of v1, /device:TPU:0, one launch (start us, length us, event | category | flops | bytes accessed | tf_op | source)
XLA Modules:
  0.0 127.5 jit_solution(15625353755704318373)
XLA Ops:
  0.7 9.2 %partial_scores.1 = f32[1,4096]{1,0:T(1,128)} custom-call(bf16[4096,512]{1,0:T(8,128)(2,1)} %values_ref.3, s32[1,4096]{1,0:T(1,128)} %bitcast.55, f32[512,512]{1,0:T(8,128)} %coef_ref.2), custom_call_target="tpu_custom_call" | custom-call | flops 4294967296 | bytes 5242880 | tf_op jit(solution)/shard_map/partial_scores/pallas_call | solution.py:64
  9.9 1.3 %constant_dynamic-slice_fusion = (f32[1,1024]{1,0:T(1,128)S(1)}, f32[1,1024]{1,0:T(1,128)S(1)}, f32[1,1024]{1,0:T(1,128)S(1)}, f32[1,1024]{1,0:T(1,128)}) fusion(f32[1,4096]{1,0:T(1,128)} %partial_scores.1, s32[]{:T(128)S(6)} %select_n.86, s32[]{:T(128)S(6)} %select_n.85, s32[]{:T(128)S(6)} %select_n.84, s32[]{:T(128)S(6)} %select_n.83), kind=kLoop, calls=%fused_computation.17 | loop fusion | bytes 32784 | tf_op jit(solution)/shard_map/dynamic_slice | solution.py:393
  11.7 2.5 %collective-permute-start.1 = (f32[1,1024]{1,0:T(1,128)S(1)}, f32[1,1024]{1,0:T(1,128)S(1)}, u32[]{:S(2)}, u32[]{:S(2)}) collective-permute-start(f32[1,1024]{1,0:T(1,128)S(1)} %get-tuple-element.23), channel_id=1, source_target_pairs={{0,2},{1,3},{2,0},{3,1},{4,6},{5,7},{6,4},{7,5},{8,10},{9,11},{10,... | collective-permute-start | bytes 12296 | tf_op jit(solution)/shard_map/ppermute | solution.py:308
  14.4 1.5 %collective-permute-done.1.refs_2_ = f32[1,1024]{1,0:T(1,128)S(1)} collective-permute-done((f32[1,1024]{1,0:T(1,128)S(1)}, f32[1,1024]{1,0:T(1,128)S(1)}, u32[]{:S(2)}, u32[]{:S(2)}) %collective-permute-start.1) | collective-permute-done | bytes 4128 | tf_op jit(solution)/shard_map/ppermute | solution.py:308
  15.8 1.4 %collective-permute-done.2.refs_3_ = f32[1,1024]{1,0:T(1,128)S(1)} collective-permute-done((f32[1,1024]{1,0:T(1,128)S(1)}, f32[1,1024]{1,0:T(1,128)S(1)}, u32[]{:S(2)}, u32[]{:S(2)}) %collective-permute-start.2) | collective-permute-done | bytes 4128 | tf_op jit(solution)/shard_map/ppermute | solution.py:308
  17.9 1.7 %build_message.1 = (f32[1,1024]{1,0:T(1,128)}, bf16[2,8,256]{2,1,0:T(8,128)(2,1)}) custom-call(f32[1,1024]{1,0:T(1,128)} %get-tuple-element.25.refs_0_, f32[1,1024]{1,0:T(1,128)} %copy-done.4, f32[1,1024]{1,0:T(1,128)} %copy-done.5, f32[1,1024]{1,0:T(1,128)} %copy-done.6, s32[1,1024]{1,0:T(1,128)} %bitcast.52, s32[1,1024]{1,0:T(1,128)} %bitcast.49), custom_call_target="tpu_custom_call" | custom-call | tf_op jit(solution)/shard_map/build_message/pallas_call | solution.py:175
  19.6 1.3 %copy.12 = bf16[2,8,256]{2,0,1:T(2,128)(2,1)} copy(bf16[2,8,256]{2,1,0:T(8,128)(2,1)} %get-tuple-element.9) | data formatting | bytes 16384 | tf_op jit(solution)/shard_map/build_message/pallas_call | solution.py:175
  20.9 5.8 %all-to-all-start.1 = ((bf16[2,8,256]{2,0,1:T(2,128)(2,1)}), bf16[2,8,256]{2,0,1:T(2,128)(2,1)S(1)}, u32[]{:S(2)}, u32[]{:S(2)}) async-start(bf16[2,8,256]{2,0,1:T(2,128)(2,1)} %copy.12), calls=%async_computation.1 | async-start | bytes 16384 | tf_op jit(solution)/shard_map/all_to_all | solution.py:399
  26.7 3.8 %pack_feats.1 = bf16[2048,256]{1,0:T(8,128)(2,1)} custom-call(bf16[1024,256]{1,0:T(8,128)(2,1)} %feats_ref.1, s32[1,1024]{1,0:T(1,128)} %bitcast.50), custom_call_target="tpu_custom_call" | custom-call | flops 1073741824 | bytes 1572864 | tf_op jit(solution)/shard_map/pack_feats/pallas_call | solution.py:135
  30.5 2.7 %all-to-all-done.1 = bf16[2,8,256]{2,0,1:T(2,128)(2,1)S(1)} async-done(((bf16[2,8,256]{2,0,1:T(2,128)(2,1)}), bf16[2,8,256]{2,0,1:T(2,128)(2,1)S(1)}, u32[]{:S(2)}, u32[]{:S(2)}) %all-to-all-start.1) | async-done | bytes 8224 | tf_op jit(solution)/shard_map/all_to_all | solution.py:399
  33.2 3.6 %all-to-all-start = ((bf16[8,256,256]{2,1,0:T(8,128)(2,1)}), bf16[8,256,256]{2,1,0:T(8,128)(2,1)S(1)}, u32[]{:S(2)}, u32[]{:S(2)}) async-start(bf16[8,256,256]{2,1,0:T(8,128)(2,1)} %bitcast.41), calls=%async_computation | async-start | bytes 2097152 | tf_op jit(solution)/shard_map/all_to_all | solution.py:383
  37.4 1.8 %slot_members.1 = f32[8,256]{1,0:T(8,128)} custom-call(s32[4]{0:T(128)} %tiles_ref.1, s32[1,2432]{1,0:T(1,128)} %reshape.48.source_ref), custom_call_target="tpu_custom_call" | custom-call | tf_op jit(solution)/shard_map/slot_members/pallas_call | solution.py:201
  39.2 1.3 %copy.15 = f32[1,1,8,256]{3,1,2,0:T(1,128)} copy(f32[1,1,8,256]{3,2,1,0:T(8,128)} %bitcast.47) | data formatting | bytes 16384
  41.1 21.2 %all-to-all-done = bf16[8,256,256]{2,1,0:T(8,128)(2,1)S(1)} async-done(((bf16[8,256,256]{2,1,0:T(8,128)(2,1)}), bf16[8,256,256]{2,1,0:T(8,128)(2,1)S(1)}, u32[]{:S(2)}, u32[]{:S(2)}) %all-to-all-start) | async-done | bytes 1048608 | tf_op jit(solution)/shard_map/all_to_all | solution.py:383
  62.3 1.0 copy-done
  63.3 4.4 %solve_members.1 = (f32[4,256]{1,0:T(4,128)}, f32[1,2048]{1,0:T(1,128)}) custom-call(bf16[2048,256]{1,0:T(8,128)(2,1)} %bitcast.40, bf16[1,2048]{1,0:T(2,128)(2,1)} %bitcast.45, bf16[1,2048]{1,0:T(2,128)(2,1)} %bitcast.44, f32[1,2048]{1,0:T(1,128)} %bitcast.43, f32[4,256]{1,0:T(4,128)} %coef_ref.3), custom_call_target="tpu_custom_call" | custom-call | tf_op jit(solution)/shard_map/solve_members/pallas_call | solution.py:276
  67.6 9.9 %all_to_all.21 = f32[8,1,256]{2,1,0:T(1,128)S(1)} all-to-all(f32[8,1,256]{2,1,0:T(1,128)} %bitcast.54), channel_id=1, replica_groups=mesh['dp'=8,'feat'=4] {'dp'}, dimensions={0} | all-to-all | bytes 16384 | tf_op jit(solution)/shard_map/all_to_all | solution.py:406
  78.1 1.7 %margins.1 = (f32[1,1024]{1,0:T(1,128)}, f32[1,1024]{1,0:T(1,128)}) custom-call(f32[8,256]{1,0:T(8,128)} %bitcast.46, s32[1,1024]{1,0:T(1,128)} %bitcast.51, f32[1,1024]{1,0:T(1,128)} %get-tuple-element.11.fixed_ref, s32[1,1024]{1,0:T(1,128)} %bitcast.53), custom_call_target="tpu_custom_call" | custom-call | tf_op jit(solution)/shard_map/margins/pallas_call | solution.py:302
  80.4 1.4 %collective-permute-start.5 = (f32[1,1024]{1,0:T(1,128)}, f32[1,1024]{1,0:T(1,128)S(1)}, u32[]{:S(2)}, u32[]{:S(2)}) collective-permute-start(f32[1,1024]{1,0:T(1,128)} %get-tuple-element.14), channel_id=1, source_target_pairs={{0,3},{1,2},{2,1},{3,0},{4,7},{5,6},{6,5},{7,4},{8,11},{9,10},{10,... | collective-permute-start | bytes 12296 | tf_op jit(solution)/shard_map/ppermute | solution.py:308
  82.6 1.1 collective-permute-done.4
  84.5 9.3 %gradient_partial.1 = f32[512,512]{1,0:T(8,128)} custom-call(bf16[4096,512]{1,0:T(8,128)(2,1)} %values_ref.3, s32[1,4096]{1,0:T(1,128)} %bitcast.56, f32[1,4096]{1,0:T(1,128)} %bitcast.48), custom_call_target="tpu_custom_call" | custom-call | flops 4294967296 | bytes 5242880 | tf_op jit(solution)/shard_map/gradient_partial/pallas_call | solution.py:105
  93.8 1.4 %broadcast_multiply_fusion = f32[512,512]{1,0:T(8,128)S(1)} fusion(f32[512,512]{1,0:T(8,128)} %gradient_partial.1), kind=kLoop, calls=%fused_computation.2 | loop fusion | flops 262144 | bytes 2097152 | tf_op jit(solution)/shard_map/mul | solution.py:419
  95.9 7.7 %collective-permute-done.6 = f16[4,64,512]{2,1,0:T(8,128)(2,1)S(1)} collective-permute-done((f16[4,64,512]{2,1,0:T(8,128)(2,1)S(1)}, f16[4,64,512]{2,1,0:T(8,128)(2,1)S(1)}, u32[]{:S(2)}, u32[]{:S(2)}) %collective-permute-start.6) | collective-permute-done | bytes 262176 | tf_op jit(solution)/shard_map/ppermute | solution.py:308
  105.0 3.3 %collective-permute-start.9 = (f16[64,512]{1,0:T(8,128)(2,1)S(1)}, f16[64,512]{1,0:T(8,128)(2,1)S(1)}, u32[]{:S(2)}, u32[]{:S(2)}) collective-permute-start(f16[64,512]{1,0:T(8,128)(2,1)S(1)} %get-tuple-element.20), channel_id=1, source_target_pairs={{0,24},{4,28},{8,16},{12,20},{16,8},{20,12},{24,0},{28,4},{1,25},{... | collective-permute-start | bytes 196616 | tf_op jit(solution)/shard_map/ppermute | solution.py:308
  108.2 3.4 %collective-permute-done.8 = f16[64,512]{1,0:T(8,128)(2,1)S(1)} collective-permute-done((f16[64,512]{1,0:T(8,128)(2,1)S(1)}, f16[64,512]{1,0:T(8,128)(2,1)S(1)}, u32[]{:S(2)}, u32[]{:S(2)}) %collective-permute-start.8) | collective-permute-done | bytes 65568 | tf_op jit(solution)/shard_map/ppermute | solution.py:308
  112.4 3.6 %collective-permute-done.10 = f16[64,512]{1,0:T(8,128)(2,1)S(1)} collective-permute-done((f16[64,512]{1,0:T(8,128)(2,1)S(1)}, f16[64,512]{1,0:T(8,128)(2,1)S(1)}, u32[]{:S(2)}, u32[]{:S(2)}) %collective-permute-start.10) | collective-permute-done | bytes 65568 | tf_op jit(solution)/shard_map/ppermute | solution.py:308
  116.3 1.3 %collective-permute-start.11 = (f16[128,512]{1,0:T(8,128)(2,1)S(1)}, f16[128,512]{1,0:T(8,128)(2,1)S(1)}, u32[]{:S(2)}, u32[]{:S(2)}) collective-permute-start(f16[128,512]{1,0:T(8,128)(2,1)S(1)} %get-tuple-element.16), channel_id=1, source_target_pairs={{0,8},{4,12},{8,0},{12,4},{16,24},{20,28},{24,16},{28,20},{1,9},{5... | collective-permute-start | bytes 393224 | tf_op jit(solution)/shard_map/ppermute | solution.py:308
  117.6 1.9 %collective-permute-start.12 = (f16[128,512]{1,0:T(8,128)(2,1)S(1)}, f16[128,512]{1,0:T(8,128)(2,1)S(1)}, u32[]{:S(2)}, u32[]{:S(2)}) collective-permute-start(f16[128,512]{1,0:T(8,128)(2,1)S(1)} %get-tuple-element.16), channel_id=1, source_target_pairs={{0,16},{4,20},{8,24},{12,28},{16,0},{20,4},{24,8},{28,12},{1,17},{... | collective-permute-start | bytes 393224 | tf_op jit(solution)/shard_map/ppermute | solution.py:308
  119.5 1.2 collective-permute-start.13
  120.7 2.3 %collective-permute-done.11 = f16[128,512]{1,0:T(8,128)(2,1)S(1)} collective-permute-done((f16[128,512]{1,0:T(8,128)(2,1)S(1)}, f16[128,512]{1,0:T(8,128)(2,1)S(1)}, u32[]{:S(2)}, u32[]{:S(2)}) %collective-permute-start.11) | collective-permute-done | bytes 131104 | tf_op jit(solution)/shard_map/ppermute | solution.py:308
  123.1 3.3 %collective-permute-done.12 = f16[128,512]{1,0:T(8,128)(2,1)S(1)} collective-permute-done((f16[128,512]{1,0:T(8,128)(2,1)S(1)}, f16[128,512]{1,0:T(8,128)(2,1)S(1)}, u32[]{:S(2)}, u32[]{:S(2)}) %collective-permute-start.12) | collective-permute-done | bytes 131104 | tf_op jit(solution)/shard_map/ppermute | solution.py:308
  126.5 1.0 copy-done.2
  (44 shorter events, 8.1 us)
Async XLA Ops:
  9.9 26.9 %copy-start.3 = (s32[2432]{0:T(1024)S(1)}, s32[2432]{0:T(1024)}, u32[]{:S(2)}) copy-start(s32[2432]{0:T(1024)} %param.16) | copy-start | bytes 29188
  11.2 3.1 %collective-permute-start = (f32[1,1024]{1,0:T(1,128)S(1)}, f32[1,1024]{1,0:T(1,128)S(1)}, u32[]{:S(2)}, u32[]{:S(2)}) collective-permute-start(f32[1,1024]{1,0:T(1,128)S(1)} %get-tuple-element.24), channel_id=1, source_target_pairs={{0,1},{1,0},{2,3},{3,2},{4,5},{5,4},{6,7},{7,6},{8,9},{9,8},{10,11... | collective-permute-start | bytes 12296 | tf_op jit(solution)/shard_map/ppermute | solution.py:308
  11.7 4.1 %collective-permute-start.1 = (f32[1,1024]{1,0:T(1,128)S(1)}, f32[1,1024]{1,0:T(1,128)S(1)}, u32[]{:S(2)}, u32[]{:S(2)}) collective-permute-start(f32[1,1024]{1,0:T(1,128)S(1)} %get-tuple-element.23), channel_id=1, source_target_pairs={{0,2},{1,3},{2,0},{3,1},{4,6},{5,7},{6,4},{7,5},{8,10},{9,11},{10,... | collective-permute-start | bytes 12296 | tf_op jit(solution)/shard_map/ppermute | solution.py:308
  14.2 3.0 %collective-permute-start.2 = (f32[1,1024]{1,0:T(1,128)S(1)}, f32[1,1024]{1,0:T(1,128)S(1)}, u32[]{:S(2)}, u32[]{:S(2)}) collective-permute-start(f32[1,1024]{1,0:T(1,128)S(1)} %get-tuple-element.22), channel_id=1, source_target_pairs={{0,3},{1,2},{2,1},{3,0},{4,7},{5,6},{6,5},{7,4},{8,11},{9,10},{10,... | collective-permute-start | bytes 12296 | tf_op jit(solution)/shard_map/ppermute | solution.py:308
  14.4 2.9 %copy-start.4 = (f32[1,1024]{1,0:T(1,128)}, f32[1,1024]{1,0:T(1,128)S(1)}, u32[]{:S(2)}) copy-start(f32[1,1024]{1,0:T(1,128)S(1)} %collective-permute-done.refs_1_) | copy-start | bytes 12292
  15.8 1.5 %copy-start.5 = (f32[1,1024]{1,0:T(1,128)}, f32[1,1024]{1,0:T(1,128)S(1)}, u32[]{:S(2)}) copy-start(f32[1,1024]{1,0:T(1,128)S(1)} %collective-permute-done.1.refs_2_) | copy-start | bytes 12292
  17.3 0.6 copy-start.6
  20.9 12.3 %all-to-all-start.1 = ((bf16[2,8,256]{2,0,1:T(2,128)(2,1)}), bf16[2,8,256]{2,0,1:T(2,128)(2,1)S(1)}, u32[]{:S(2)}, u32[]{:S(2)}) async-start(bf16[2,8,256]{2,0,1:T(2,128)(2,1)} %copy.12), calls=%async_computation.1 | async-start | bytes 16384 | tf_op jit(solution)/shard_map/all_to_all | solution.py:399
  33.2 29.1 %all-to-all-start = ((bf16[8,256,256]{2,1,0:T(8,128)(2,1)}), bf16[8,256,256]{2,1,0:T(8,128)(2,1)S(1)}, u32[]{:S(2)}, u32[]{:S(2)}) async-start(bf16[8,256,256]{2,1,0:T(8,128)(2,1)} %bitcast.41), calls=%async_computation | async-start | bytes 2097152 | tf_op jit(solution)/shard_map/all_to_all | solution.py:383
  62.3 1.0 copy-start
  79.9 2.6 %collective-permute-start.3 = (f32[1,1024]{1,0:T(1,128)}, f32[1,1024]{1,0:T(1,128)S(1)}, u32[]{:S(2)}, u32[]{:S(2)}) collective-permute-start(f32[1,1024]{1,0:T(1,128)} %get-tuple-element.14), channel_id=1, source_target_pairs={{0,1},{1,0},{2,3},{3,2},{4,5},{5,4},{6,7},{7,6},{8,9},{9,8},{10,11... | collective-permute-start | bytes 12296 | tf_op jit(solution)/shard_map/ppermute | solution.py:308
  79.9 3.8 %collective-permute-start.4 = (f32[1,1024]{1,0:T(1,128)}, f32[1,1024]{1,0:T(1,128)S(1)}, u32[]{:S(2)}, u32[]{:S(2)}) collective-permute-start(f32[1,1024]{1,0:T(1,128)} %get-tuple-element.14), channel_id=1, source_target_pairs={{0,2},{1,3},{2,0},{3,1},{4,6},{5,7},{6,4},{7,5},{8,10},{9,11},{10,... | collective-permute-start | bytes 12296 | tf_op jit(solution)/shard_map/ppermute | solution.py:308
  80.4 3.4 %collective-permute-start.5 = (f32[1,1024]{1,0:T(1,128)}, f32[1,1024]{1,0:T(1,128)S(1)}, u32[]{:S(2)}, u32[]{:S(2)}) collective-permute-start(f32[1,1024]{1,0:T(1,128)} %get-tuple-element.14), channel_id=1, source_target_pairs={{0,3},{1,2},{2,1},{3,0},{4,7},{5,6},{6,5},{7,4},{8,11},{9,10},{10,... | collective-permute-start | bytes 12296 | tf_op jit(solution)/shard_map/ppermute | solution.py:308
  93.8 22.4 %copy-start.1 = (f32[512,512]{1,0:T(8,128)S(1)}, f32[512,512]{1,0:T(8,128)}, u32[]{:S(2)}) copy-start(f32[512,512]{1,0:T(8,128)} %coef_ref.2) | copy-start | bytes 3145732
  95.3 8.3 %collective-permute-start.6 = (f16[4,64,512]{2,1,0:T(8,128)(2,1)S(1)}, f16[4,64,512]{2,1,0:T(8,128)(2,1)S(1)}, u32[]{:S(2)}, u32[]{:S(2)}) collective-permute-start(f16[4,64,512]{2,1,0:T(8,128)(2,1)S(1)} %fusion), channel_id=1, source_target_pairs={{0,4},{4,0},{8,12},{12,8},{16,20},{20,16},{24,28},{28,24},{1,5},{5... | collective-permute-start | bytes 786440 | tf_op jit(solution)/shard_map/ppermute | solution.py:308
  103.8 4.5 %collective-permute-start.7 = (f16[64,512]{1,0:T(8,128)(2,1)S(1)}, f16[64,512]{1,0:T(8,128)(2,1)S(1)}, u32[]{:S(2)}, u32[]{:S(2)}) collective-permute-start(f16[64,512]{1,0:T(8,128)(2,1)S(1)} %get-tuple-element.19), channel_id=1, source_target_pairs={{0,8},{4,12},{8,0},{12,4},{16,24},{20,28},{24,16},{28,20},{1,9},{5... | collective-permute-start | bytes 196616 | tf_op jit(solution)/shard_map/ppermute | solution.py:308
  104.3 7.3 %collective-permute-start.8 = (f16[64,512]{1,0:T(8,128)(2,1)S(1)}, f16[64,512]{1,0:T(8,128)(2,1)S(1)}, u32[]{:S(2)}, u32[]{:S(2)}) collective-permute-start(f16[64,512]{1,0:T(8,128)(2,1)S(1)} %get-tuple-element.21), channel_id=1, source_target_pairs={{0,16},{4,20},{8,24},{12,28},{16,0},{20,4},{24,8},{28,12},{1,17},{... | collective-permute-start | bytes 196616 | tf_op jit(solution)/shard_map/ppermute | solution.py:308
  105.0 6.7 %collective-permute-start.9 = (f16[64,512]{1,0:T(8,128)(2,1)S(1)}, f16[64,512]{1,0:T(8,128)(2,1)S(1)}, u32[]{:S(2)}, u32[]{:S(2)}) collective-permute-start(f16[64,512]{1,0:T(8,128)(2,1)S(1)} %get-tuple-element.20), channel_id=1, source_target_pairs={{0,24},{4,28},{8,16},{12,20},{16,8},{20,12},{24,0},{28,4},{1,25},{... | collective-permute-start | bytes 196616 | tf_op jit(solution)/shard_map/ppermute | solution.py:308
  111.7 4.3 %collective-permute-start.10 = (f16[64,512]{1,0:T(8,128)(2,1)S(1)}, f16[64,512]{1,0:T(8,128)(2,1)S(1)}, u32[]{:S(2)}, u32[]{:S(2)}) collective-permute-start(f16[64,512]{1,0:T(8,128)(2,1)S(1)} %fusion.3), channel_id=1, source_target_pairs={{0,4},{4,0},{8,12},{12,8},{16,20},{20,16},{24,28},{28,24},{1,5},{5... | collective-permute-start | bytes 196616 | tf_op jit(solution)/shard_map/ppermute | solution.py:308
  116.3 6.8 %collective-permute-start.11 = (f16[128,512]{1,0:T(8,128)(2,1)S(1)}, f16[128,512]{1,0:T(8,128)(2,1)S(1)}, u32[]{:S(2)}, u32[]{:S(2)}) collective-permute-start(f16[128,512]{1,0:T(8,128)(2,1)S(1)} %get-tuple-element.16), channel_id=1, source_target_pairs={{0,8},{4,12},{8,0},{12,4},{16,24},{20,28},{24,16},{28,20},{1,9},{5... | collective-permute-start | bytes 393224 | tf_op jit(solution)/shard_map/ppermute | solution.py:308
  117.6 8.8 %collective-permute-start.12 = (f16[128,512]{1,0:T(8,128)(2,1)S(1)}, f16[128,512]{1,0:T(8,128)(2,1)S(1)}, u32[]{:S(2)}, u32[]{:S(2)}) collective-permute-start(f16[128,512]{1,0:T(8,128)(2,1)S(1)} %get-tuple-element.16), channel_id=1, source_target_pairs={{0,16},{4,20},{8,24},{12,28},{16,0},{20,4},{24,8},{28,12},{1,17},{... | collective-permute-start | bytes 393224 | tf_op jit(solution)/shard_map/ppermute | solution.py:308
  119.5 6.9 %collective-permute-start.13 = (f16[128,512]{1,0:T(8,128)(2,1)S(1)}, f16[128,512]{1,0:T(8,128)(2,1)S(1)}, u32[]{:S(2)}, u32[]{:S(2)}) collective-permute-start(f16[128,512]{1,0:T(8,128)(2,1)S(1)} %get-tuple-element.16), channel_id=1, source_target_pairs={{0,24},{4,28},{8,16},{12,20},{16,8},{20,12},{24,0},{28,4},{1,25},{... | collective-permute-start | bytes 393224 | tf_op jit(solution)/shard_map/ppermute | solution.py:308
  126.5 1.0 copy-start.2

commit v2 on v1

v2 whole, which is shorter than its diff:
```python
import jax
import jax.numpy as jnp
from jax import lax
from jax.experimental import pallas as pl
from jax.experimental.pallas import tpu as pltpu
from jax.sharding import PartitionSpec as P

CG_ITERS = 2
TILE = 128

ridge_member = 1.0
ridge_fixed = 1.0
bf16 = jnp.bfloat16
f32 = jnp.float32
f16 = jnp.float16


def split(value, parts):
    out = []
    for _ in range(parts):
        piece = value.astype(bf16)
        out.append(piece)
        value = value - piece.astype(f32)
    return out


def dot_nt(a, b):
    return lax.dot_general(a, b, (((1,), (1,)), ((), ())), preferred_element_type=f32)


def dot_nn(a, b):
    return jnp.dot(a, b, preferred_element_type=f32)


def rows_iota(shape):
    return lax.broadcasted_iota(jnp.int32, shape, 0)


def hot(index, count):
    return rows_iota((count, index.shape[1])) == index


def sigmoid(x):
    return 1.0 / (1.0 + jnp.exp(-x))


def partial_kernel(values_ref, block_ref, coef_ref, *refs):
    outs, (high_ref, low_ref) = refs[:-2], refs[-2:]

    @pl.when(pl.program_id(0) == 0)
    def _():
        high, low = split(coef_ref[...], 2)
        high_ref[...] = high
        low_ref[...] = low

    values = values_ref[...]
    product = dot_nt(high_ref[...], values) + dot_nt(low_ref[...], values)
    mask = hot(block_ref[...], product.shape[0])
    score = jnp.sum(jnp.where(mask, product, 0.0), axis=0, keepdims=True)
    target = pl.program_id(0) ^ lax.axis_index("feat")
    for k, out_ref in enumerate(outs):

        @pl.when(target == k)
        def _():
            out_ref[...] = score


def partial_scores(fixed_values, block_row, fixed_coef, rows_here):
    rows, width = fixed_values.shape
    blocks = fixed_coef.shape[0]
    shards = rows // rows_here
    return pl.pallas_call(
        partial_kernel,
        grid=(shards,),
        in_specs=[
            pl.BlockSpec((rows_here, width), lambda i: (i, 0)),
            pl.BlockSpec((1, rows_here), lambda i: (0, i)),
            pl.BlockSpec((blocks, width), lambda i: (0, 0)),
        ],
        out_specs=[pl.BlockSpec((1, rows_here), lambda i: (0, 0))] * shards,
        out_shape=[jax.ShapeDtypeStruct((1, rows_here), f32)] * shards,
        scratch_shapes=[pltpu.VMEM((blocks, width), bf16)] * 2,
        cost_estimate=pl.CostEstimate(
            flops=4 * rows * blocks * width,
            bytes_accessed=2 * rows * width + 4 * blocks * width,
            transcendentals=0,
        ),
        name="partial_scores",
    )(fixed_values, block_row, fixed_coef)


def grad_kernel(flip, dp_count, values_ref, block_ref, *refs):
    pieces, out_ref = refs[:-1], refs[-1]
    kept = out_ref.shape[0]
    chunk = 2 * kept // dp_count
    rows = pieces[0].shape[1]
    parity = (lax.axis_index("dp") + flip) % 2
    feat = lax.axis_index("feat")
    for k, piece in enumerate(pieces):
        at = pl.ds(pl.multiple_of((feat ^ k) * rows, rows), rows)
        block = block_ref[:, at]
        local = (block // (2 * chunk)) * chunk + block % chunk
        local = jnp.where((block // chunk) % 2 == parity, local, -1)
        mask = hot(local, kept)
        high, low = split(piece[...], 2)
        left_high = jnp.where(mask, high.astype(f32), 0.0).astype(bf16)
        left_low = jnp.where(mask, low.astype(f32), 0.0).astype(bf16)
        values = values_ref[at, :]
        total = dot_nn(left_high, values) + dot_nn(left_low, values)
        if k == 0:
            out_ref[...] = total
        else:
            out_ref[...] += total


def gradient_partial(flip, dp_count, fixed_values, block_row, pieces, blocks):
    rows, width = fixed_values.shape

    def kernel(*refs):
        grad_kernel(flip, dp_count, *refs)

    return pl.pallas_call(
        kernel,
        out_shape=jax.ShapeDtypeStruct((blocks // 2, width), f32),
        cost_estimate=pl.CostEstimate(
            flops=2 * rows * blocks * width,
            bytes_accessed=2 * rows * width + 2 * blocks * width,
            transcendentals=0,
        ),
        compiler_params=pltpu.CompilerParams(vmem_limit_bytes=24 << 20),
    )(fixed_values, block_row, *pieces)


def pack_kernel(feats_ref, slot_ref, out_ref):
    count = out_ref.shape[0]
    start = pl.program_id(0) * count
    mask = (rows_iota((count, slot_ref.shape[1])) + start) == slot_ref[...]
    one_hot = jnp.where(mask, 1.0, 0.0).astype(bf16)
    out_ref[...] = dot_nn(one_hot, feats_ref[...]).astype(bf16)


def pack_feats(member_feats, slot_row, slot_total):
    rows, width = member_feats.shape
    step = min(1024, slot_total)
    return pl.pallas_call(
        pack_kernel,
        grid=(slot_total // step,),
        in_specs=[
            pl.BlockSpec((rows, width), lambda i: (0, 0)),
            pl.BlockSpec((1, rows), lambda i: (0, 0)),
        ],
        out_specs=pl.BlockSpec((step, width), lambda i: (i, 0)),
        out_shape=jax.ShapeDtypeStruct((slot_total, width), bf16),
        cost_estimate=pl.CostEstimate(
            flops=2 * rows * slot_total * width,
            bytes_accessed=2 * rows * width + 2 * slot_total * width,
            transcendentals=0,
        ),
        name="pack_feats",
    )(member_feats, slot_row)


def message_kernel(parts_refs, label_ref, slot_ref, fixed_ref, out_ref):
    fixed = parts_refs[0][...]
    for part in parts_refs[1:]:
        fixed = fixed + part[...]
    fixed_ref[...] = fixed
    destinations, _, capacity = out_ref.shape
    slot = slot_ref[...]
    owner = slot // capacity
    owner_hot = hot(owner, destinations)
    place_hot = jnp.where(hot(slot - owner * capacity, capacity), 1.0, 0.0).astype(bf16)
    score = fixed.astype(bf16).astype(f32)
    label = label_ref[...].astype(f32)
    both = jnp.concatenate(
        [jnp.where(owner_hot, score, 0.0), jnp.where(owner_hot, label, 0.0)], axis=0
    )
    placed = dot_nt(both.astype(bf16), place_hot)
    out_ref[:, 0, :] = placed[:destinations]
    out_ref[:, 1, :] = placed[destinations:]


def build_message(parts, label_row, slot_row, dp_count, capacity):
    rows = slot_row.shape[1]

    def kernel(*refs):
        message_kernel(refs[: len(parts)], *refs[len(parts) :])

    return pl.pallas_call(
        kernel,
        out_shape=(
            jax.ShapeDtypeStruct((1, rows), f32),
            jax.ShapeDtypeStruct((dp_count, 2, capacity), f32),
        ),
        name="build_message",
    )(*parts, label_row, slot_row)


def slot_member_kernel(tiles_ref, source_ref, out_ref):
    slots, capacity = out_ref.shape
    source = source_ref[...]
    position = lax.broadcasted_iota(jnp.int32, source.shape, 1) // TILE
    member = jnp.zeros(source.shape, jnp.int32)
    end = jnp.int32(0)
    for m in range(tiles_ref.shape[0]):
        end = end + tiles_ref[m]
        member = member + (position >= end).astype(jnp.int32)
    sender = source // capacity
    sender_hot = jnp.where(hot(sender, slots), member.astype(f32) + 1.0, 0.0).astype(bf16)
    place_hot = jnp.where(hot(source - sender * capacity, capacity), 1.0, 0.0).astype(bf16)
    out_ref[...] = dot_nt(sender_hot, place_hot) - 1.0


def slot_members(member_tiles, source_row, dp_count, capacity):
    return pl.pallas_call(
        slot_member_kernel,
        in_specs=[
            pl.BlockSpec(memory_space=pltpu.SMEM),
            pl.BlockSpec(memory_space=pltpu.VMEM),
        ],
        out_specs=pl.BlockSpec(memory_space=pltpu.VMEM),
        out_shape=jax.ShapeDtypeStruct((dp_count, capacity), f32),
        name="slot_members",
    )(member_tiles, source_row)


def lane_row(pieces):
    lanes = pieces.shape[-1]
    pieces = pieces.reshape(-1, lanes)
    return jnp.concatenate([pieces[i : i + 1] for i in range(pieces.shape[0])], axis=1)


def solve_kernel(feats_ref, message_ref, member_ref, coef_ref, updated_ref, scores_ref):
    feats = feats_ref[...]
    coef = coef_ref[...]
    count = coef.shape[0]
    slots = feats.shape[0]
    lanes = message_ref.shape[2]
    message = message_ref[...]
    sent_score = lane_row(message[:, 0, :])
    label = lane_row(message[:, 1, :])
    own = rows_iota((count, slots)).astype(f32) == lane_row(member_ref[...])

    def pick(vectors):
        high, low = split(vectors, 2)
        both = dot_nt(jnp.concatenate([high, low], axis=0), feats)
        each = both[:count] + both[count:]
        return jnp.sum(jnp.where(own, each, 0.0), axis=0, keepdims=True)

    def spread(row_weights):
        high, low = split(jnp.where(own, row_weights, 0.0), 2)
        return jnp.concatenate([high, low], axis=0)

    def gather(row_weights):
        both = dot_nn(spread(row_weights), feats)
        return both[:count] + both[count:]

    base = pick(coef)
    logits = sent_score + base
    probability = sigmoid(logits)
    weight = probability * (1.0 - probability)
    gradient = gather(label - probability) - ridge_member * coef
    wide = feats.astype(f32)
    square_high, square_low = split(wide * wide, 2)
    weights = spread(weight)
    both = dot_nn(weights, square_high) + dot_nn(weights, square_low)
    diagonal = both[:count] + both[count:] + ridge_member
    step_sum = jnp.zeros_like(coef)
    new_scores = base
    remain = gradient
    scaled = remain / diagonal
    search = scaled
    inner_product = jnp.sum(remain * scaled, axis=1, keepdims=True)
    for iteration in range(CG_ITERS):
        projected = pick(search)
        if iteration + 1 < CG_ITERS:
            image = gather(weight * projected) + ridge_member * search
            curvature = jnp.sum(search * image, axis=1, keepdims=True)
        else:
            row_part = jnp.where(own, weight * projected * projected, 0.0)
            curvature = jnp.sum(row_part, axis=1, keepdims=True) + ridge_member * jnp.sum(
                search * search, axis=1, keepdims=True
            )
        alpha_step = inner_product / curvature
        step_sum = step_sum + alpha_step * search
        row_alpha = jnp.sum(jnp.where(own, alpha_step, 0.0), axis=0, keepdims=True)
        new_scores = new_scores + row_alpha * projected
        if iteration + 1 < CG_ITERS:
            remain = remain - alpha_step * image
            scaled = remain / diagonal
            inner_next = jnp.sum(remain * scaled, axis=1, keepdims=True)
            search = scaled + (inner_next / inner_product) * search
            inner_product = inner_next
    updated_ref[...] = coef + step_sum
    for i in range(scores_ref.shape[0]):
        scores_ref[i] = new_scores[:, i * lanes : (i + 1) * lanes]


def solve_members(feats, message, member_slots, member_coef):
    senders, _, capacity = message.shape
    return pl.pallas_call(
        solve_kernel,
        out_shape=(
            jax.ShapeDtypeStruct(member_coef.shape, f32),
            jax.ShapeDtypeStruct((senders, 1, capacity), f32),
        ),
        name="solve_members",
    )(feats, message, member_slots, member_coef)


def margin_kernel(returned_ref, slot_ref, fixed_ref, label_ref, margin_ref, residual_ref):
    owners, _, capacity = returned_ref.shape
    slot = slot_ref[...]
    owner = slot // capacity
    place_hot = jnp.where(hot(slot - owner * capacity, capacity), 1.0, 0.0).astype(bf16)
    pieces = split(returned_ref[...].reshape(owners, capacity), 3)
    looked_up = dot_nn(jnp.concatenate(pieces, axis=0), place_hot)
    looked_up = looked_up[:owners] + (looked_up[owners : 2 * owners] + looked_up[2 * owners :])
    score = jnp.sum(jnp.where(hot(owner, owners), looked_up, 0.0), axis=0, keepdims=True)
    margin = fixed_ref[...] + score
    margin_ref[...] = margin
    residual_ref[...] = label_ref[...].astype(f32) - sigmoid(margin)


def margins(returned, slot_row, fixed_row, label_row):
    out = jax.ShapeDtypeStruct(slot_row.shape, f32)
    return pl.pallas_call(margin_kernel, out_shape=(out, out), name="margins")(
        returned, slot_row, fixed_row, label_row
    )


def swap(value, axis, offset):
    return lax.ppermute(
        value, axis, [(i, i ^ offset) for i in range(lax.axis_size(axis))]
    )


def pick_index(value, index):
    return lax.dynamic_index_in_dim(value, index, 0, keepdims=False)


def exchange(message, side, place, half):
    if half > 4:
        return lax.all_to_all(message, "dp", 0, 0, tiled=True)
    pairs = message.reshape((half, 2) + message.shape[1:])
    own = lax.dynamic_index_in_dim(pairs, side, 1, keepdims=False)
    other = swap(lax.dynamic_index_in_dim(pairs, 1 - side, 1, keepdims=False), "dp", 1)
    both = jnp.where(
        side == 0, jnp.stack([own, other], axis=1), jnp.stack([other, own], axis=1)
    )
    out = jnp.zeros_like(both)
    for k in range(half):
        entry = pick_index(both, place ^ k)
        got = entry if k == 0 else swap(entry, "dp", 2 * k)
        out = lax.dynamic_update_index_in_dim(out, got, place ^ k, 0)
    return out.reshape(message.shape)


def reduce_rest(kept, place, stride):
    count = kept.shape[0]
    if count <= 4:
        sends = kept.astype(f16)
        total = pick_index(kept, place)
        for k in range(1, count):
            got = swap(pick_index(sends, place ^ k), "dp", stride * k)
            total = total + got.astype(f32)
        return total
    low = count // 2
    top = place // low
    view = kept.reshape((2, low) + kept.shape[1:])
    got = swap(pick_index(view, 1 - top).astype(f16), "dp", stride * low)
    return reduce_rest(pick_index(view, top) + got.astype(f32), place % low, stride)


def spread_rest(pair, place, count, stride, coef):
    rows = pair.shape[0]
    out = jnp.zeros(coef.shape, f32)

    def put(out, got, at):
        own_coef = lax.dynamic_slice_in_dim(coef, at, got.shape[0], 0)
        grad = ridge_fixed * own_coef - got.astype(f32)
        return lax.dynamic_update_slice_in_dim(out, grad, at, 0)

    if count <= 4:
        for k in range(count):
            got = pair if k == 0 else swap(pair, "dp", stride * k)
            out = put(out, got, (place ^ k) * rows)
        return out
    bit = 1
    while bit < count:
        other = swap(pair, "dp", stride * bit)
        pair = jnp.where(
            (place // bit) % 2 == 0,
            jnp.concatenate([pair, other]),
            jnp.concatenate([other, pair]),
        )
        bit *= 2
    return put(out, pair, 0)


def body(
    member_feats,
    labels,
    fixed_values,
    fixed_blocks,
    fixed_coef,
    member_coef,
    row_slot,
    tile_source,
    member_tiles,
):
    dp_count = lax.axis_size("dp")
    feat_count = lax.axis_size("feat")
    rows_here = member_feats.shape[0]
    blocks, block_width = fixed_coef.shape
    capacity = 2 * rows_here // dp_count
    slot_total = dp_count * capacity
    group_rows = fixed_values.shape[0]
    side = lax.axis_index("dp") % 2
    place = lax.axis_index("dp") // 2
    half = dp_count // 2
    chunk = blocks // dp_count

    slot_row = row_slot.reshape(1, rows_here)
    label_row = labels.reshape(1, rows_here)
    block_row = fixed_blocks.reshape(1, group_rows)

    send_feats = pack_feats(member_feats, slot_row, slot_total)
    got_feats = lax.all_to_all(
        send_feats.reshape(dp_count, capacity, -1), "dp", 0, 0, tiled=True
    ).reshape(slot_total, -1)
    member_slots = slot_members(
        member_tiles, tile_source.reshape(1, -1), dp_count, capacity
    )

    sends = partial_scores(fixed_values, block_row, fixed_coef, rows_here)
    parts = [sends[0]] + [swap(sends[k], "feat", k) for k in range(1, feat_count)]
    fixed_row, message = build_message(parts, label_row, slot_row, dp_count, capacity)
    got = exchange(message, side, place, half)

    if capacity % 128:
        got = jnp.moveaxis(got, 1, 0).reshape(1, 2, slot_total)
        member_slots = member_slots.reshape(1, slot_total)
    updated_coef, new_scores = solve_members(got_feats, got, member_slots, member_coef)
    returned = lax.all_to_all(
        new_scores.reshape(dp_count, 1, capacity), "dp", 0, 0, tiled=True
    )
    margin, residual = margins(returned, slot_row, fixed_row, label_row)

    scaled = residual * (1.0 / dp_count)
    pieces = [scaled] + [swap(scaled, "feat", k) for k in range(1, feat_count)]
    theirs = gradient_partial(1, dp_count, fixed_values, block_row, pieces, blocks)
    got_half = swap(theirs.astype(f16), "dp", 1)
    mine = gradient_partial(0, dp_count, fixed_values, block_row, pieces, blocks)
    kept = mine + got_half.astype(f32)
    summed = reduce_rest(kept.reshape(half, chunk, block_width), place, 2).astype(f16)
    other = swap(summed, "dp", 1)
    pair = jnp.where(
        side == 0, jnp.concatenate([summed, other]), jnp.concatenate([other, summed])
    )
    fixed_grad = spread_rest(pair, place, half, 2, fixed_coef)
    return (margin.reshape(rows_here), updated_coef, fixed_grad)


def solution(mesh):
    placed = (
        P(("dp", "feat"), None),
        P(("dp", "feat")),
        P("dp", "feat"),
        P("dp", "feat"),
        P("feat", None),
        P(("dp", "feat"), None),
        P(("dp", "feat")),
        P(("dp", "feat")),
        P(("dp", "feat")),
    )
    return jax.shard_map(
        body,
        mesh=mesh,
        in_specs=placed,
        out_specs=(P(("dp", "feat")), P(("dp", "feat"), None), P("feat", None)),
        check_vma=False,
    )
```

time: 129 us -> 102 us (0.79)
  waiting for transfers between devices: 48.4 us -> 29.4 us
  Pallas kernels: 32 us -> 24.9 us
  starting transfers between devices: 24.6 us -> 28.4 us
  local copies, waits for them, and re-layouts: 10 us -> 6.23 us
    all_to_all x2 -> x1, waiting for transfers between devices: 23.9 us -> 0.01 us  [body(): lax.all_to_all(send_feats.reshape(dp_count, capacity, -1), 'dp', 0, 0, ti...]
    pallas_call x2 -> x3, Pallas kernels: 18.5 us -> 12.3 us  [the longest x1 7.63 us: partial_scores(): pl.pallas_call(partial_kernel, grid=(shards,), in_specs=[pl.BlockSpec((ro...]
    ppermute x14 -> x18, starting transfers between devices: 15.2 us -> 21.1 us  [swap(): lax.ppermute(value, axis, [(i, i ^ offset) for i in range(lax.axis_size(a...]
    ppermute x14 -> x18, waiting for transfers between devices: 24.5 us -> 29.4 us  [swap(): lax.ppermute(value, axis, [(i, i ^ offset) for i in range(lax.axis_size(a...]
    all_to_all x2 -> x1, starting transfers between devices: 9.36 us -> 7.28 us  [body(): lax.all_to_all(send_feats.reshape(dp_count, capacity, -1), 'dp', 0, 0, ti...]
    pallas_call x1 -> x0, local copies, waits for them, and re-layouts: 1.29 us -> none  [build_message(): pl.pallas_call(kernel, out_shape=(jax.ShapeDtypeStruct((1, rows), f32), j...]
    unnamed x17 -> x20, local copies, waits for them, and re-layouts: 5.05 us -> 4.71 us
  transfers between devices with their start and end apart: 16 -> 19, of which waited for: 10 -> 11; matrix products, arithmetic and copies ran while one was open for 3% -> 1% of each run, Pallas kernels for 4% -> 13%
where the time goes in v2:
time: 102 us
  waiting for transfers between devices  29.4 us (29%)
  starting transfers between devices  28.4 us (28%)
  Pallas kernels  24.9 us (24%)
  blocking collectives  10.8 us (11%)
  local copies, waits for them, and re-layouts  6.23 us (6%)
  other arithmetic  1.08 us (1%)
    ppermute x18, waiting for transfers between devices, swap(): lax.ppermute(value, axis, [(i, i ^ offset) for i in range(lax.axis_size(a...  29.4 us
    ppermute x18, starting transfers between devices, swap(): lax.ppermute(value, axis, [(i, i ^ offset) for i in range(lax.axis_size(a...  21.1 us
    all_to_all x1, blocking collectives, body(): lax.all_to_all(new_scores.reshape(dp_count, 1, capacity), 'dp', 0, 0, til...  10.8 us
    pallas_call x1, Pallas kernels, partial_scores(): pl.pallas_call(partial_kernel, grid=(shards,), in_specs=[pl.BlockSpec((ro...  7.63 us
    all_to_all x1, starting transfers between devices, body(): lax.all_to_all(send_feats.reshape(dp_count, capacity, -1), 'dp', 0, 0, ti...  7.28 us
    unnamed x20, local copies, waits for them, and re-layouts  4.71 us
    pallas_call x2, Pallas kernels, gradient_partial(): pl.pallas_call(kernel, out_shape=jax.ShapeDtypeStruct((blocks // 2, width...  4.64 us
    pallas_call x1, Pallas kernels, solve_members(): pl.pallas_call(solve_kernel, out_shape=(jax.ShapeDtypeStruct(member_coef....  4.33 us
  transfers between devices with their start and end apart: 19, of which 11 were waited for; matrix products, arithmetic and copies ran while one was open for 1% of the time, Pallas kernels for 13%

profile of v2, /device:TPU:0, one launch (start us, length us, event | category | flops | bytes accessed | tf_op | source)
XLA Modules:
  0.0 101.6 jit_solution(4880484793685526621)
XLA Ops:
  0.6 3.3 %pack_feats.1 = bf16[2048,256]{1,0:T(8,128)(2,1)} custom-call(bf16[1024,256]{1,0:T(8,128)(2,1)} %feats_ref.1, s32[1,1024]{1,0:T(1,128)} %bitcast.47), custom_call_target="tpu_custom_call" | custom-call | flops 1073741824 | bytes 1572864 | tf_op jit(solution)/shard_map/pack_feats/pallas_call | solution.py:145
  3.9 7.3 %all-to-all-start = ((bf16[8,256,256]{2,1,0:T(8,128)(2,1)}), bf16[8,256,256]{2,1,0:T(8,128)(2,1)S(1)}, u32[]{:S(2)}, u32[]{:S(2)}) async-start(bf16[8,256,256]{2,1,0:T(8,128)(2,1)} %bitcast.44), calls=%async_computation | async-start | bytes 2097152 | tf_op jit(solution)/shard_map/all_to_all | solution.py:429
  11.2 7.6 %partial_scores.1 = (f32[1,1024]{1,0:T(1,128)}, f32[1,1024]{1,0:T(1,128)}, f32[1,1024]{1,0:T(1,128)}, f32[1,1024]{1,0:T(1,128)}) custom-call(bf16[4096,512]{1,0:T(8,128)(2,1)} %refs_0_.3, s32[1,4096]{1,0:T(1,128)} %bitcast.38, f32[512,512]{1,0:T(8,128)} %coef_ref.2), custom_call_target="tpu_custom_call" | custom-call | flops 4294967296 | bytes 5242880 | tf_op jit(solution)/shard_map/partial_scores/pallas_call | solution.py:72
  18.9 1.6 %collective-permute-start.1 = (f32[1,1024]{1,0:T(1,128)}, f32[1,1024]{1,0:T(1,128)S(1)}, u32[]{:S(2)}, u32[]{:S(2)}) collective-permute-start(f32[1,1024]{1,0:T(1,128)} %get-tuple-element.15), channel_id=1, source_target_pairs={{0,2},{1,3},{2,0},{3,1},{4,6},{5,7},{6,4},{7,5},{8,10},{9,11},{10,... | collective-permute-start | bytes 12296 | tf_op jit(solution)/shard_map/ppermute | solution.py:333
  20.7 2.0 %collective-permute-done.1.refs_2_ = f32[1,1024]{1,0:T(1,128)S(1)} collective-permute-done((f32[1,1024]{1,0:T(1,128)}, f32[1,1024]{1,0:T(1,128)S(1)}, u32[]{:S(2)}, u32[]{:S(2)}) %collective-permute-start.1) | collective-permute-done | bytes 4128 | tf_op jit(solution)/shard_map/ppermute | solution.py:333
  24.3 1.6 %build_message.1 = (f32[1,1024]{1,0:T(1,128)}, f32[8,2,256]{2,1,0:T(2,128)}) custom-call(f32[1,1024]{1,0:T(1,128)} %get-tuple-element.13.refs_0_, f32[1,1024]{1,0:T(1,128)} %copy-done.7, f32[1,1024]{1,0:T(1,128)} %copy-done.8, f32[1,1024]{1,0:T(1,128)} %copy-done.9, s32[1,1024]{1,0:T(1,128)} %bitcast.50, s32[1,1024]{1,0:T(1,128)} %bitcast.48), custom_call_target="tpu_custom_call" | custom-call | tf_op jit(solution)/shard_map/build_message/pallas_call | solution.py:189
  26.6 2.0 %collective-permute-start.3 = (f32[4,2,256]{2,1,0:T(2,128)S(1)}, f32[4,2,256]{2,1,0:T(2,128)S(1)}, u32[]{:S(2)}, u32[]{:S(2)}) collective-permute-start(f32[4,2,256]{2,1,0:T(2,128)S(1)} %get-tuple-element.33), channel_id=1, source_target_pairs={{0,4},{4,0},{8,12},{12,8},{16,20},{20,16},{24,28},{28,24},{1,5},{5... | collective-permute-start | bytes 24584 | tf_op jit(solution)/shard_map/ppermute | solution.py:333
  28.6 1.7 %collective-permute-done.3 = f32[4,2,256]{2,1,0:T(2,128)S(1)} collective-permute-done((f32[4,2,256]{2,1,0:T(2,128)S(1)}, f32[4,2,256]{2,1,0:T(2,128)S(1)}, u32[]{:S(2)}, u32[]{:S(2)}) %collective-permute-start.3) | collective-permute-done | bytes 8224 | tf_op jit(solution)/shard_map/ppermute | solution.py:333
  30.4 2.0 %collective-permute-start.4 = (f32[2,2,256]{2,1,0:T(2,128)S(1)}, f32[2,2,256]{2,1,0:T(2,128)S(1)}, u32[]{:S(2)}, u32[]{:S(2)}) collective-permute-start(f32[2,2,256]{2,1,0:T(2,128)S(1)} %get-tuple-element.30), channel_id=1, source_target_pairs={{0,8},{4,12},{8,0},{12,4},{16,24},{20,28},{24,16},{28,20},{1,9},{5... | collective-permute-start | bytes 12296 | tf_op jit(solution)/shard_map/ppermute | solution.py:333
  33.0 1.8 %slot_members.1.member_ref = f32[8,256]{1,0:T(8,128)} custom-call(s32[4]{0:T(128)} %tiles_ref.1, s32[1,2432]{1,0:T(1,128)} %reshape.43.source_ref), custom_call_target="tpu_custom_call" | custom-call | tf_op jit(solution)/shard_map/slot_members/pallas_call | solution.py:215
  34.8 2.4 %collective-permute-start.5 = (f32[2,2,256]{2,1,0:T(2,128)S(1)}, f32[2,2,256]{2,1,0:T(2,128)S(1)}, u32[]{:S(2)}, u32[]{:S(2)}) collective-permute-start(f32[2,2,256]{2,1,0:T(2,128)S(1)} %get-tuple-element.29), channel_id=1, source_target_pairs={{0,16},{4,20},{8,24},{12,28},{16,0},{20,4},{24,8},{28,12},{1,17},{... | collective-permute-start | bytes 12296 | tf_op jit(solution)/shard_map/ppermute | solution.py:333
  38.0 1.3 %collective-permute-done.5 = f32[2,2,256]{2,1,0:T(2,128)S(1)} collective-permute-done((f32[2,2,256]{2,1,0:T(2,128)S(1)}, f32[2,2,256]{2,1,0:T(2,128)S(1)}, u32[]{:S(2)}, u32[]{:S(2)}) %collective-permute-start.5) | collective-permute-done | bytes 4128 | tf_op jit(solution)/shard_map/ppermute | solution.py:333
  39.3 3.3 %collective-permute-done.6 = f32[2,2,256]{2,1,0:T(2,128)S(1)} collective-permute-done((f32[2,2,256]{2,1,0:T(2,128)S(1)}, f32[2,2,256]{2,1,0:T(2,128)S(1)}, u32[]{:S(2)}, u32[]{:S(2)}) %collective-permute-start.6) | collective-permute-done | bytes 4128 | tf_op jit(solution)/shard_map/ppermute | solution.py:333
  43.5 4.3 %solve_members.1 = (f32[4,256]{1,0:T(4,128)}, f32[8,1,256]{2,1,0:T(1,128)}) custom-call(bf16[2048,256]{1,0:T(8,128)(2,1)} %bitcast.41, f32[8,2,256]{2,1,0:T(2,128)} %bitcast.45, f32[8,256]{1,0:T(8,128)} %slot_members.1.member_ref, f32[4,256]{1,0:T(4,128)} %coef_ref.3), custom_call_target="tpu_custom_call" | custom-call | tf_op jit(solution)/shard_map/solve_members/pallas_call | solution.py:301
  47.9 10.8 %all_to_all.10.returned_ref = f32[8,1,256]{2,1,0:T(1,128)} all-to-all(f32[8,1,256]{2,1,0:T(1,128)} %get-tuple-element.18), channel_id=1, replica_groups=mesh['dp'=8,'feat'=4] {'dp'}, dimensions={0} | all-to-all | bytes 16384 | tf_op jit(solution)/shard_map/all_to_all | solution.py:445
  58.7 1.6 %margins.1 = (f32[1,1024]{1,0:T(1,128)}, f32[1,1024]{1,0:T(1,128)}) custom-call(f32[8,1,256]{2,1,0:T(1,128)} %all_to_all.10.returned_ref, s32[1,1024]{1,0:T(1,128)} %bitcast.49, f32[1,1024]{1,0:T(1,128)} %get-tuple-element.19.fixed_ref, s32[1,1024]{1,0:T(1,128)} %bitcast.51), custom_call_target="tpu_custom_call" | custom-call | tf_op jit(solution)/shard_map/margins/pallas_call | solution.py:327
  61.1 1.7 %collective-permute-start.9 = (f32[1,1024]{1,0:T(1,128)S(1)}, f32[1,1024]{1,0:T(1,128)S(1)}, u32[]{:S(2)}, u32[]{:S(2)}) collective-permute-start(f32[1,1024]{1,0:T(1,128)S(1)} %broadcast_multiply_fusion.refs_2_), channel_id=1, source_target_pairs={{0,3},{1,2},{2,1},{3,0},{4,7},{5,6},{6,5},{7,4},{8,11},{9,10},{10,... | collective-permute-start | bytes 12296 | tf_op jit(solution)/shard_map/ppermute | solution.py:333
  62.8 1.7 %collective-permute-done.8.refs_4_ = f32[1,1024]{1,0:T(1,128)S(1)} collective-permute-done((f32[1,1024]{1,0:T(1,128)S(1)}, f32[1,1024]{1,0:T(1,128)S(1)}, u32[]{:S(2)}, u32[]{:S(2)}) %collective-permute-start.8) | collective-permute-done | bytes 4128 | tf_op jit(solution)/shard_map/ppermute | solution.py:333
  64.6 2.2 %copy-done = bf16[4096,512]{1,0:T(8,128)(2,1)S(1)} copy-done((bf16[4096,512]{1,0:T(8,128)(2,1)S(1)}, bf16[4096,512]{1,0:T(8,128)(2,1)}, u32[]{:S(2)}) %copy-start) | copy-done | bytes 4194328
  66.7 2.3 %shard_map.113 = f32[256,512]{1,0:T(8,128)S(1)} custom-call(bf16[4096,512]{1,0:T(8,128)(2,1)S(1)} %copy-done, s32[1,4096]{1,0:T(1,128)S(1)} %bitcast.39, f32[1,1024]{1,0:T(1,128)S(1)} %broadcast_multiply_fusion.refs_2_, f32[1,1024]{1,0:T(1,128)S(1)} %collective-permute-done.7.refs_3_, f32[1,1024]{1,0:T(1,128)S(1)} %collective-permute-done.8.refs_4_, ...), custom_call_target="tpu_custom_call" | custom-call | flops 2147483648 | bytes 4718592 | tf_op jit(solution)/shard_map/pallas_call | solution.py:122
  69.7 2.3 %shard_map.112 = f32[256,512]{1,0:T(8,128)S(1)} custom-call(bf16[4096,512]{1,0:T(8,128)(2,1)S(1)} %copy-done, s32[1,4096]{1,0:T(1,128)S(1)} %bitcast.40, f32[1,1024]{1,0:T(1,128)S(1)} %broadcast_multiply_fusion.refs_2_, f32[1,1024]{1,0:T(1,128)S(1)} %collective-permute-done.7.refs_3_, f32[1,1024]{1,0:T(1,128)S(1)} %collective-permute-done.8.refs_4_, ...), custom_call_target="tpu_custom_call" | custom-call | flops 2147483648 | bytes 4718592 | tf_op jit(solution)/shard_map/pallas_call | solution.py:122
  72.1 5.4 %collective-permute-done.10 = f16[256,512]{1,0:T(8,128)(2,1)S(1)} collective-permute-done((f16[256,512]{1,0:T(8,128)(2,1)S(1)}, f16[256,512]{1,0:T(8,128)(2,1)S(1)}, u32[]{:S(2)}, u32[]{:S(2)}) %collective-permute-start.10) | collective-permute-done | bytes 262176 | tf_op jit(solution)/shard_map/ppermute | solution.py:333
  78.3 1.1 %collective-permute-start.12 = (f16[64,512]{1,0:T(8,128)(2,1)S(1)}, f16[64,512]{1,0:T(8,128)(2,1)S(1)}, u32[]{:S(2)}, u32[]{:S(2)}) collective-permute-start(f16[64,512]{1,0:T(8,128)(2,1)S(1)} %get-tuple-element.27), channel_id=1, source_target_pairs={{0,16},{4,20},{8,24},{12,28},{16,0},{20,4},{24,8},{28,12},{1,17},{... | collective-permute-start | bytes 196616 | tf_op jit(solution)/shard_map/ppermute | solution.py:333
  79.4 2.8 %collective-permute-start.13 = (f16[64,512]{1,0:T(8,128)(2,1)S(1)}, f16[64,512]{1,0:T(8,128)(2,1)S(1)}, u32[]{:S(2)}, u32[]{:S(2)}) collective-permute-start(f16[64,512]{1,0:T(8,128)(2,1)S(1)} %get-tuple-element.26), channel_id=1, source_target_pairs={{0,24},{4,28},{8,16},{12,20},{16,8},{20,12},{24,0},{28,4},{1,25},{... | collective-permute-start | bytes 196616 | tf_op jit(solution)/shard_map/ppermute | solution.py:333
  82.2 3.5 %collective-permute-done.12 = f16[64,512]{1,0:T(8,128)(2,1)S(1)} collective-permute-done((f16[64,512]{1,0:T(8,128)(2,1)S(1)}, f16[64,512]{1,0:T(8,128)(2,1)S(1)}, u32[]{:S(2)}, u32[]{:S(2)}) %collective-permute-start.12) | collective-permute-done | bytes 65568 | tf_op jit(solution)/shard_map/ppermute | solution.py:333
  86.4 3.6 %collective-permute-done.14 = f16[64,512]{1,0:T(8,128)(2,1)S(1)} collective-permute-done((f16[64,512]{1,0:T(8,128)(2,1)S(1)}, f16[64,512]{1,0:T(8,128)(2,1)S(1)}, u32[]{:S(2)}, u32[]{:S(2)}) %collective-permute-start.14) | collective-permute-done | bytes 65568 | tf_op jit(solution)/shard_map/ppermute | solution.py:333
  90.2 1.3 %collective-permute-start.15 = (f16[128,512]{1,0:T(8,128)(2,1)S(1)}, f16[128,512]{1,0:T(8,128)(2,1)S(1)}, u32[]{:S(2)}, u32[]{:S(2)}) collective-permute-start(f16[128,512]{1,0:T(8,128)(2,1)S(1)} %get-tuple-element.24), channel_id=1, source_target_pairs={{0,8},{4,12},{8,0},{12,4},{16,24},{20,28},{24,16},{28,20},{1,9},{5... | collective-permute-start | bytes 393224 | tf_op jit(solution)/shard_map/ppermute | solution.py:333
  91.6 1.9 %collective-permute-start.16 = (f16[128,512]{1,0:T(8,128)(2,1)S(1)}, f16[128,512]{1,0:T(8,128)(2,1)S(1)}, u32[]{:S(2)}, u32[]{:S(2)}) collective-permute-start(f16[128,512]{1,0:T(8,128)(2,1)S(1)} %get-tuple-element.24), channel_id=1, source_target_pairs={{0,16},{4,20},{8,24},{12,28},{16,0},{20,4},{24,8},{28,12},{1,17},{... | collective-permute-start | bytes 393224 | tf_op jit(solution)/shard_map/ppermute | solution.py:333
  93.4 1.3 %collective-permute-start.17 = (f16[128,512]{1,0:T(8,128)(2,1)S(1)}, f16[128,512]{1,0:T(8,128)(2,1)S(1)}, u32[]{:S(2)}, u32[]{:S(2)}) collective-permute-start(f16[128,512]{1,0:T(8,128)(2,1)S(1)} %get-tuple-element.24), channel_id=1, source_target_pairs={{0,24},{4,28},{8,16},{12,20},{16,8},{20,12},{24,0},{28,4},{1,25},{... | collective-permute-start | bytes 393224 | tf_op jit(solution)/shard_map/ppermute | solution.py:333
  94.7 2.5 %collective-permute-done.15 = f16[128,512]{1,0:T(8,128)(2,1)S(1)} collective-permute-done((f16[128,512]{1,0:T(8,128)(2,1)S(1)}, f16[128,512]{1,0:T(8,128)(2,1)S(1)}, u32[]{:S(2)}, u32[]{:S(2)}) %collective-permute-start.15) | collective-permute-done | bytes 131104 | tf_op jit(solution)/shard_map/ppermute | solution.py:333
  97.2 3.3 %collective-permute-done.16 = f16[128,512]{1,0:T(8,128)(2,1)S(1)} collective-permute-done((f16[128,512]{1,0:T(8,128)(2,1)S(1)}, f16[128,512]{1,0:T(8,128)(2,1)S(1)}, u32[]{:S(2)}, u32[]{:S(2)}) %collective-permute-start.16) | collective-permute-done | bytes 131104 | tf_op jit(solution)/shard_map/ppermute | solution.py:333
  100.7 1.0 copy-done.4
  (54 shorter events, 8.3 us)
Async XLA Ops:
  3.9 38.6 %all-to-all-start = ((bf16[8,256,256]{2,1,0:T(8,128)(2,1)}), bf16[8,256,256]{2,1,0:T(8,128)(2,1)S(1)}, u32[]{:S(2)}, u32[]{:S(2)}) async-start(bf16[8,256,256]{2,1,0:T(8,128)(2,1)} %bitcast.44), calls=%async_computation | async-start | bytes 2097152 | tf_op jit(solution)/shard_map/all_to_all | solution.py:429
  11.2 21.2 %copy-start.6 = (s32[2432]{0:T(1024)S(1)}, s32[2432]{0:T(1024)}, u32[]{:S(2)}) copy-start(s32[2432]{0:T(1024)} %param.16) | copy-start | bytes 29188
  11.2 53.3 %copy-start.1 = (s32[4096,1]{0,1:T(1,128)S(1)}, s32[4096,1]{0,1:T(1,128)}, u32[]{:S(2)}) copy-start(s32[4096,1]{0,1:T(1,128)} %param.12) | copy-start | bytes 49156
  18.9 1.9 %collective-permute-start = (f32[1,1024]{1,0:T(1,128)}, f32[1,1024]{1,0:T(1,128)S(1)}, u32[]{:S(2)}, u32[]{:S(2)}) collective-permute-start(f32[1,1024]{1,0:T(1,128)} %get-tuple-element.14), channel_id=1, source_target_pairs={{0,1},{1,0},{2,3},{3,2},{4,5},{5,4},{6,7},{7,6},{8,9},{9,8},{10,11... | collective-permute-start | bytes 12296 | tf_op jit(solution)/shard_map/ppermute | solution.py:333
  18.9 3.9 %collective-permute-start.1 = (f32[1,1024]{1,0:T(1,128)}, f32[1,1024]{1,0:T(1,128)S(1)}, u32[]{:S(2)}, u32[]{:S(2)}) collective-permute-start(f32[1,1024]{1,0:T(1,128)} %get-tuple-element.15), channel_id=1, source_target_pairs={{0,2},{1,3},{2,0},{3,1},{4,6},{5,7},{6,4},{7,5},{8,10},{9,11},{10,... | collective-permute-start | bytes 12296 | tf_op jit(solution)/shard_map/ppermute | solution.py:333
  20.5 3.2 %collective-permute-start.2 = (f32[1,1024]{1,0:T(1,128)}, f32[1,1024]{1,0:T(1,128)S(1)}, u32[]{:S(2)}, u32[]{:S(2)}) collective-permute-start(f32[1,1024]{1,0:T(1,128)} %get-tuple-element.16), channel_id=1, source_target_pairs={{0,3},{1,2},{2,1},{3,0},{4,7},{5,6},{6,5},{7,4},{8,11},{9,10},{10,... | collective-permute-start | bytes 12296 | tf_op jit(solution)/shard_map/ppermute | solution.py:333
  20.7 3.0 %copy-start.7 = (f32[1,1024]{1,0:T(1,128)}, f32[1,1024]{1,0:T(1,128)S(1)}, u32[]{:S(2)}) copy-start(f32[1,1024]{1,0:T(1,128)S(1)} %collective-permute-done.refs_1_) | copy-start | bytes 12292
  22.8 1.0 copy-start.8
  23.7 0.6 copy-start.9
  26.6 3.7 %collective-permute-start.3 = (f32[4,2,256]{2,1,0:T(2,128)S(1)}, f32[4,2,256]{2,1,0:T(2,128)S(1)}, u32[]{:S(2)}, u32[]{:S(2)}) collective-permute-start(f32[4,2,256]{2,1,0:T(2,128)S(1)} %get-tuple-element.33), channel_id=1, source_target_pairs={{0,4},{4,0},{8,12},{12,8},{16,20},{20,16},{24,28},{28,24},{1,5},{5... | collective-permute-start | bytes 24584 | tf_op jit(solution)/shard_map/ppermute | solution.py:333
  30.4 7.5 %collective-permute-start.4 = (f32[2,2,256]{2,1,0:T(2,128)S(1)}, f32[2,2,256]{2,1,0:T(2,128)S(1)}, u32[]{:S(2)}, u32[]{:S(2)}) collective-permute-start(f32[2,2,256]{2,1,0:T(2,128)S(1)} %get-tuple-element.30), channel_id=1, source_target_pairs={{0,8},{4,12},{8,0},{12,4},{16,24},{20,28},{24,16},{28,20},{1,9},{5... | collective-permute-start | bytes 12296 | tf_op jit(solution)/shard_map/ppermute | solution.py:333
  34.8 4.5 %collective-permute-start.5 = (f32[2,2,256]{2,1,0:T(2,128)S(1)}, f32[2,2,256]{2,1,0:T(2,128)S(1)}, u32[]{:S(2)}, u32[]{:S(2)}) collective-permute-start(f32[2,2,256]{2,1,0:T(2,128)S(1)} %get-tuple-element.29), channel_id=1, source_target_pairs={{0,16},{4,20},{8,24},{12,28},{16,0},{20,4},{24,8},{28,12},{1,17},{... | collective-permute-start | bytes 12296 | tf_op jit(solution)/shard_map/ppermute | solution.py:333
  37.1 5.4 %collective-permute-start.6 = (f32[2,2,256]{2,1,0:T(2,128)S(1)}, f32[2,2,256]{2,1,0:T(2,128)S(1)}, u32[]{:S(2)}, u32[]{:S(2)}) collective-permute-start(f32[2,2,256]{2,1,0:T(2,128)S(1)} %get-tuple-element.28), channel_id=1, source_target_pairs={{0,24},{4,28},{8,16},{12,20},{16,8},{20,12},{24,0},{28,4},{1,25},{... | collective-permute-start | bytes 12296 | tf_op jit(solution)/shard_map/ppermute | solution.py:333
  42.6 0.6 copy-start.5
  42.6 1.0 copy-start.2
  60.9 1.9 %collective-permute-start.7 = (f32[1,1024]{1,0:T(1,128)S(1)}, f32[1,1024]{1,0:T(1,128)S(1)}, u32[]{:S(2)}, u32[]{:S(2)}) collective-permute-start(f32[1,1024]{1,0:T(1,128)S(1)} %broadcast_multiply_fusion.refs_2_), channel_id=1, source_target_pairs={{0,1},{1,0},{2,3},{3,2},{4,5},{5,4},{6,7},{7,6},{8,9},{9,8},{10,11... | collective-permute-start | bytes 12296 | tf_op jit(solution)/shard_map/ppermute | solution.py:333
  60.9 3.6 %collective-permute-start.8 = (f32[1,1024]{1,0:T(1,128)S(1)}, f32[1,1024]{1,0:T(1,128)S(1)}, u32[]{:S(2)}, u32[]{:S(2)}) collective-permute-start(f32[1,1024]{1,0:T(1,128)S(1)} %broadcast_multiply_fusion.refs_2_), channel_id=1, source_target_pairs={{0,2},{1,3},{2,0},{3,1},{4,6},{5,7},{6,4},{7,5},{8,10},{9,11},{10,... | collective-permute-start | bytes 12296 | tf_op jit(solution)/shard_map/ppermute | solution.py:333
  61.1 3.4 %collective-permute-start.9 = (f32[1,1024]{1,0:T(1,128)S(1)}, f32[1,1024]{1,0:T(1,128)S(1)}, u32[]{:S(2)}, u32[]{:S(2)}) collective-permute-start(f32[1,1024]{1,0:T(1,128)S(1)} %broadcast_multiply_fusion.refs_2_), channel_id=1, source_target_pairs={{0,3},{1,2},{2,1},{3,0},{4,7},{5,6},{6,5},{7,4},{8,11},{9,10},{10,... | collective-permute-start | bytes 12296 | tf_op jit(solution)/shard_map/ppermute | solution.py:333
  64.6 2.2 %copy-start = (bf16[4096,512]{1,0:T(8,128)(2,1)S(1)}, bf16[4096,512]{1,0:T(8,128)(2,1)}, u32[]{:S(2)}) copy-start(bf16[4096,512]{1,0:T(8,128)(2,1)} %refs_0_.3) | copy-start | bytes 12582916
  69.1 21.0 %copy-start.3 = (f32[512,512]{1,0:T(8,128)S(1)}, f32[512,512]{1,0:T(8,128)}, u32[]{:S(2)}) copy-start(f32[512,512]{1,0:T(8,128)} %coef_ref.2) | copy-start | bytes 3145732
  69.1 8.4 %collective-permute-start.10 = (f16[256,512]{1,0:T(8,128)(2,1)S(1)}, f16[256,512]{1,0:T(8,128)(2,1)S(1)}, u32[]{:S(2)}, u32[]{:S(2)}) collective-permute-start(f16[256,512]{1,0:T(8,128)(2,1)S(1)} %convert_element_type.33), channel_id=1, source_target_pairs={{0,4},{4,0},{8,12},{12,8},{16,20},{20,16},{24,28},{28,24},{1,5},{5... | collective-permute-start | bytes 786440 | tf_op jit(solution)/shard_map/ppermute | solution.py:333
  77.7 4.5 %collective-permute-start.11 = (f16[64,512]{1,0:T(8,128)(2,1)S(1)}, f16[64,512]{1,0:T(8,128)(2,1)S(1)}, u32[]{:S(2)}, u32[]{:S(2)}) collective-permute-start(f16[64,512]{1,0:T(8,128)(2,1)S(1)} %get-tuple-element.25), channel_id=1, source_target_pairs={{0,8},{4,12},{8,0},{12,4},{16,24},{20,28},{24,16},{28,20},{1,9},{5... | collective-permute-start | bytes 196616 | tf_op jit(solution)/shard_map/ppermute | solution.py:333
  78.3 7.4 %collective-permute-start.12 = (f16[64,512]{1,0:T(8,128)(2,1)S(1)}, f16[64,512]{1,0:T(8,128)(2,1)S(1)}, u32[]{:S(2)}, u32[]{:S(2)}) collective-permute-start(f16[64,512]{1,0:T(8,128)(2,1)S(1)} %get-tuple-element.27), channel_id=1, source_target_pairs={{0,16},{4,20},{8,24},{12,28},{16,0},{20,4},{24,8},{28,12},{1,17},{... | collective-permute-start | bytes 196616 | tf_op jit(solution)/shard_map/ppermute | solution.py:333
  79.4 6.3 %collective-permute-start.13 = (f16[64,512]{1,0:T(8,128)(2,1)S(1)}, f16[64,512]{1,0:T(8,128)(2,1)S(1)}, u32[]{:S(2)}, u32[]{:S(2)}) collective-permute-start(f16[64,512]{1,0:T(8,128)(2,1)S(1)} %get-tuple-element.26), channel_id=1, source_target_pairs={{0,24},{4,28},{8,16},{12,20},{16,8},{20,12},{24,0},{28,4},{1,25},{... | collective-permute-start | bytes 196616 | tf_op jit(solution)/shard_map/ppermute | solution.py:333
  85.7 4.3 %collective-permute-start.14 = (f16[64,512]{1,0:T(8,128)(2,1)S(1)}, f16[64,512]{1,0:T(8,128)(2,1)S(1)}, u32[]{:S(2)}, u32[]{:S(2)}) collective-permute-start(f16[64,512]{1,0:T(8,128)(2,1)S(1)} %fusion.2), channel_id=1, source_target_pairs={{0,4},{4,0},{8,12},{12,8},{16,20},{20,16},{24,28},{28,24},{1,5},{5... | collective-permute-start | bytes 196616 | tf_op jit(solution)/shard_map/ppermute | solution.py:333
  90.2 6.9 %collective-permute-start.15 = (f16[128,512]{1,0:T(8,128)(2,1)S(1)}, f16[128,512]{1,0:T(8,128)(2,1)S(1)}, u32[]{:S(2)}, u32[]{:S(2)}) collective-permute-start(f16[128,512]{1,0:T(8,128)(2,1)S(1)} %get-tuple-element.24), channel_id=1, source_target_pairs={{0,8},{4,12},{8,0},{12,4},{16,24},{20,28},{24,16},{28,20},{1,9},{5... | collective-permute-start | bytes 393224 | tf_op jit(solution)/shard_map/ppermute | solution.py:333
  91.6 9.0 %collective-permute-start.16 = (f16[128,512]{1,0:T(8,128)(2,1)S(1)}, f16[128,512]{1,0:T(8,128)(2,1)S(1)}, u32[]{:S(2)}, u32[]{:S(2)}) collective-permute-start(f16[128,512]{1,0:T(8,128)(2,1)S(1)} %get-tuple-element.24), channel_id=1, source_target_pairs={{0,16},{4,20},{8,24},{12,28},{16,0},{20,4},{24,8},{28,12},{1,17},{... | collective-permute-start | bytes 393224 | tf_op jit(solution)/shard_map/ppermute | solution.py:333
  93.4 7.2 %collective-permute-start.17 = (f16[128,512]{1,0:T(8,128)(2,1)S(1)}, f16[128,512]{1,0:T(8,128)(2,1)S(1)}, u32[]{:S(2)}, u32[]{:S(2)}) collective-permute-start(f16[128,512]{1,0:T(8,128)(2,1)S(1)} %get-tuple-element.24), channel_id=1, source_target_pairs={{0,24},{4,28},{8,16},{12,20},{16,8},{20,12},{24,0},{28,4},{1,25},{... | collective-permute-start | bytes 393224 | tf_op jit(solution)/shard_map/ppermute | solution.py:333
  100.7 1.0 copy-start.4

commit v3 on v2

--- a/solution.py
+++ b/solution.py
@@ -44,133 +44,230 @@
     return 1.0 / (1.0 + jnp.exp(-x))
 
 
-def partial_kernel(values_ref, block_ref, coef_ref, *refs):
-    outs, (high_ref, low_ref) = refs[:-2], refs[-2:]
-
-    @pl.when(pl.program_id(0) == 0)
-    def _():
-        high, low = split(coef_ref[...], 2)
-        high_ref[...] = high
-        low_ref[...] = low
-
-    values = values_ref[...]
-    product = dot_nt(high_ref[...], values) + dot_nt(low_ref[...], values)
-    mask = hot(block_ref[...], product.shape[0])
-    score = jnp.sum(jnp.where(mask, product, 0.0), axis=0, keepdims=True)
-    target = pl.program_id(0) ^ lax.axis_index("feat")
-    for k, out_ref in enumerate(outs):
-
-        @pl.when(target == k)
-        def _():
-            out_ref[...] = score
-
-
-def partial_scores(fixed_values, block_row, fixed_coef, rows_here):
+def compiler_params(mebibytes=50):
+    return pltpu.CompilerParams(vmem_limit_bytes=mebibytes << 20)
+
+
+def partial_kernel(
+    start_ref, values_ref, block_ref, coef_ref, label_ref, slot_ref, out_ref, rest_ref, sem
+):
+    rows = out_ref.shape[1]
+    blocks = coef_ref.shape[0]
+    shards = values_ref.shape[0] // rows
+    copies = [
+        pltpu.make_async_copy(
+            values_ref.at[pl.ds((i + 1) * rows, rows)], rest_ref.at[i], sem.at[i]
+        )
+        for i in range(shards - 1)
+    ]
+    for copy in copies:
+        copy.start()
+    high, low = split(coef_ref[...].T, 2)
+    lanes = lax.broadcasted_iota(jnp.int32, (1, TILE), 1)
+    out_ref[shards : shards + 1, :] = label_ref[...].astype(f32)
+    out_ref[shards + 1 : shards + 2, :] = slot_ref[...].astype(f32)
+    for i in range(shards):
+        block = block_ref[:, i * rows : (i + 1) * rows]
+        column = jnp.broadcast_to(block, (TILE, rows)).T
+        if i > 0:
+            copies[i - 1].wait()
+        values = start_ref[...] if i == 0 else rest_ref[i - 1]
+        product = dot_nn(values, high) + dot_nn(values, low)
+        total = jnp.zeros((rows, TILE), f32)
+        for at in range(0, blocks, TILE):
+            total = total + jnp.where(column == lanes + at, product[:, at : at + TILE], 0.0)
+        out_ref[i : i + 1, :] = jnp.sum(total.T, axis=0, keepdims=True)
+
+
+def partial_scores(start, fixed_values, block_row, fixed_coef, label_row, slot_row):
     rows, width = fixed_values.shape
+    rows_here = slot_row.shape[1]
     blocks = fixed_coef.shape[0]
     shards = rows // rows_here
+    vmem = pl.BlockSpec(memory_space=pltpu.VMEM)
     return pl.pallas_call(
         partial_kernel,
-        grid=(shards,),
-        in_specs=[
-            pl.BlockSpec((rows_here, width), lambda i: (i, 0)),
-            pl.BlockSpec((1, rows_here), lambda i: (0, i)),
-            pl.BlockSpec((blocks, width), lambda i: (0, 0)),
+        in_specs=[vmem, pl.BlockSpec(memory_space=pltpu.HBM)] + [vmem] * 4,
+        out_specs=vmem,
+        out_shape=jax.ShapeDtypeStruct((shards + 2, rows_here), f32),
+        scratch_shapes=[
+            pltpu.VMEM((shards - 1, rows_here, width), bf16),
+            pltpu.SemaphoreType.DMA((shards - 1,)),
         ],
-        out_specs=[pl.BlockSpec((1, rows_here), lambda i: (0, 0))] * shards,
-        out_shape=[jax.ShapeDtypeStruct((1, rows_here), f32)] * shards,
-        scratch_shapes=[pltpu.VMEM((blocks, width), bf16)] * 2,
         cost_estimate=pl.CostEstimate(
             flops=4 * rows * blocks * width,
             bytes_accessed=2 * rows * width + 4 * blocks * width,
             transcendentals=0,
         ),
+        compiler_params=compiler_params(50),
         name="partial_scores",
-    )(fixed_values, block_row, fixed_coef)
-
-
-def grad_kernel(flip, dp_count, values_ref, block_ref, *refs):
-    pieces, out_ref = refs[:-1], refs[-1]
+    )(start, fixed_values, block_row, fixed_coef, label_row, slot_row)
+
+
+def add_blocks(
+    flip, dp_count, values_ref, block_ref, residual_rows, out_ref, first=True
+):
     kept = out_ref.shape[0]
     chunk = 2 * kept // dp_count
-    rows = pieces[0].shape[1]
+    rows = residual_rows[0].shape[1]
     parity = (lax.axis_index("dp") + flip) % 2
-    feat = lax.axis_index("feat")
-    for k, piece in enumerate(pieces):
-        at = pl.ds(pl.multiple_of((feat ^ k) * rows, rows), rows)
-        block = block_ref[:, at]
+    for i, residual in enumerate(residual_rows):
+        block = block_ref[:, i * rows : (i + 1) * rows]
         local = (block // (2 * chunk)) * chunk + block % chunk
         local = jnp.where((block // chunk) % 2 == parity, local, -1)
         mask = hot(local, kept)
-        high, low = split(piece[...], 2)
+        high, low = split(residual, 2)
         left_high = jnp.where(mask, high.astype(f32), 0.0).astype(bf16)
         left_low = jnp.where(mask, low.astype(f32), 0.0).astype(bf16)
-        values = values_ref[at, :]
+        values = values_ref[i * rows : (i + 1) * rows, :]
         total = dot_nn(left_high, values) + dot_nn(left_low, values)
-        if k == 0:
+        if first is True and i == 0:
             out_ref[...] = total
+        elif first is True:
+            out_ref[...] += total
         else:
-            out_ref[...] += total
-
-
-def gradient_partial(flip, dp_count, fixed_values, block_row, pieces, blocks):
+            out_ref[...] = jnp.where(first, 0.0, out_ref[...]) + total
+
+
+def margin_kernel(
+    dp_count, returned_ref, fixed_ref, label_ref, slot_ref, values_ref, block_ref,
+    margin_ref, residual_ref, out_ref, all_ref, held_ref, copy_sem,
+):
+    copy = pltpu.make_async_copy(values_ref, held_ref, copy_sem)
+    copy.start()
+    sources, _, capacity = returned_ref.shape
+    shards, _ = fixed_ref.shape
+    pieces = split(returned_ref[...].reshape(sources, capacity), 3)
+    table = jnp.concatenate(pieces, axis=0)
+    residual_rows = []
+    for i in range(shards):
+        slot = slot_ref[i : i + 1, :].astype(jnp.int32)
+        owner = slot // capacity
+        place_hot = jnp.where(hot(slot - owner * capacity, capacity), 1.0, 0.0).astype(bf16)
+        found = dot_nn(table, place_hot)
+        found = found[:sources] + (found[sources : 2 * sources] + found[2 * sources :])
+        owner_hot = hot(owner * shards + i, sources)
+        score = jnp.sum(jnp.where(owner_hot, found, 0.0), axis=0, keepdims=True)
+        margin = fixed_ref[i : i + 1, :] + score
+        all_ref[i : i + 1, :] = margin
+        residual = (label_ref[i : i + 1, :] - sigmoid(margin)) * (1.0 / dp_count)
+        residual_ref[i : i + 1, :] = residual
+        residual_rows.append(residual)
+    margin_ref[...] = all_ref[pl.ds(lax.axis_index("feat"), 1), :]
+    copy.wait()
+    add_blocks(1, dp_count, held_ref, block_ref, residual_rows, out_ref)
+
+
+def margins_and_theirs(returned, fixed, label, slot, fixed_values, block_row, blocks, dp_count):
+    shards, rows = fixed.shape
+    width = fixed_values.shape[1]
+
+    def kernel(*refs):
+        margin_kernel(dp_count, *refs)
+
+    vmem = pl.BlockSpec(memory_space=pltpu.VMEM)
+    return pl.pallas_call(
+        kernel,
+        in_specs=[vmem] * 4 + [pl.BlockSpec(memory_space=pltpu.HBM), vmem],
+        out_specs=[vmem] * 3,
+        out_shape=(
+            jax.ShapeDtypeStruct((1, rows), f32),
+            jax.ShapeDtypeStruct((shards, rows), f32),
+            jax.ShapeDtypeStruct((blocks // 2, width), f32),
+        ),
+        scratch_shapes=[
+            pltpu.VMEM((shards, rows), f32),
+            pltpu.VMEM(fixed_values.shape, fixed_values.dtype),
+            pltpu.SemaphoreType.DMA,
+        ],
+        compiler_params=compiler_params(50),
+        name="margins_and_theirs",
+    )(returned, fixed, label, slot, fixed_values, block_row)
+
+
+def mine_kernel(dp_count, residual_ref, values_ref, block_ref, out_ref):
+    residual = residual_ref[pl.ds(pl.program_id(0), 1), :]
+    add_blocks(0, dp_count, values_ref, block_ref, [residual], out_ref, pl.program_id(0) == 0)
+
+
+def gradient_mine(residual, fixed_values, block_row, blocks, dp_count):
     rows, width = fixed_values.shape
+    shards, rows_here = residual.shape
 
     def kernel(*refs):
-        grad_kernel(flip, dp_count, *refs)
+        mine_kernel(dp_count, *refs)
 
     return pl.pallas_call(
         kernel,
+        grid=(shards,),
+        in_specs=[
+            pl.BlockSpec((shards, rows_here), lambda i: (0, 0)),
+            pl.BlockSpec((rows_here, width), lambda i: (i, 0)),
+            pl.BlockSpec((1, rows_here), lambda i: (0, i)),
+        ],
+        out_specs=pl.BlockSpec((blocks // 2, width), lambda i: (0, 0)),
         out_shape=jax.ShapeDtypeStruct((blocks // 2, width), f32),
         cost_estimate=pl.CostEstimate(
             flops=2 * rows * blocks * width,
             bytes_accessed=2 * rows * width + 2 * blocks * width,
             transcendentals=0,
         ),
-        compiler_params=pltpu.CompilerParams(vmem_limit_bytes=24 << 20),
-    )(fixed_values, block_row, *pieces)
-
-
-def pack_kernel(feats_ref, slot_ref, out_ref):
-    count = out_ref.shape[0]
-    start = pl.program_id(0) * count
-    mask = (rows_iota((count, slot_ref.shape[1])) + start) == slot_ref[...]
-    one_hot = jnp.where(mask, 1.0, 0.0).astype(bf16)
-    out_ref[...] = dot_nn(one_hot, feats_ref[...]).astype(bf16)
-
-
-def pack_feats(member_feats, slot_row, slot_total):
+        compiler_params=compiler_params(50),
+        name="gradient_mine",
+    )(residual, fixed_values, block_row)
+
+
+def pack_kernel(values_ref, feats_ref, slot_ref, out_ref, start_ref, copy_sem):
+    first = values_ref.at[pl.ds(0, start_ref.shape[0])]
+    copy = pltpu.make_async_copy(first, start_ref, copy_sem)
+    copy.start()
+    total = out_ref.shape[0]
+    step = min(1024, total)
+    for start in range(0, total, step):
+        mask = (rows_iota((step, slot_ref.shape[1])) + start) == slot_ref[...]
+        one_hot = jnp.where(mask, 1.0, 0.0).astype(bf16)
+        out_ref[start : start + step, :] = dot_nn(one_hot, feats_ref[...]).astype(bf16)
+    copy.wait()
+
+
+def pack_feats(fixed_values, member_feats, slot_row, slot_total):
     rows, width = member_feats.shape
-    step = min(1024, slot_total)
+    vmem = pl.BlockSpec(memory_space=pltpu.VMEM)
     return pl.pallas_call(
         pack_kernel,
-        grid=(slot_total // step,),
-        in_specs=[
-            pl.BlockSpec((rows, width), lambda i: (0, 0)),
-            pl.BlockSpec((1, rows), lambda i: (0, 0)),
-        ],
-        out_specs=pl.BlockSpec((step, width), lambda i: (i, 0)),
-        out_shape=jax.ShapeDtypeStruct((slot_total, width), bf16),
+        in_specs=[pl.BlockSpec(memory_space=pltpu.HBM), vmem, vmem],
+        out_specs=[vmem, vmem],
+        out_shape=(
+            jax.ShapeDtypeStruct((slot_total, width), bf16),
+            jax.ShapeDtypeStruct((rows, fixed_values.shape[1]), bf16),
+        ),
+        scratch_shapes=[pltpu.SemaphoreType.DMA],
         cost_estimate=pl.CostEstimate(
             flops=2 * rows * slot_total * width,
             bytes_accessed=2 * rows * width + 2 * slot_total * width,
             transcendentals=0,
         ),
+        compiler_params=compiler_params(50),
         name="pack_feats",
-    )(member_feats, slot_row)
-
-
-def message_kernel(parts_refs, label_ref, slot_ref, fixed_ref, out_ref):
-    fixed = parts_refs[0][...]
-    for part in parts_refs[1:]:
-        fixed = fixed + part[...]
+    )(fixed_values, member_feats, slot_row)
+
+
+def message_kernel(pieces, label_ref, slot_ref, fixed_ref, labels_ref, slots_ref, out_ref):
+    shards = fixed_ref.shape[0]
+    feat = lax.axis_index("feat")
+    fixed = pieces[0][:shards, :]
+    for piece in pieces[1:]:
+        fixed = fixed + piece[:shards, :]
     fixed_ref[...] = fixed
+    for k, piece in enumerate(pieces):
+        labels_ref[pl.ds(feat ^ k, 1), :] = piece[shards : shards + 1, :]
+        slots_ref[pl.ds(feat ^ k, 1), :] = piece[shards + 1 : shards + 2, :]
     destinations, _, capacity = out_ref.shape
     slot = slot_ref[...]
     owner = slot // capacity
     owner_hot = hot(owner, destinations)
     place_hot = jnp.where(hot(slot - owner * capacity, capacity), 1.0, 0.0).astype(bf16)
-    score = fixed.astype(bf16).astype(f32)
+    score = fixed_ref[pl.ds(feat, 1), :].astype(bf16).astype(f32)
     label = label_ref[...].astype(f32)
     both = jnp.concatenate(
         [jnp.where(owner_hot, score, 0.0), jnp.where(owner_hot, label, 0.0)], axis=0
@@ -180,20 +277,20 @@
     out_ref[:, 1, :] = placed[destinations:]
 
 
-def build_message(parts, label_row, slot_row, dp_count, capacity):
+def build_message(pieces, label_row, slot_row, dp_count, capacity):
     rows = slot_row.shape[1]
+    shards = len(pieces)
 
     def kernel(*refs):
-        message_kernel(refs[: len(parts)], *refs[len(parts) :])
+        message_kernel(refs[:shards], *refs[shards:])
 
     return pl.pallas_call(
         kernel,
-        out_shape=(
-            jax.ShapeDtypeStruct((1, rows), f32),
-            jax.ShapeDtypeStruct((dp_count, 2, capacity), f32),
-        ),
+        out_shape=[jax.ShapeDtypeStruct((shards, rows), f32)] * 3
+        + [jax.ShapeDtypeStruct((dp_count, 2, capacity), f32)],
+        compiler_params=compiler_params(),
         name="build_message",
-    )(*parts, label_row, slot_row)
+    )(*pieces, label_row, slot_row)
 
 
 def slot_member_kernel(tiles_ref, source_ref, out_ref):
@@ -220,6 +317,7 @@
         ],
         out_specs=pl.BlockSpec(memory_space=pltpu.VMEM),
         out_shape=jax.ShapeDtypeStruct((dp_count, capacity), f32),
+        compiler_params=compiler_params(),
         name="slot_members",
     )(member_tiles, source_row)
 
@@ -292,41 +390,23 @@
             search = scaled + (inner_next / inner_product) * search
             inner_product = inner_next
     updated_ref[...] = coef + step_sum
-    for i in range(scores_ref.shape[0]):
-        scores_ref[i] = new_scores[:, i * lanes : (i + 1) * lanes]
-
-
-def solve_members(feats, message, member_slots, member_coef):
+    copies = scores_ref.shape[0] * lanes // slots
+    for i in range(slots // lanes):
+        for copy in range(copies):
+            scores_ref[i * copies + copy] = new_scores[:, i * lanes : (i + 1) * lanes]
+
+
+def solve_members(feats, message, member_slots, member_coef, copies):
     senders, _, capacity = message.shape
     return pl.pallas_call(
         solve_kernel,
         out_shape=(
             jax.ShapeDtypeStruct(member_coef.shape, f32),
-            jax.ShapeDtypeStruct((senders, 1, capacity), f32),
+            jax.ShapeDtypeStruct((senders * copies, 1, capacity), f32),
         ),
+        compiler_params=compiler_params(),
         name="solve_members",
     )(feats, message, member_slots, member_coef)
-
-
-def margin_kernel(returned_ref, slot_ref, fixed_ref, label_ref, margin_ref, residual_ref):
-    owners, _, capacity = returned_ref.shape
-    slot = slot_ref[...]
-    owner = slot // capacity
-    place_hot = jnp.where(hot(slot - owner * capacity, capacity), 1.0, 0.0).astype(bf16)
-    pieces = split(returned_ref[...].reshape(owners, capacity), 3)
-    looked_up = dot_nn(jnp.concatenate(pieces, axis=0), place_hot)
-    looked_up = looked_up[:owners] + (looked_up[owners : 2 * owners] + looked_up[2 * owners :])
-    score = jnp.sum(jnp.where(hot(owner, owners), looked_up, 0.0), axis=0, keepdims=True)
-    margin = fixed_ref[...] + score
-    margin_ref[...] = margin
-    residual_ref[...] = label_ref[...].astype(f32) - sigmoid(margin)
-
-
-def margins(returned, slot_row, fixed_row, label_row):
-    out = jax.ShapeDtypeStruct(slot_row.shape, f32)
-    return pl.pallas_call(margin_kernel, out_shape=(out, out), name="margins")(
-        returned, slot_row, fixed_row, label_row
-    )
 
 
 def swap(value, axis, offset):
@@ -425,7 +505,7 @@
     label_row = labels.reshape(1, rows_here)
     block_row = fixed_blocks.reshape(1, group_rows)
 
-    send_feats = pack_feats(member_feats, slot_row, slot_total)
+    send_feats, start = pack_feats(fixed_values, member_feats, slot_row, slot_total)
     got_feats = lax.all_to_all(
         send_feats.reshape(dp_count, capacity, -1), "dp", 0, 0, tiled=True
     ).reshape(slot_total, -1)
@@ -433,25 +513,32 @@
         member_tiles, tile_source.reshape(1, -1), dp_count, capacity
     )
 
-    sends = partial_scores(fixed_values, block_row, fixed_coef, rows_here)
-    parts = [sends[0]] + [swap(sends[k], "feat", k) for k in range(1, feat_count)]
-    fixed_row, message = build_message(parts, label_row, slot_row, dp_count, capacity)
+    own = partial_scores(
+        start, fixed_values, block_row, fixed_coef, label_row, slot_row
+    )
+    pieces = [own] + [swap(own, "feat", k) for k in range(1, feat_count)]
+    fixed, label, slot, message = build_message(
+        pieces, label_row, slot_row, dp_count, capacity
+    )
     got = exchange(message, side, place, half)
 
     if capacity % 128:
         got = jnp.moveaxis(got, 1, 0).reshape(1, 2, slot_total)
         member_slots = member_slots.reshape(1, slot_total)
-    updated_coef, new_scores = solve_members(got_feats, got, member_slots, member_coef)
-    returned = lax.all_to_all(
-        new_scores.reshape(dp_count, 1, capacity), "dp", 0, 0, tiled=True
-    )
-    margin, residual = margins(returned, slot_row, fixed_row, label_row)
-
-    scaled = residual * (1.0 / dp_count)
-    pieces = [scaled] + [swap(scaled, "feat", k) for k in range(1, feat_count)]
-    theirs = gradient_partial(1, dp_count, fixed_values, block_row, pieces, blocks)
+        updated_coef, new_scores = solve_members(got_feats, got, member_slots, member_coef, 1)
+        new_scores = jnp.broadcast_to(
+            new_scores.reshape(dp_count, 1, 1, capacity), (dp_count, feat_count, 1, capacity)
+        ).reshape(dp_count * feat_count, 1, capacity)
+    else:
+        updated_coef, new_scores = solve_members(
+            got_feats, got, member_slots, member_coef, feat_count
+        )
+    returned = lax.all_to_all(new_scores, ("dp", "feat"), 0, 0, tiled=True)
+    margin, residual, theirs = margins_and_theirs(
+        returned, fixed, label, slot, fixed_values, block_row, blocks, dp_count
+    )
     got_half = swap(theirs.astype(f16), "dp", 1)
-    mine = gradient_partial(0, dp_count, fixed_values, block_row, pieces, blocks)
+    mine = gradient_mine(residual, fixed_values, block_row, blocks, dp_count)
     kept = mine + got_half.astype(f32)
     summed = reduce_rest(kept.reshape(half, chunk, block_width), place, 2).astype(f16)
     other = swap(summed, "dp", 1)

time: 102 us -> 90.4 us (0.89)
  Pallas kernels: 24.9 us -> 21.5 us
  local copies, waits for them, and re-layouts: 6.23 us -> 3.04 us
  waiting for transfers between devices: 29.4 us -> 26.6 us
    ppermute x18 -> x15, waiting for transfers between devices: 29.4 us -> 26.6 us  [swap(): lax.ppermute(value, axis, [(i, i ^ offset) for i in range(lax.axis_size(a...]
    unnamed x20, local copies, waits for them, and re-layouts: 4.71 us -> 2.81 us
    pallas_call x6 -> x5, Pallas kernels: 18.8 us -> 17.5 us  [the longest x1 5.6 us: partial_scores(): pl.pallas_call(partial_kernel, in_specs=[vmem, pl.BlockSpec(memory_space=...]
    pallas_call x1, Pallas kernels: 4.33 us -> 3.11 us  [solve_members(): pl.pallas_call(solve_kernel, out_shape=(jax.ShapeDtypeStruct(member_coef....]
    ppermute x18 -> x15, starting transfers between devices: 21.1 us -> 20.4 us  [swap(): lax.ppermute(value, axis, [(i, i ^ offset) for i in range(lax.axis_size(a...]
  transfers between devices with their start and end apart: 19 -> 16, of which waited for: 11 -> 11; matrix products, arithmetic and copies ran while one was open for 1% -> 0% of each run, Pallas kernels for 13% -> 13%
where the time goes in v3:
time: 90.4 us; the launch traced here: 90 us
  starting transfers between devices  27.7 us (31%)
  waiting for transfers between devices  26.6 us (29%)
  Pallas kernels  21.5 us (24%)
  blocking collectives  9.84 us (11%)
  local copies, waits for them, and re-layouts  3.04 us (3%)
    ppermute x15, waiting for transfers between devices, swap(): lax.ppermute(value, axis, [(i, i ^ offset) for i in range(lax.axis_size(a...  26.6 us
    ppermute x15, starting transfers between devices, swap(): lax.ppermute(value, axis, [(i, i ^ offset) for i in range(lax.axis_size(a...  20.4 us
    all_to_all x1, blocking collectives, body(): returned = lax.all_to_all(new_scores, ('dp', 'feat'), 0, 0, tiled=True)  9.84 us
    all_to_all x1, starting transfers between devices, body(): lax.all_to_all(send_feats.reshape(dp_count, capacity, -1), 'dp', 0, 0, ti...  7.29 us
    pallas_call x1, Pallas kernels, partial_scores(): pl.pallas_call(partial_kernel, in_specs=[vmem, pl.BlockSpec(memory_space=...  5.6 us
    pallas_call x1, Pallas kernels, gradient_mine(): pl.pallas_call(kernel, grid=(shards,), in_specs=[pl.BlockSpec((shards, ro...  4.7 us
    pallas_call x1, Pallas kernels, margins_and_theirs(): pl.pallas_call(kernel, in_specs=[vmem] * 4 + [pl.BlockSpec(memory_space=p...  4.59 us
    pallas_call x1, Pallas kernels, solve_members(): pl.pallas_call(solve_kernel, out_shape=(jax.ShapeDtypeStruct(member_coef....  3.11 us
  transfers between devices with their start and end apart: 16, of which 11 were waited for; matrix products, arithmetic and copies ran while one was open for 0% of the time, Pallas kernels for 13%

profile of v3, /device:TPU:0, one launch (start us, length us, event | category | flops | bytes accessed | tf_op | source)
XLA Modules:
  0.0 90.0 jit_solution(410530407297561950)
XLA Ops:
  0.7 1.1 %copy-done.1 = bf16[1024,256]{1,0:T(8,128)(2,1)S(1)} copy-done((bf16[1024,256]{1,0:T(8,128)(2,1)S(1)}, bf16[1024,256]{1,0:T(8,128)(2,1)}, u32[]{:S(2)}) %copy-start.1) | copy-done | bytes 524312
  1.8 0.7 copy-done.3
  2.5 2.3 %pack_feats.1 = (bf16[2048,256]{1,0:T(8,128)(2,1)}, bf16[1024,512]{1,0:T(8,128)(2,1)S(1)}) custom-call(bf16[4096,512]{1,0:T(8,128)(2,1)} %refs_1_.1, bf16[1024,256]{1,0:T(8,128)(2,1)S(1)} %copy-done.1, s32[1,1024]{1,0:T(1,128)S(1)} %bitcast.44), custom_call_target="tpu_custom_call" | custom-call | flops 1073741824 | bytes 1572864 | tf_op jit(solution)/shard_map/pack_feats/pallas_call | solution.py:236
  4.7 7.3 %all-to-all-start = ((bf16[8,256,256]{2,1,0:T(8,128)(2,1)}), bf16[8,256,256]{2,1,0:T(8,128)(2,1)S(1)}, u32[]{:S(2)}, u32[]{:S(2)}) async-start(bf16[8,256,256]{2,1,0:T(8,128)(2,1)} %bitcast.1), calls=%async_computation | async-start | bytes 2097152 | tf_op jit(solution)/shard_map/all_to_all | solution.py:509
  12.1 5.6 %partial_scores.1.refs_0_ = f32[6,1024]{1,0:T(8,128)S(1)} custom-call(bf16[1024,512]{1,0:T(8,128)(2,1)S(1)} %get-tuple-element.15.start_ref, bf16[4096,512]{1,0:T(8,128)(2,1)} %refs_1_.1, s32[1,4096]{1,0:T(1,128)S(1)} %bitcast.40, f32[512,512]{1,0:T(8,128)S(1)} %copy-done, s32[1,1024]{1,0:T(1,128)S(1)} %bitcast.47, s32[1,1024]{1,0:T(1,128)S(1)} %bitcast.45), custom_call_target="tpu_custom_call" | custom-call | flops 4294967296 | bytes 5242880 | tf_op jit(solution)/shard_map/partial_scores/pallas_call | solution.py:88
  17.8 1.6 %collective-permute-start.1 = (f32[6,1024]{1,0:T(8,128)S(1)}, f32[6,1024]{1,0:T(8,128)S(1)}, u32[]{:S(2)}, u32[]{:S(2)}) collective-permute-start(f32[6,1024]{1,0:T(8,128)S(1)} %partial_scores.1.refs_0_), channel_id=1, source_target_pairs={{0,2},{1,3},{2,0},{3,1},{4,6},{5,7},{6,4},{7,5},{8,10},{9,11},{10,... | collective-permute-start | bytes 73736 | tf_op jit(solution)/shard_map/ppermute | solution.py:413
  19.7 2.1 %collective-permute-done.1.refs_2_ = f32[6,1024]{1,0:T(8,128)S(1)} collective-permute-done((f32[6,1024]{1,0:T(8,128)S(1)}, f32[6,1024]{1,0:T(8,128)S(1)}, u32[]{:S(2)}, u32[]{:S(2)}) %collective-permute-start.1) | collective-permute-done | bytes 24608 | tf_op jit(solution)/shard_map/ppermute | solution.py:413
  21.8 1.0 %collective-permute-done.2.refs_3_ = f32[6,1024]{1,0:T(8,128)S(1)} collective-permute-done((f32[6,1024]{1,0:T(8,128)S(1)}, f32[6,1024]{1,0:T(8,128)S(1)}, u32[]{:S(2)}, u32[]{:S(2)}) %collective-permute-start.2) | collective-permute-done | bytes 24608 | tf_op jit(solution)/shard_map/ppermute | solution.py:413
  23.1 2.1 %collective-permute-start.3 = (f32[4,2,256]{2,1,0:T(2,128)S(1)}, f32[4,2,256]{2,1,0:T(2,128)S(1)}, u32[]{:S(2)}, u32[]{:S(2)}) collective-permute-start(f32[4,2,256]{2,1,0:T(2,128)S(1)} %get-tuple-element.35), channel_id=1, source_target_pairs={{0,4},{4,0},{8,12},{12,8},{16,20},{20,16},{24,28},{28,24},{1,5},{5... | collective-permute-start | bytes 24584 | tf_op jit(solution)/shard_map/ppermute | solution.py:413
  25.1 1.6 %collective-permute-done.3 = f32[4,2,256]{2,1,0:T(2,128)S(1)} collective-permute-done((f32[4,2,256]{2,1,0:T(2,128)S(1)}, f32[4,2,256]{2,1,0:T(2,128)S(1)}, u32[]{:S(2)}, u32[]{:S(2)}) %collective-permute-start.3) | collective-permute-done | bytes 8224 | tf_op jit(solution)/shard_map/ppermute | solution.py:413
  26.8 2.3 %collective-permute-start.4 = (f32[2,2,256]{2,1,0:T(2,128)S(1)}, f32[2,2,256]{2,1,0:T(2,128)S(1)}, u32[]{:S(2)}, u32[]{:S(2)}) collective-permute-start(f32[2,2,256]{2,1,0:T(2,128)S(1)} %get-tuple-element.32), channel_id=1, source_target_pairs={{0,8},{4,12},{8,0},{12,4},{16,24},{20,28},{24,16},{28,20},{1,9},{5... | collective-permute-start | bytes 12296 | tf_op jit(solution)/shard_map/ppermute | solution.py:413
  29.2 1.0 %slot_members.1.member_ref = f32[8,256]{1,0:T(8,128)S(1)} custom-call(s32[4]{0:T(128)S(1)} %copy-done.7, s32[1,2432]{1,0:T(1,128)S(1)} %reshape.43.source_ref), custom_call_target="tpu_custom_call" | custom-call | tf_op jit(solution)/shard_map/slot_members/pallas_call | solution.py:312
  30.1 3.4 %collective-permute-start.5 = (f32[2,2,256]{2,1,0:T(2,128)S(1)}, f32[2,2,256]{2,1,0:T(2,128)S(1)}, u32[]{:S(2)}, u32[]{:S(2)}) collective-permute-start(f32[2,2,256]{2,1,0:T(2,128)S(1)} %get-tuple-element.31), channel_id=1, source_target_pairs={{0,16},{4,20},{8,24},{12,28},{16,0},{20,4},{24,8},{28,12},{1,17},{... | collective-permute-start | bytes 12296 | tf_op jit(solution)/shard_map/ppermute | solution.py:413
  33.6 4.5 %collective-permute-done.5 = f32[2,2,256]{2,1,0:T(2,128)S(1)} collective-permute-done((f32[2,2,256]{2,1,0:T(2,128)S(1)}, f32[2,2,256]{2,1,0:T(2,128)S(1)}, u32[]{:S(2)}, u32[]{:S(2)}) %collective-permute-start.5) | collective-permute-done | bytes 4128 | tf_op jit(solution)/shard_map/ppermute | solution.py:413
  38.1 0.9 %collective-permute-done.6 = f32[2,2,256]{2,1,0:T(2,128)S(1)} collective-permute-done((f32[2,2,256]{2,1,0:T(2,128)S(1)}, f32[2,2,256]{2,1,0:T(2,128)S(1)}, u32[]{:S(2)}, u32[]{:S(2)}) %collective-permute-start.6) | collective-permute-done | bytes 4128 | tf_op jit(solution)/shard_map/ppermute | solution.py:413
  39.0 3.1 %solve_members.1 = (f32[4,256]{1,0:T(4,128)}, f32[32,1,256]{2,1,0:T(1,128)S(1)}) custom-call(bf16[2048,256]{1,0:T(8,128)(2,1)S(1)} %bitcast.38, f32[8,2,256]{2,1,0:T(2,128)S(1)} %bitcast.39, f32[8,256]{1,0:T(8,128)S(1)} %slot_members.1.member_ref, f32[4,256]{1,0:T(4,128)S(1)} %copy-done.5), custom_call_target="tpu_custom_call" | custom-call | tf_op jit(solution)/shard_map/solve_members/pallas_call | solution.py:401
  42.1 9.8 %all_to_all.10.refs_0_ = f32[32,1,256]{2,1,0:T(1,128)S(1)} all-to-all(f32[32,1,256]{2,1,0:T(1,128)S(1)} %get-tuple-element.17), channel_id=1, replica_groups=mesh['dp'=8,'feat'=4] {'dp','feat'}, dimensions={0} | all-to-all | bytes 65536 | tf_op jit(solution)/shard_map/all_to_all | solution.py:536
  51.9 4.6 %margins_and_theirs.1 = (f32[1,1024]{1,0:T(1,128)}, f32[4,1024]{1,0:T(4,128)S(1)}, f32[256,512]{1,0:T(8,128)S(1)}) custom-call(f32[32,1,256]{2,1,0:T(1,128)S(1)} %all_to_all.10.refs_0_, f32[4,1024]{1,0:T(4,128)S(1)} %get-tuple-element.18.refs_1_, f32[4,1024]{1,0:T(4,128)S(1)} %get-tuple-element.19.refs_2_, f32[4,1024]{1,0:T(4,128)S(1)} %get-tuple-element.20.refs_3_, ...), custom_call_target="tpu_custom_call" | custom-call | tf_op jit(solution)/shard_map/margins_and_theirs/pallas_call | solution.py:169
  56.6 0.6 collective-permute-start.7
  57.2 4.7 %gradient_mine.1 = f32[256,512]{1,0:T(8,128)S(1)} custom-call(f32[4,1024]{1,0:T(4,128)S(1)} %get-tuple-element.23.refs_0_, bf16[4096,512]{1,0:T(8,128)(2,1)} %refs_1_.1, s32[1,4096]{1,0:T(1,128)S(1)} %bitcast.42), custom_call_target="tpu_custom_call" | custom-call | flops 2147483648 | bytes 4718592 | tf_op jit(solution)/shard_map/gradient_mine/pallas_call | solution.py:200
  61.9 3.1 %collective-permute-done.7 = f16[256,512]{1,0:T(8,128)(2,1)S(1)} collective-permute-done((f16[256,512]{1,0:T(8,128)(2,1)S(1)}, f16[256,512]{1,0:T(8,128)(2,1)S(1)}, u32[]{:S(2)}, u32[]{:S(2)}) %collective-permute-start.7) | collective-permute-done | bytes 262176 | tf_op jit(solution)/shard_map/ppermute | solution.py:413
  66.0 3.7 %collective-permute-start.9 = (f16[64,512]{1,0:T(8,128)(2,1)S(1)}, f16[64,512]{1,0:T(8,128)(2,1)S(1)}, u32[]{:S(2)}, u32[]{:S(2)}) collective-permute-start(f16[64,512]{1,0:T(8,128)(2,1)S(1)} %get-tuple-element.29), channel_id=1, source_target_pairs={{0,16},{4,20},{8,24},{12,28},{16,0},{20,4},{24,8},{28,12},{1,17},{... | collective-permute-start | bytes 196616 | tf_op jit(solution)/shard_map/ppermute | solution.py:413
  69.6 2.2 %collective-permute-done.10 = f16[64,512]{1,0:T(8,128)(2,1)S(1)} collective-permute-done((f16[64,512]{1,0:T(8,128)(2,1)S(1)}, f16[64,512]{1,0:T(8,128)(2,1)S(1)}, u32[]{:S(2)}, u32[]{:S(2)}) %collective-permute-start.10) | collective-permute-done | bytes 65568 | tf_op jit(solution)/shard_map/ppermute | solution.py:413
  71.8 1.5 %collective-permute-done.9 = f16[64,512]{1,0:T(8,128)(2,1)S(1)} collective-permute-done((f16[64,512]{1,0:T(8,128)(2,1)S(1)}, f16[64,512]{1,0:T(8,128)(2,1)S(1)}, u32[]{:S(2)}, u32[]{:S(2)}) %collective-permute-start.9) | collective-permute-done | bytes 65568 | tf_op jit(solution)/shard_map/ppermute | solution.py:413
  73.3 1.1 %collective-permute-start.11 = (f16[64,512]{1,0:T(8,128)(2,1)S(1)}, f16[64,512]{1,0:T(8,128)(2,1)S(1)}, u32[]{:S(2)}, u32[]{:S(2)}) collective-permute-start(f16[64,512]{1,0:T(8,128)(2,1)S(1)} %fusion.2), channel_id=1, source_target_pairs={{0,4},{4,0},{8,12},{12,8},{16,20},{20,16},{24,28},{28,24},{1,5},{5... | collective-permute-start | bytes 196616 | tf_op jit(solution)/shard_map/ppermute | solution.py:413
  74.4 3.2 %collective-permute-done.11 = f16[64,512]{1,0:T(8,128)(2,1)S(1)} collective-permute-done((f16[64,512]{1,0:T(8,128)(2,1)S(1)}, f16[64,512]{1,0:T(8,128)(2,1)S(1)}, u32[]{:S(2)}, u32[]{:S(2)}) %collective-permute-start.11) | collective-permute-done | bytes 65568 | tf_op jit(solution)/shard_map/ppermute | solution.py:413
  77.8 0.6 collective-permute-start.12
  78.5 1.1 %collective-permute-start.13 = (f16[128,512]{1,0:T(8,128)(2,1)S(1)}, f16[128,512]{1,0:T(8,128)(2,1)S(1)}, u32[]{:S(2)}, u32[]{:S(2)}) collective-permute-start(f16[128,512]{1,0:T(8,128)(2,1)S(1)} %get-tuple-element.26), channel_id=1, source_target_pairs={{0,16},{4,20},{8,24},{12,28},{16,0},{20,4},{24,8},{28,12},{1,17},{... | collective-permute-start | bytes 393224 | tf_op jit(solution)/shard_map/ppermute | solution.py:413
  79.5 2.8 %collective-permute-start.14 = (f16[128,512]{1,0:T(8,128)(2,1)S(1)}, f16[128,512]{1,0:T(8,128)(2,1)S(1)}, u32[]{:S(2)}, u32[]{:S(2)}) collective-permute-start(f16[128,512]{1,0:T(8,128)(2,1)S(1)} %get-tuple-element.26), channel_id=1, source_target_pairs={{0,24},{4,28},{8,16},{12,20},{16,8},{20,12},{24,0},{28,4},{1,25},{... | collective-permute-start | bytes 393224 | tf_op jit(solution)/shard_map/ppermute | solution.py:413
  82.3 2.9 %collective-permute-done.12 = f16[128,512]{1,0:T(8,128)(2,1)S(1)} collective-permute-done((f16[128,512]{1,0:T(8,128)(2,1)S(1)}, f16[128,512]{1,0:T(8,128)(2,1)S(1)}, u32[]{:S(2)}, u32[]{:S(2)}) %collective-permute-start.12) | collective-permute-done | bytes 131104 | tf_op jit(solution)/shard_map/ppermute | solution.py:413
  85.2 3.7 %collective-permute-done.13 = f16[128,512]{1,0:T(8,128)(2,1)S(1)} collective-permute-done((f16[128,512]{1,0:T(8,128)(2,1)S(1)}, f16[128,512]{1,0:T(8,128)(2,1)S(1)}, u32[]{:S(2)}, u32[]{:S(2)}) %collective-permute-start.13) | collective-permute-done | bytes 131104 | tf_op jit(solution)/shard_map/ppermute | solution.py:413
  89.0 1.0 %copy-done.8 = f32[512,512]{1,0:T(8,128)} copy-done((f32[512,512]{1,0:T(8,128)}, f32[512,512]{1,0:T(8,128)S(1)}, u32[]{:S(2)}) %copy-start.8) | copy-done | bytes 1048600
  (46 shorter events, 2.1 us)
Async XLA Ops:
  0.6 11.4 %copy-start = (f32[512,512]{1,0:T(8,128)S(1)}, f32[512,512]{1,0:T(8,128)}, u32[]{:S(2)}) copy-start(f32[512,512]{1,0:T(8,128)} %coef_ref.2) | copy-start | bytes 3145732
  0.6 1.1 %copy-start.1 = (bf16[1024,256]{1,0:T(8,128)(2,1)S(1)}, bf16[1024,256]{1,0:T(8,128)(2,1)}, u32[]{:S(2)}) copy-start(bf16[1024,256]{1,0:T(8,128)(2,1)} %feats_ref.1) | copy-start | bytes 1572868
  1.8 0.7 copy-start.3
  2.5 9.6 %copy-start.2 = (s32[4096,1]{0,1:T(1,128)S(1)}, s32[4096,1]{0,1:T(1,128)}, u32[]{:S(2)}) copy-start(s32[4096,1]{0,1:T(1,128)} %param.12) | copy-start | bytes 49156
  2.5 9.6 %copy-start.4 = (s32[1024]{0:T(1024)S(1)}, s32[1024]{0:T(1024)}, u32[]{:S(2)}) copy-start(s32[1024]{0:T(1024)} %param.15) | copy-start | bytes 12292
  2.5 9.6 %copy-start.6 = (s32[1024]{0:T(1024)S(1)}, s32[1024]{0:T(1024)}, u32[]{:S(2)}) copy-start(s32[1024]{0:T(1024)} %param.10) | copy-start | bytes 12292
  4.7 34.2 %all-to-all-start = ((bf16[8,256,256]{2,1,0:T(8,128)(2,1)}), bf16[8,256,256]{2,1,0:T(8,128)(2,1)S(1)}, u32[]{:S(2)}, u32[]{:S(2)}) async-start(bf16[8,256,256]{2,1,0:T(8,128)(2,1)} %bitcast.1), calls=%async_computation | async-start | bytes 2097152 | tf_op jit(solution)/shard_map/all_to_all | solution.py:509
  12.1 17.1 %copy-start.9 = (s32[2432]{0:T(1024)S(1)}, s32[2432]{0:T(1024)}, u32[]{:S(2)}) copy-start(s32[2432]{0:T(1024)} %param.16) | copy-start | bytes 29188
  12.1 17.1 %copy-start.7 = (s32[4]{0:T(128)S(1)}, s32[4]{0:T(128)}, u32[]{:S(2)}) copy-start(s32[4]{0:T(128)} %tiles_ref.1) | copy-start | bytes 52
  12.1 26.9 %copy-start.5 = (f32[4,256]{1,0:T(4,128)S(1)}, f32[4,256]{1,0:T(4,128)}, u32[]{:S(2)}) copy-start(f32[4,256]{1,0:T(4,128)} %coef_ref.3) | copy-start | bytes 12292
  17.7 1.9 %collective-permute-start = (f32[6,1024]{1,0:T(8,128)S(1)}, f32[6,1024]{1,0:T(8,128)S(1)}, u32[]{:S(2)}, u32[]{:S(2)}) collective-permute-start(f32[6,1024]{1,0:T(8,128)S(1)} %partial_scores.1.refs_0_), channel_id=1, source_target_pairs={{0,1},{1,0},{2,3},{3,2},{4,5},{5,4},{6,7},{7,6},{8,9},{9,8},{10,11... | collective-permute-start | bytes 73736 | tf_op jit(solution)/shard_map/ppermute | solution.py:413
  17.8 4.0 %collective-permute-start.1 = (f32[6,1024]{1,0:T(8,128)S(1)}, f32[6,1024]{1,0:T(8,128)S(1)}, u32[]{:S(2)}, u32[]{:S(2)}) collective-permute-start(f32[6,1024]{1,0:T(8,128)S(1)} %partial_scores.1.refs_0_), channel_id=1, source_target_pairs={{0,2},{1,3},{2,0},{3,1},{4,6},{5,7},{6,4},{7,5},{8,10},{9,11},{10,... | collective-permute-start | bytes 73736 | tf_op jit(solution)/shard_map/ppermute | solution.py:413
  19.4 3.4 %collective-permute-start.2 = (f32[6,1024]{1,0:T(8,128)S(1)}, f32[6,1024]{1,0:T(8,128)S(1)}, u32[]{:S(2)}, u32[]{:S(2)}) collective-permute-start(f32[6,1024]{1,0:T(8,128)S(1)} %partial_scores.1.refs_0_), channel_id=1, source_target_pairs={{0,3},{1,2},{2,1},{3,0},{4,7},{5,6},{6,5},{7,4},{8,11},{9,10},{10,... | collective-permute-start | bytes 73736 | tf_op jit(solution)/shard_map/ppermute | solution.py:413
  23.1 3.7 %collective-permute-start.3 = (f32[4,2,256]{2,1,0:T(2,128)S(1)}, f32[4,2,256]{2,1,0:T(2,128)S(1)}, u32[]{:S(2)}, u32[]{:S(2)}) collective-permute-start(f32[4,2,256]{2,1,0:T(2,128)S(1)} %get-tuple-element.35), channel_id=1, source_target_pairs={{0,4},{4,0},{8,12},{12,8},{16,20},{20,16},{24,28},{28,24},{1,5},{5... | collective-permute-start | bytes 24584 | tf_op jit(solution)/shard_map/ppermute | solution.py:413
  26.8 6.8 %collective-permute-start.4 = (f32[2,2,256]{2,1,0:T(2,128)S(1)}, f32[2,2,256]{2,1,0:T(2,128)S(1)}, u32[]{:S(2)}, u32[]{:S(2)}) collective-permute-start(f32[2,2,256]{2,1,0:T(2,128)S(1)} %get-tuple-element.32), channel_id=1, source_target_pairs={{0,8},{4,12},{8,0},{12,4},{16,24},{20,28},{24,16},{28,20},{1,9},{5... | collective-permute-start | bytes 12296 | tf_op jit(solution)/shard_map/ppermute | solution.py:413
  30.1 7.9 %collective-permute-start.5 = (f32[2,2,256]{2,1,0:T(2,128)S(1)}, f32[2,2,256]{2,1,0:T(2,128)S(1)}, u32[]{:S(2)}, u32[]{:S(2)}) collective-permute-start(f32[2,2,256]{2,1,0:T(2,128)S(1)} %get-tuple-element.31), channel_id=1, source_target_pairs={{0,16},{4,20},{8,24},{12,28},{16,0},{20,4},{24,8},{28,12},{1,17},{... | collective-permute-start | bytes 12296 | tf_op jit(solution)/shard_map/ppermute | solution.py:413
  33.6 5.4 %collective-permute-start.6 = (f32[2,2,256]{2,1,0:T(2,128)S(1)}, f32[2,2,256]{2,1,0:T(2,128)S(1)}, u32[]{:S(2)}, u32[]{:S(2)}) collective-permute-start(f32[2,2,256]{2,1,0:T(2,128)S(1)} %get-tuple-element.30), channel_id=1, source_target_pairs={{0,24},{4,28},{8,16},{12,20},{16,8},{20,12},{24,0},{28,4},{1,25},{... | collective-permute-start | bytes 12296 | tf_op jit(solution)/shard_map/ppermute | solution.py:413
  56.6 8.4 %collective-permute-start.7 = (f16[256,512]{1,0:T(8,128)(2,1)S(1)}, f16[256,512]{1,0:T(8,128)(2,1)S(1)}, u32[]{:S(2)}, u32[]{:S(2)}) collective-permute-start(f16[256,512]{1,0:T(8,128)(2,1)S(1)} %convert_element_type.33), channel_id=1, source_target_pairs={{0,4},{4,0},{8,12},{12,8},{16,20},{20,16},{24,28},{28,24},{1,5},{5... | collective-permute-start | bytes 786440 | tf_op jit(solution)/shard_map/ppermute | solution.py:413
  65.2 6.6 %collective-permute-start.10 = (f16[64,512]{1,0:T(8,128)(2,1)S(1)}, f16[64,512]{1,0:T(8,128)(2,1)S(1)}, u32[]{:S(2)}, u32[]{:S(2)}) collective-permute-start(f16[64,512]{1,0:T(8,128)(2,1)S(1)} %get-tuple-element.28), channel_id=1, source_target_pairs={{0,24},{4,28},{8,16},{12,20},{16,8},{20,12},{24,0},{28,4},{1,25},{... | collective-permute-start | bytes 196616 | tf_op jit(solution)/shard_map/ppermute | solution.py:413
  65.8 6.1 %collective-permute-start.8 = (f16[64,512]{1,0:T(8,128)(2,1)S(1)}, f16[64,512]{1,0:T(8,128)(2,1)S(1)}, u32[]{:S(2)}, u32[]{:S(2)}) collective-permute-start(f16[64,512]{1,0:T(8,128)(2,1)S(1)} %get-tuple-element.27), channel_id=1, source_target_pairs={{0,8},{4,12},{8,0},{12,4},{16,24},{20,28},{24,16},{28,20},{1,9},{5... | collective-permute-start | bytes 196616 | tf_op jit(solution)/shard_map/ppermute | solution.py:413
  66.0 7.3 %collective-permute-start.9 = (f16[64,512]{1,0:T(8,128)(2,1)S(1)}, f16[64,512]{1,0:T(8,128)(2,1)S(1)}, u32[]{:S(2)}, u32[]{:S(2)}) collective-permute-start(f16[64,512]{1,0:T(8,128)(2,1)S(1)} %get-tuple-element.29), channel_id=1, source_target_pairs={{0,16},{4,20},{8,24},{12,28},{16,0},{20,4},{24,8},{28,12},{1,17},{... | collective-permute-start | bytes 196616 | tf_op jit(solution)/shard_map/ppermute | solution.py:413
  73.3 4.3 %collective-permute-start.11 = (f16[64,512]{1,0:T(8,128)(2,1)S(1)}, f16[64,512]{1,0:T(8,128)(2,1)S(1)}, u32[]{:S(2)}, u32[]{:S(2)}) collective-permute-start(f16[64,512]{1,0:T(8,128)(2,1)S(1)} %fusion.2), channel_id=1, source_target_pairs={{0,4},{4,0},{8,12},{12,8},{16,20},{20,16},{24,28},{28,24},{1,5},{5... | collective-permute-start | bytes 196616 | tf_op jit(solution)/shard_map/ppermute | solution.py:413
  77.8 7.3 %collective-permute-start.12 = (f16[128,512]{1,0:T(8,128)(2,1)S(1)}, f16[128,512]{1,0:T(8,128)(2,1)S(1)}, u32[]{:S(2)}, u32[]{:S(2)}) collective-permute-start(f16[128,512]{1,0:T(8,128)(2,1)S(1)} %get-tuple-element.26), channel_id=1, source_target_pairs={{0,8},{4,12},{8,0},{12,4},{16,24},{20,28},{24,16},{28,20},{1,9},{5... | collective-permute-start | bytes 393224 | tf_op jit(solution)/shard_map/ppermute | solution.py:413
  78.5 10.5 %collective-permute-start.13 = (f16[128,512]{1,0:T(8,128)(2,1)S(1)}, f16[128,512]{1,0:T(8,128)(2,1)S(1)}, u32[]{:S(2)}, u32[]{:S(2)}) collective-permute-start(f16[128,512]{1,0:T(8,128)(2,1)S(1)} %get-tuple-element.26), channel_id=1, source_target_pairs={{0,16},{4,20},{8,24},{12,28},{16,0},{20,4},{24,8},{28,12},{1,17},{... | collective-permute-start | bytes 393224 | tf_op jit(solution)/shard_map/ppermute | solution.py:413
  79.5 9.4 %collective-permute-start.14 = (f16[128,512]{1,0:T(8,128)(2,1)S(1)}, f16[128,512]{1,0:T(8,128)(2,1)S(1)}, u32[]{:S(2)}, u32[]{:S(2)}) collective-permute-start(f16[128,512]{1,0:T(8,128)(2,1)S(1)} %get-tuple-element.26), channel_id=1, source_target_pairs={{0,24},{4,28},{8,16},{12,20},{16,8},{20,12},{24,0},{28,4},{1,25},{... | collective-permute-start | bytes 393224 | tf_op jit(solution)/shard_map/ppermute | solution.py:413
  89.0 1.0 %copy-start.8 = (f32[512,512]{1,0:T(8,128)}, f32[512,512]{1,0:T(8,128)S(1)}, u32[]{:S(2)}) copy-start(f32[512,512]{1,0:T(8,128)S(1)} %subtract_dynamic-update-slice_fusion) | copy-start | bytes 3145732

commit v4 on v3

--- a/solution.py
+++ b/solution.py
@@ -105,15 +105,16 @@
 
 
 def add_blocks(
-    flip, dp_count, values_ref, block_ref, residual_rows, out_ref, first=True
+    flip, dp_count, values_ref, block_ref, residual_rows, out_ref
 ):
     kept = out_ref.shape[0]
     chunk = 2 * kept // dp_count
     rows = residual_rows[0].shape[1]
     parity = (lax.axis_index("dp") + flip) % 2
+    place = lax.axis_index("dp") // 2
     for i, residual in enumerate(residual_rows):
         block = block_ref[:, i * rows : (i + 1) * rows]
-        local = (block // (2 * chunk)) * chunk + block % chunk
+        local = ((block // (2 * chunk)) ^ place) * chunk + block % chunk
         local = jnp.where((block // chunk) % 2 == parity, local, -1)
         mask = hot(local, kept)
         high, low = split(residual, 2)
@@ -121,17 +122,15 @@
         left_low = jnp.where(mask, low.astype(f32), 0.0).astype(bf16)
         values = values_ref[i * rows : (i + 1) * rows, :]
         total = dot_nn(left_high, values) + dot_nn(left_low, values)
-        if first is True and i == 0:
+        if i == 0:
             out_ref[...] = total
-        elif first is True:
+        else:
             out_ref[...] += total
-        else:
-            out_ref[...] = jnp.where(first, 0.0, out_ref[...]) + total
 
 
 def margin_kernel(
     dp_count, returned_ref, fixed_ref, label_ref, slot_ref, values_ref, block_ref,
-    margin_ref, residual_ref, out_ref, all_ref, held_ref, copy_sem,
+    margin_ref, residual_ref, out_ref, held_ref, all_ref, copy_sem,
 ):
     copy = pltpu.make_async_copy(values_ref, held_ref, copy_sem)
     copy.start()
@@ -169,43 +168,32 @@
     return pl.pallas_call(
         kernel,
         in_specs=[vmem] * 4 + [pl.BlockSpec(memory_space=pltpu.HBM), vmem],
-        out_specs=[vmem] * 3,
+        out_specs=[vmem] * 4,
         out_shape=(
             jax.ShapeDtypeStruct((1, rows), f32),
             jax.ShapeDtypeStruct((shards, rows), f32),
             jax.ShapeDtypeStruct((blocks // 2, width), f32),
+            jax.ShapeDtypeStruct(fixed_values.shape, fixed_values.dtype),
         ),
-        scratch_shapes=[
-            pltpu.VMEM((shards, rows), f32),
-            pltpu.VMEM(fixed_values.shape, fixed_values.dtype),
-            pltpu.SemaphoreType.DMA,
-        ],
+        scratch_shapes=[pltpu.VMEM((shards, rows), f32), pltpu.SemaphoreType.DMA],
         compiler_params=compiler_params(50),
         name="margins_and_theirs",
     )(returned, fixed, label, slot, fixed_values, block_row)
 
 
 def mine_kernel(dp_count, residual_ref, values_ref, block_ref, out_ref):
-    residual = residual_ref[pl.ds(pl.program_id(0), 1), :]
-    add_blocks(0, dp_count, values_ref, block_ref, [residual], out_ref, pl.program_id(0) == 0)
+    residual_rows = [residual_ref[i : i + 1, :] for i in range(residual_ref.shape[0])]
+    add_blocks(0, dp_count, values_ref, block_ref, residual_rows, out_ref)
 
 
 def gradient_mine(residual, fixed_values, block_row, blocks, dp_count):
     rows, width = fixed_values.shape
-    shards, rows_here = residual.shape
 
     def kernel(*refs):
         mine_kernel(dp_count, *refs)
 
     return pl.pallas_call(
         kernel,
-        grid=(shards,),
-        in_specs=[
-            pl.BlockSpec((shards, rows_here), lambda i: (0, 0)),
-            pl.BlockSpec((rows_here, width), lambda i: (i, 0)),
-            pl.BlockSpec((1, rows_here), lambda i: (0, i)),
-        ],
-        out_specs=pl.BlockSpec((blocks // 2, width), lambda i: (0, 0)),
         out_shape=jax.ShapeDtypeStruct((blocks // 2, width), f32),
         cost_estimate=pl.CostEstimate(
             flops=2 * rows * blocks * width,
@@ -217,17 +205,25 @@
     )(residual, fixed_values, block_row)
 
 
-def pack_kernel(values_ref, feats_ref, slot_ref, out_ref, start_ref, copy_sem):
-    first = values_ref.at[pl.ds(0, start_ref.shape[0])]
-    copy = pltpu.make_async_copy(first, start_ref, copy_sem)
-    copy.start()
+def pack_kernel(
+    values_ref, feats_in_ref, slot_in_ref, out_ref, start_ref, feats_ref, slot_ref, sem
+):
+    copies = [
+        pltpu.make_async_copy(slot_in_ref, slot_ref, sem.at[0]),
+        pltpu.make_async_copy(feats_in_ref, feats_ref, sem.at[1]),
+        pltpu.make_async_copy(values_ref.at[pl.ds(0, start_ref.shape[0])], start_ref, sem.at[2]),
+    ]
+    for copy in copies:
+        copy.start()
+    copies[0].wait()
+    copies[1].wait()
     total = out_ref.shape[0]
     step = min(1024, total)
     for start in range(0, total, step):
         mask = (rows_iota((step, slot_ref.shape[1])) + start) == slot_ref[...]
         one_hot = jnp.where(mask, 1.0, 0.0).astype(bf16)
         out_ref[start : start + step, :] = dot_nn(one_hot, feats_ref[...]).astype(bf16)
-    copy.wait()
+    copies[2].wait()
 
 
 def pack_feats(fixed_values, member_feats, slot_row, slot_total):
@@ -235,13 +231,17 @@
     vmem = pl.BlockSpec(memory_space=pltpu.VMEM)
     return pl.pallas_call(
         pack_kernel,
-        in_specs=[pl.BlockSpec(memory_space=pltpu.HBM), vmem, vmem],
+        in_specs=[pl.BlockSpec(memory_space=pltpu.HBM)] * 3,
         out_specs=[vmem, vmem],
         out_shape=(
             jax.ShapeDtypeStruct((slot_total, width), bf16),
             jax.ShapeDtypeStruct((rows, fixed_values.shape[1]), bf16),
         ),
-        scratch_shapes=[pltpu.SemaphoreType.DMA],
+        scratch_shapes=[
+            pltpu.VMEM((rows, width), bf16),
+            pltpu.VMEM((1, rows), jnp.int32),
+            pltpu.SemaphoreType.DMA((3,)),
+        ],
         cost_estimate=pl.CostEstimate(
             flops=2 * rows * slot_total * width,
             bytes_accessed=2 * rows * width + 2 * slot_total * width,
@@ -436,46 +436,54 @@
     return out.reshape(message.shape)
 
 
-def reduce_rest(kept, place, stride):
-    count = kept.shape[0]
-    if count <= 4:
-        sends = kept.astype(f16)
-        total = pick_index(kept, place)
-        for k in range(1, count):
-            got = swap(pick_index(sends, place ^ k), "dp", stride * k)
-            total = total + got.astype(f32)
-        return total
-    low = count // 2
-    top = place // low
-    view = kept.reshape((2, low) + kept.shape[1:])
-    got = swap(pick_index(view, 1 - top).astype(f16), "dp", stride * low)
-    return reduce_rest(pick_index(view, top) + got.astype(f32), place % low, stride)
-
-
-def spread_rest(pair, place, count, stride, coef):
-    rows = pair.shape[0]
+def reduce_chunks(theirs, mine, half):
+    chunk = mine.shape[0] // half
+    sends = theirs.astype(f16)
+    if half > 4:
+        kept = mine + swap(sends, "dp", 1).astype(f32)
+        low = half // 2
+        while low:
+            got = swap(kept[low * chunk :].astype(f16), "dp", 2 * low)
+            kept = kept[: low * chunk] + got.astype(f32)
+            low //= 2
+        return kept
+    kept = [None] * half
+    for k in reversed(range(half)):
+        at = slice(k * chunk, (k + 1) * chunk)
+        kept[k] = mine[at] + swap(sends[at], "dp", 1).astype(f32)
+    total = kept[0]
+    for k in reversed(range(1, half)):
+        total = total + swap(kept[k].astype(f16), "dp", 2 * k).astype(f32)
+    return total
+
+
+def spread_chunks(own, side, place, half, coef):
+    rows = own.shape[0]
     out = jnp.zeros(coef.shape, f32)
 
-    def put(out, got, at):
-        own_coef = lax.dynamic_slice_in_dim(coef, at, got.shape[0], 0)
+    def put(out, got, k, parity):
+        at = ((place ^ k) * 2 + parity) * rows
+        own_coef = lax.dynamic_slice_in_dim(coef, at, rows, 0)
         grad = ridge_fixed * own_coef - got.astype(f32)
         return lax.dynamic_update_slice_in_dim(out, grad, at, 0)
 
-    if count <= 4:
-        for k in range(count):
-            got = pair if k == 0 else swap(pair, "dp", stride * k)
-            out = put(out, got, (place ^ k) * rows)
+    if half > 4:
+        whole = own
+        low = 1
+        while low < half:
+            whole = jnp.concatenate([whole, swap(whole, "dp", 2 * low)])
+            low *= 2
+        other = swap(whole, "dp", 1)
+        for k in range(half):
+            at = slice(k * rows, (k + 1) * rows)
+            out = put(out, whole[at], k, side)
+            out = put(out, other[at], k, 1 - side)
         return out
-    bit = 1
-    while bit < count:
-        other = swap(pair, "dp", stride * bit)
-        pair = jnp.where(
-            (place // bit) % 2 == 0,
-            jnp.concatenate([pair, other]),
-            jnp.concatenate([other, pair]),
-        )
-        bit *= 2
-    return put(out, pair, 0)
+    same = [own] + [swap(own, "dp", 2 * k) for k in range(1, half)]
+    for k in range(half):
+        out = put(out, same[k], k, side)
+        out = put(out, swap(same[k], "dp", 1), k, 1 - side)
+    return out
 
 
 def body(
@@ -492,14 +500,13 @@
     dp_count = lax.axis_size("dp")
     feat_count = lax.axis_size("feat")
     rows_here = member_feats.shape[0]
-    blocks, block_width = fixed_coef.shape
+    blocks = fixed_coef.shape[0]
     capacity = 2 * rows_here // dp_count
     slot_total = dp_count * capacity
     group_rows = fixed_values.shape[0]
     side = lax.axis_index("dp") % 2
     place = lax.axis_index("dp") // 2
     half = dp_count // 2
-    chunk = blocks // dp_count
 
     slot_row = row_slot.reshape(1, rows_here)
     label_row = labels.reshape(1, rows_here)
@@ -534,18 +541,12 @@
             got_feats, got, member_slots, member_coef, feat_count
         )
     returned = lax.all_to_all(new_scores, ("dp", "feat"), 0, 0, tiled=True)
-    margin, residual, theirs = margins_and_theirs(
+    margin, residual, theirs, values = margins_and_theirs(
         returned, fixed, label, slot, fixed_values, block_row, blocks, dp_count
     )
-    got_half = swap(theirs.astype(f16), "dp", 1)
-    mine = gradient_mine(residual, fixed_values, block_row, blocks, dp_count)
-    kept = mine + got_half.astype(f32)
-    summed = reduce_rest(kept.reshape(half, chunk, block_width), place, 2).astype(f16)
-    other = swap(summed, "dp", 1)
-    pair = jnp.where(
-        side == 0, jnp.concatenate([summed, other]), jnp.concatenate([other, summed])
-    )
-    fixed_grad = spread_rest(pair, place, half, 2, fixed_coef)
+    mine = gradient_mine(residual, values, block_row, blocks, dp_count)
+    summed = reduce_chunks(theirs, mine, half).astype(f16)
+    fixed_grad = spread_chunks(summed, side, place, half, fixed_coef)
     return (margin.reshape(rows_here), updated_coef, fixed_grad)
 
 

time: 90.4 us -> 88.5 us (0.979)
  waiting for transfers between devices: 26.6 us -> 19.2 us
  starting transfers between devices: 27.7 us -> 33.3 us
    ppermute x15 -> x21, waiting for transfers between devices: 26.6 us -> 19.2 us  [swap(): lax.ppermute(value, axis, [(i, i ^ offset) for i in range(lax.axis_size(a...]
    ppermute x15 -> x21, starting transfers between devices: 20.4 us -> 26.1 us  [swap(): lax.ppermute(value, axis, [(i, i ^ offset) for i in range(lax.axis_size(a...]
  transfers between devices with their start and end apart: 16 -> 22, of which waited for: 11 -> 11; matrix products, arithmetic and copies ran while one was open for 0% -> 0% of each run, Pallas kernels for 13% -> 13%
where the time goes in v4:
time: 88.5 us; the launch traced here: 88.2 us
  starting transfers between devices  33.3 us (38%)
  Pallas kernels  21.4 us (24%)
  waiting for transfers between devices  19.2 us (22%)
  blocking collectives  9.84 us (11%)
  local copies, waits for them, and re-layouts  3.04 us (3%)
  between operations  0.93 us (1%)
    ppermute x21, starting transfers between devices, swap(): lax.ppermute(value, axis, [(i, i ^ offset) for i in range(lax.axis_size(a...  26.1 us
    ppermute x21, waiting for transfers between devices, swap(): lax.ppermute(value, axis, [(i, i ^ offset) for i in range(lax.axis_size(a...  19.2 us
    all_to_all x1, blocking collectives, body(): returned = lax.all_to_all(new_scores, ('dp', 'feat'), 0, 0, tiled=True)  9.84 us
    all_to_all x1, starting transfers between devices, body(): lax.all_to_all(send_feats.reshape(dp_count, capacity, -1), 'dp', 0, 0, ti...  7.29 us
    pallas_call x1, Pallas kernels, partial_scores(): pl.pallas_call(partial_kernel, in_specs=[vmem, pl.BlockSpec(memory_space=...  5.6 us
    pallas_call x1, Pallas kernels, margins_and_theirs(): pl.pallas_call(kernel, in_specs=[vmem] * 4 + [pl.BlockSpec(memory_space=p...  4.69 us
    pallas_call x1, Pallas kernels, gradient_mine(): pl.pallas_call(kernel, out_shape=jax.ShapeDtypeStruct((blocks // 2, width...  4.5 us
    pallas_call x1, Pallas kernels, solve_members(): pl.pallas_call(solve_kernel, out_shape=(jax.ShapeDtypeStruct(member_coef....  3.11 us
  transfers between devices with their start and end apart: 22, of which 11 were waited for; matrix products, arithmetic and copies ran while one was open for 0% of the time, Pallas kernels for 13%

profile of v4, /device:TPU:0, one launch (start us, length us, event | category | flops | bytes accessed | tf_op | source)
XLA Modules:
  0.0 88.2 jit_solution(13065364230098958231)
XLA Ops:
  0.7 1.1 %copy-done.1 = bf16[1024,256]{1,0:T(8,128)(2,1)S(1)} copy-done((bf16[1024,256]{1,0:T(8,128)(2,1)S(1)}, bf16[1024,256]{1,0:T(8,128)(2,1)}, u32[]{:S(2)}) %copy-start.1) | copy-done | bytes 524312
  2.5 2.3 %pack_feats.1 = (bf16[2048,256]{1,0:T(8,128)(2,1)}, bf16[1024,512]{1,0:T(8,128)(2,1)S(1)}) custom-call(bf16[4096,512]{1,0:T(8,128)(2,1)} %refs_4_.1, bf16[1024,256]{1,0:T(8,128)(2,1)S(1)} %copy-done.1, s32[1,1024]{1,0:T(1,128)S(1)} %bitcast.29), custom_call_target="tpu_custom_call" | custom-call | flops 1073741824 | bytes 1572864 | tf_op jit(solution)/shard_map/pack_feats/pallas_call | solution.py:232
  4.8 7.3 %all-to-all-start = ((bf16[8,256,256]{2,1,0:T(8,128)(2,1)}), bf16[8,256,256]{2,1,0:T(8,128)(2,1)S(1)}, u32[]{:S(2)}, u32[]{:S(2)}) async-start(bf16[8,256,256]{2,1,0:T(8,128)(2,1)} %bitcast.1), calls=%async_computation | async-start | bytes 2097152 | tf_op jit(solution)/shard_map/all_to_all | solution.py:516
  12.1 5.6 %partial_scores.1.refs_0_ = f32[6,1024]{1,0:T(8,128)S(1)} custom-call(bf16[1024,512]{1,0:T(8,128)(2,1)S(1)} %get-tuple-element.16.start_ref, bf16[4096,512]{1,0:T(8,128)(2,1)} %refs_4_.1, s32[1,4096]{1,0:T(1,128)S(1)} %bitcast.25, f32[512,512]{1,0:T(8,128)S(1)} %copy-done, s32[1,1024]{1,0:T(1,128)S(1)} %bitcast.32, s32[1,1024]{1,0:T(1,128)S(1)} %bitcast.30), custom_call_target="tpu_custom_call" | custom-call | flops 4294967296 | bytes 5242880 | tf_op jit(solution)/shard_map/partial_scores/pallas_call | solution.py:88
  17.8 1.6 %collective-permute-start.1 = (f32[6,1024]{1,0:T(8,128)S(1)}, f32[6,1024]{1,0:T(8,128)S(1)}, u32[]{:S(2)}, u32[]{:S(2)}) collective-permute-start(f32[6,1024]{1,0:T(8,128)S(1)} %partial_scores.1.refs_0_), channel_id=1, source_target_pairs={{0,2},{1,3},{2,0},{3,1},{4,6},{5,7},{6,4},{7,5},{8,10},{9,11},{10,... | collective-permute-start | bytes 73736 | tf_op jit(solution)/shard_map/ppermute | solution.py:413
  19.7 2.1 %collective-permute-done.1.refs_2_ = f32[6,1024]{1,0:T(8,128)S(1)} collective-permute-done((f32[6,1024]{1,0:T(8,128)S(1)}, f32[6,1024]{1,0:T(8,128)S(1)}, u32[]{:S(2)}, u32[]{:S(2)}) %collective-permute-start.1) | collective-permute-done | bytes 24608 | tf_op jit(solution)/shard_map/ppermute | solution.py:413
  21.8 1.0 %collective-permute-done.2.refs_3_ = f32[6,1024]{1,0:T(8,128)S(1)} collective-permute-done((f32[6,1024]{1,0:T(8,128)S(1)}, f32[6,1024]{1,0:T(8,128)S(1)}, u32[]{:S(2)}, u32[]{:S(2)}) %collective-permute-start.2) | collective-permute-done | bytes 24608 | tf_op jit(solution)/shard_map/ppermute | solution.py:413
  23.1 2.1 %collective-permute-start.3 = (f32[4,2,256]{2,1,0:T(2,128)S(1)}, f32[4,2,256]{2,1,0:T(2,128)S(1)}, u32[]{:S(2)}, u32[]{:S(2)}) collective-permute-start(f32[4,2,256]{2,1,0:T(2,128)S(1)} %get-tuple-element.41), channel_id=1, source_target_pairs={{0,4},{4,0},{8,12},{12,8},{16,20},{20,16},{24,28},{28,24},{1,5},{5... | collective-permute-start | bytes 24584 | tf_op jit(solution)/shard_map/ppermute | solution.py:413
  25.2 1.6 %collective-permute-done.3 = f32[4,2,256]{2,1,0:T(2,128)S(1)} collective-permute-done((f32[4,2,256]{2,1,0:T(2,128)S(1)}, f32[4,2,256]{2,1,0:T(2,128)S(1)}, u32[]{:S(2)}, u32[]{:S(2)}) %collective-permute-start.3) | collective-permute-done | bytes 8224 | tf_op jit(solution)/shard_map/ppermute | solution.py:413
  26.8 2.3 %collective-permute-start.4 = (f32[2,2,256]{2,1,0:T(2,128)S(1)}, f32[2,2,256]{2,1,0:T(2,128)S(1)}, u32[]{:S(2)}, u32[]{:S(2)}) collective-permute-start(f32[2,2,256]{2,1,0:T(2,128)S(1)} %get-tuple-element.38), channel_id=1, source_target_pairs={{0,8},{4,12},{8,0},{12,4},{16,24},{20,28},{24,16},{28,20},{1,9},{5... | collective-permute-start | bytes 12296 | tf_op jit(solution)/shard_map/ppermute | solution.py:413
  29.2 1.0 %slot_members.1.member_ref = f32[8,256]{1,0:T(8,128)S(1)} custom-call(s32[4]{0:T(128)S(1)} %copy-done.7, s32[1,2432]{1,0:T(1,128)S(1)} %reshape.40.source_ref), custom_call_target="tpu_custom_call" | custom-call | tf_op jit(solution)/shard_map/slot_members/pallas_call | solution.py:312
  30.2 3.4 %collective-permute-start.5 = (f32[2,2,256]{2,1,0:T(2,128)S(1)}, f32[2,2,256]{2,1,0:T(2,128)S(1)}, u32[]{:S(2)}, u32[]{:S(2)}) collective-permute-start(f32[2,2,256]{2,1,0:T(2,128)S(1)} %get-tuple-element.37), channel_id=1, source_target_pairs={{0,16},{4,20},{8,24},{12,28},{16,0},{20,4},{24,8},{28,12},{1,17},{... | collective-permute-start | bytes 12296 | tf_op jit(solution)/shard_map/ppermute | solution.py:413
  33.6 4.5 %collective-permute-done.5 = f32[2,2,256]{2,1,0:T(2,128)S(1)} collective-permute-done((f32[2,2,256]{2,1,0:T(2,128)S(1)}, f32[2,2,256]{2,1,0:T(2,128)S(1)}, u32[]{:S(2)}, u32[]{:S(2)}) %collective-permute-start.5) | collective-permute-done | bytes 4128 | tf_op jit(solution)/shard_map/ppermute | solution.py:413
  38.1 0.9 %collective-permute-done.6 = f32[2,2,256]{2,1,0:T(2,128)S(1)} collective-permute-done((f32[2,2,256]{2,1,0:T(2,128)S(1)}, f32[2,2,256]{2,1,0:T(2,128)S(1)}, u32[]{:S(2)}, u32[]{:S(2)}) %collective-permute-start.6) | collective-permute-done | bytes 4128 | tf_op jit(solution)/shard_map/ppermute | solution.py:413
  39.0 3.1 %solve_members.1 = (f32[4,256]{1,0:T(4,128)}, f32[32,1,256]{2,1,0:T(1,128)S(1)}) custom-call(bf16[2048,256]{1,0:T(8,128)(2,1)S(1)} %bitcast.23, f32[8,2,256]{2,1,0:T(2,128)S(1)} %bitcast.24, f32[8,256]{1,0:T(8,128)S(1)} %slot_members.1.member_ref, f32[4,256]{1,0:T(4,128)S(1)} %copy-done.5), custom_call_target="tpu_custom_call" | custom-call | tf_op jit(solution)/shard_map/solve_members/pallas_call | solution.py:401
  42.1 9.8 %all_to_all.10.refs_0_ = f32[32,1,256]{2,1,0:T(1,128)S(1)} all-to-all(f32[32,1,256]{2,1,0:T(1,128)S(1)} %get-tuple-element.18), channel_id=1, replica_groups=mesh['dp'=8,'feat'=4] {'dp','feat'}, dimensions={0} | all-to-all | bytes 65536 | tf_op jit(solution)/shard_map/all_to_all | solution.py:543
  52.0 4.7 %margins_and_theirs.1 = (f32[1,1024]{1,0:T(1,128)}, f32[4,1024]{1,0:T(4,128)S(1)}, f32[256,512]{1,0:T(8,128)S(1)}, bf16[4096,512]{1,0:T(8,128)(2,1)}) custom-call(f32[32,1,256]{2,1,0:T(1,128)S(1)} %all_to_all.10.refs_0_, f32[4,1024]{1,0:T(4,128)S(1)} %get-tuple-element.19.refs_1_, f32[4,1024]{1,0:T(4,128)S(1)} %get-tuple-element.20.refs_2_, ...), custom_call_target="tpu_custom_call" | custom-call | tf_op jit(solution)/shard_map/margins_and_theirs/pallas_call | solution.py:168
  57.4 1.4 %collective-permute-start.12 = (f16[64,512]{1,0:T(8,128)(2,1)S(1)}, f16[64,512]{1,0:T(8,128)(2,1)S(1)}, u32[]{:S(2)}, u32[]{:S(2)}) collective-permute-start(f16[64,512]{1,0:T(8,128)(2,1)S(1)} %get-tuple-element.33), channel_id=1, source_target_pairs={{0,4},{4,0},{8,12},{12,8},{16,20},{20,16},{24,28},{28,24},{1,5},{5... | collective-permute-start | bytes 196616 | tf_op jit(solution)/shard_map/ppermute | solution.py:413
  59.4 1.4 %collective-permute-start.7 = (f16[64,512]{1,0:T(8,128)(2,1)S(1)}, f16[64,512]{1,0:T(8,128)(2,1)S(1)}, u32[]{:S(2)}, u32[]{:S(2)}) collective-permute-start(f16[64,512]{1,0:T(8,128)(2,1)S(1)} %get-tuple-element.32), channel_id=1, source_target_pairs={{0,4},{4,0},{8,12},{12,8},{16,20},{20,16},{24,28},{28,24},{1,5},{5... | collective-permute-start | bytes 196616 | tf_op jit(solution)/shard_map/ppermute | solution.py:413
  60.9 4.5 %gradient_mine.1 = f32[256,512]{1,0:T(8,128)S(1)} custom-call(f32[4,1024]{1,0:T(4,128)S(1)} %get-tuple-element.24.refs_0_, bf16[4096,512]{1,0:T(8,128)(2,1)} %get-tuple-element.25.refs_1_, s32[1,4096]{1,0:T(1,128)S(1)} %bitcast.27), custom_call_target="tpu_custom_call" | custom-call | flops 2147483648 | bytes 4718592 | tf_op jit(solution)/shard_map/gradient_mine/pallas_call | solution.py:195
  66.7 3.2 %collective-permute-start.9 = (f16[64,512]{1,0:T(8,128)(2,1)S(1)}, f16[64,512]{1,0:T(8,128)(2,1)S(1)}, u32[]{:S(2)}, u32[]{:S(2)}) collective-permute-start(f16[64,512]{1,0:T(8,128)(2,1)S(1)} %get-tuple-element.29), channel_id=1, source_target_pairs={{0,24},{4,28},{8,16},{12,20},{16,8},{20,12},{24,0},{28,4},{1,25},{... | collective-permute-start | bytes 196616 | tf_op jit(solution)/shard_map/ppermute | solution.py:413
  69.9 2.1 %collective-permute-done.11 = f16[64,512]{1,0:T(8,128)(2,1)S(1)} collective-permute-done((f16[64,512]{1,0:T(8,128)(2,1)S(1)}, f16[64,512]{1,0:T(8,128)(2,1)S(1)}, u32[]{:S(2)}, u32[]{:S(2)}) %collective-permute-start.11) | collective-permute-done | bytes 65568 | tf_op jit(solution)/shard_map/ppermute | solution.py:413
  72.0 1.0 %collective-permute-done.9 = f16[64,512]{1,0:T(8,128)(2,1)S(1)} collective-permute-done((f16[64,512]{1,0:T(8,128)(2,1)S(1)}, f16[64,512]{1,0:T(8,128)(2,1)S(1)}, u32[]{:S(2)}, u32[]{:S(2)}) %collective-permute-start.9) | collective-permute-done | bytes 65568 | tf_op jit(solution)/shard_map/ppermute | solution.py:413
  73.2 1.1 %collective-permute-start.15 = (f16[64,512]{1,0:T(8,128)(2,1)S(1)}, f16[64,512]{1,0:T(8,128)(2,1)S(1)}, u32[]{:S(2)}, u32[]{:S(2)}) collective-permute-start(f16[64,512]{1,0:T(8,128)(2,1)S(1)} %get-tuple-element.28), channel_id=1, source_target_pairs={{0,8},{4,12},{8,0},{12,4},{16,24},{20,28},{24,16},{28,20},{1,9},{5... | collective-permute-start | bytes 196616 | tf_op jit(solution)/shard_map/ppermute | solution.py:413
  74.2 2.6 %collective-permute-start.17 = (f16[64,512]{1,0:T(8,128)(2,1)S(1)}, f16[64,512]{1,0:T(8,128)(2,1)S(1)}, u32[]{:S(2)}, u32[]{:S(2)}) collective-permute-start(f16[64,512]{1,0:T(8,128)(2,1)S(1)} %get-tuple-element.28), channel_id=1, source_target_pairs={{0,16},{4,20},{8,24},{12,28},{16,0},{20,4},{24,8},{28,12},{1,17},{... | collective-permute-start | bytes 196616 | tf_op jit(solution)/shard_map/ppermute | solution.py:413
  76.8 0.8 collective-permute-start.19
  78.2 1.4 %collective-permute-start.16 = (f16[64,512]{1,0:T(8,128)(2,1)S(1)}, f16[64,512]{1,0:T(8,128)(2,1)S(1)}, u32[]{:S(2)}, u32[]{:S(2)}) collective-permute-start(f16[64,512]{1,0:T(8,128)(2,1)S(1)} %collective-permute-done.15), channel_id=1, source_target_pairs={{0,4},{4,0},{8,12},{12,8},{16,20},{20,16},{24,28},{28,24},{1,5},{5... | collective-permute-start | bytes 196616 | tf_op jit(solution)/shard_map/ppermute | solution.py:413
  79.7 0.9 collective-permute-done.17
  81.2 1.7 %collective-permute-done.19 = f16[64,512]{1,0:T(8,128)(2,1)S(1)} collective-permute-done((f16[64,512]{1,0:T(8,128)(2,1)S(1)}, f16[64,512]{1,0:T(8,128)(2,1)S(1)}, u32[]{:S(2)}, u32[]{:S(2)}) %collective-permute-start.19) | collective-permute-done | bytes 65568 | tf_op jit(solution)/shard_map/ppermute | solution.py:413
  83.6 1.2 %collective-permute-done.18 = f16[64,512]{1,0:T(8,128)(2,1)S(1)} collective-permute-done((f16[64,512]{1,0:T(8,128)(2,1)S(1)}, f16[64,512]{1,0:T(8,128)(2,1)S(1)}, u32[]{:S(2)}, u32[]{:S(2)}) %collective-permute-start.18) | collective-permute-done | bytes 65568 | tf_op jit(solution)/shard_map/ppermute | solution.py:413
  84.8 2.3 %collective-permute-done.20 = f16[64,512]{1,0:T(8,128)(2,1)S(1)} collective-permute-done((f16[64,512]{1,0:T(8,128)(2,1)S(1)}, f16[64,512]{1,0:T(8,128)(2,1)S(1)}, u32[]{:S(2)}, u32[]{:S(2)}) %collective-permute-start.20) | collective-permute-done | bytes 65568 | tf_op jit(solution)/shard_map/ppermute | solution.py:413
  87.2 1.0 %copy-done.8 = f32[512,512]{1,0:T(8,128)} copy-done((f32[512,512]{1,0:T(8,128)}, f32[512,512]{1,0:T(8,128)S(1)}, u32[]{:S(2)}) %copy-start.8) | copy-done | bytes 1048600
  (60 shorter events, 6.2 us)
Async XLA Ops:
  0.6 11.4 %copy-start = (f32[512,512]{1,0:T(8,128)S(1)}, f32[512,512]{1,0:T(8,128)}, u32[]{:S(2)}) copy-start(f32[512,512]{1,0:T(8,128)} %coef_ref.2) | copy-start | bytes 3145732
  0.6 1.1 %copy-start.1 = (bf16[1024,256]{1,0:T(8,128)(2,1)S(1)}, bf16[1024,256]{1,0:T(8,128)(2,1)}, u32[]{:S(2)}) copy-start(bf16[1024,256]{1,0:T(8,128)(2,1)} %feats_in_ref.1) | copy-start | bytes 1572868
  1.8 0.7 copy-start.3
  2.5 9.6 %copy-start.2 = (s32[4096,1]{0,1:T(1,128)S(1)}, s32[4096,1]{0,1:T(1,128)}, u32[]{:S(2)}) copy-start(s32[4096,1]{0,1:T(1,128)} %param.12) | copy-start | bytes 49156
  2.5 9.6 %copy-start.4 = (s32[1024]{0:T(1024)S(1)}, s32[1024]{0:T(1024)}, u32[]{:S(2)}) copy-start(s32[1024]{0:T(1024)} %param.15) | copy-start | bytes 12292
  2.5 9.6 %copy-start.6 = (s32[1024]{0:T(1024)S(1)}, s32[1024]{0:T(1024)}, u32[]{:S(2)}) copy-start(s32[1024]{0:T(1024)} %param.10) | copy-start | bytes 12292
  4.8 34.2 %all-to-all-start = ((bf16[8,256,256]{2,1,0:T(8,128)(2,1)}), bf16[8,256,256]{2,1,0:T(8,128)(2,1)S(1)}, u32[]{:S(2)}, u32[]{:S(2)}) async-start(bf16[8,256,256]{2,1,0:T(8,128)(2,1)} %bitcast.1), calls=%async_computation | async-start | bytes 2097152 | tf_op jit(solution)/shard_map/all_to_all | solution.py:516
  12.1 17.1 %copy-start.9 = (s32[2432]{0:T(1024)S(1)}, s32[2432]{0:T(1024)}, u32[]{:S(2)}) copy-start(s32[2432]{0:T(1024)} %param.16) | copy-start | bytes 29188
  12.1 17.1 %copy-start.7 = (s32[4]{0:T(128)S(1)}, s32[4]{0:T(128)}, u32[]{:S(2)}) copy-start(s32[4]{0:T(128)} %tiles_ref.1) | copy-start | bytes 52
  12.1 26.9 %copy-start.5 = (f32[4,256]{1,0:T(4,128)S(1)}, f32[4,256]{1,0:T(4,128)}, u32[]{:S(2)}) copy-start(f32[4,256]{1,0:T(4,128)} %coef_ref.3) | copy-start | bytes 12292
  17.7 1.9 %collective-permute-start = (f32[6,1024]{1,0:T(8,128)S(1)}, f32[6,1024]{1,0:T(8,128)S(1)}, u32[]{:S(2)}, u32[]{:S(2)}) collective-permute-start(f32[6,1024]{1,0:T(8,128)S(1)} %partial_scores.1.refs_0_), channel_id=1, source_target_pairs={{0,1},{1,0},{2,3},{3,2},{4,5},{5,4},{6,7},{7,6},{8,9},{9,8},{10,11... | collective-permute-start | bytes 73736 | tf_op jit(solution)/shard_map/ppermute | solution.py:413
  17.8 4.0 %collective-permute-start.1 = (f32[6,1024]{1,0:T(8,128)S(1)}, f32[6,1024]{1,0:T(8,128)S(1)}, u32[]{:S(2)}, u32[]{:S(2)}) collective-permute-start(f32[6,1024]{1,0:T(8,128)S(1)} %partial_scores.1.refs_0_), channel_id=1, source_target_pairs={{0,2},{1,3},{2,0},{3,1},{4,6},{5,7},{6,4},{7,5},{8,10},{9,11},{10,... | collective-permute-start | bytes 73736 | tf_op jit(solution)/shard_map/ppermute | solution.py:413
  19.4 3.4 %collective-permute-start.2 = (f32[6,1024]{1,0:T(8,128)S(1)}, f32[6,1024]{1,0:T(8,128)S(1)}, u32[]{:S(2)}, u32[]{:S(2)}) collective-permute-start(f32[6,1024]{1,0:T(8,128)S(1)} %partial_scores.1.refs_0_), channel_id=1, source_target_pairs={{0,3},{1,2},{2,1},{3,0},{4,7},{5,6},{6,5},{7,4},{8,11},{9,10},{10,... | collective-permute-start | bytes 73736 | tf_op jit(solution)/shard_map/ppermute | solution.py:413
  23.1 3.7 %collective-permute-start.3 = (f32[4,2,256]{2,1,0:T(2,128)S(1)}, f32[4,2,256]{2,1,0:T(2,128)S(1)}, u32[]{:S(2)}, u32[]{:S(2)}) collective-permute-start(f32[4,2,256]{2,1,0:T(2,128)S(1)} %get-tuple-element.41), channel_id=1, source_target_pairs={{0,4},{4,0},{8,12},{12,8},{16,20},{20,16},{24,28},{28,24},{1,5},{5... | collective-permute-start | bytes 24584 | tf_op jit(solution)/shard_map/ppermute | solution.py:413
  26.8 6.8 %collective-permute-start.4 = (f32[2,2,256]{2,1,0:T(2,128)S(1)}, f32[2,2,256]{2,1,0:T(2,128)S(1)}, u32[]{:S(2)}, u32[]{:S(2)}) collective-permute-start(f32[2,2,256]{2,1,0:T(2,128)S(1)} %get-tuple-element.38), channel_id=1, source_target_pairs={{0,8},{4,12},{8,0},{12,4},{16,24},{20,28},{24,16},{28,20},{1,9},{5... | collective-permute-start | bytes 12296 | tf_op jit(solution)/shard_map/ppermute | solution.py:413
  30.2 7.9 %collective-permute-start.5 = (f32[2,2,256]{2,1,0:T(2,128)S(1)}, f32[2,2,256]{2,1,0:T(2,128)S(1)}, u32[]{:S(2)}, u32[]{:S(2)}) collective-permute-start(f32[2,2,256]{2,1,0:T(2,128)S(1)} %get-tuple-element.37), channel_id=1, source_target_pairs={{0,16},{4,20},{8,24},{12,28},{16,0},{20,4},{24,8},{28,12},{1,17},{... | collective-permute-start | bytes 12296 | tf_op jit(solution)/shard_map/ppermute | solution.py:413
  33.6 5.4 %collective-permute-start.6 = (f32[2,2,256]{2,1,0:T(2,128)S(1)}, f32[2,2,256]{2,1,0:T(2,128)S(1)}, u32[]{:S(2)}, u32[]{:S(2)}) collective-permute-start(f32[2,2,256]{2,1,0:T(2,128)S(1)} %get-tuple-element.36), channel_id=1, source_target_pairs={{0,24},{4,28},{8,16},{12,20},{16,8},{20,12},{24,0},{28,4},{1,25},{... | collective-permute-start | bytes 12296 | tf_op jit(solution)/shard_map/ppermute | solution.py:413
  56.8 8.6 %collective-permute-start.10 = (f16[64,512]{1,0:T(8,128)(2,1)S(1)}, f16[64,512]{1,0:T(8,128)(2,1)S(1)}, u32[]{:S(2)}, u32[]{:S(2)}) collective-permute-start(f16[64,512]{1,0:T(8,128)(2,1)S(1)} %get-tuple-element.34), channel_id=1, source_target_pairs={{0,4},{4,0},{8,12},{12,8},{16,20},{20,16},{24,28},{28,24},{1,5},{5... | collective-permute-start | bytes 196616 | tf_op jit(solution)/shard_map/ppermute | solution.py:413
  57.4 8.0 %collective-permute-start.12 = (f16[64,512]{1,0:T(8,128)(2,1)S(1)}, f16[64,512]{1,0:T(8,128)(2,1)S(1)}, u32[]{:S(2)}, u32[]{:S(2)}) collective-permute-start(f16[64,512]{1,0:T(8,128)(2,1)S(1)} %get-tuple-element.33), channel_id=1, source_target_pairs={{0,4},{4,0},{8,12},{12,8},{16,20},{20,16},{24,28},{28,24},{1,5},{5... | collective-permute-start | bytes 196616 | tf_op jit(solution)/shard_map/ppermute | solution.py:413
  58.8 6.6 %collective-permute-start.8 = (f16[64,512]{1,0:T(8,128)(2,1)S(1)}, f16[64,512]{1,0:T(8,128)(2,1)S(1)}, u32[]{:S(2)}, u32[]{:S(2)}) collective-permute-start(f16[64,512]{1,0:T(8,128)(2,1)S(1)} %get-tuple-element.35), channel_id=1, source_target_pairs={{0,4},{4,0},{8,12},{12,8},{16,20},{20,16},{24,28},{28,24},{1,5},{5... | collective-permute-start | bytes 196616 | tf_op jit(solution)/shard_map/ppermute | solution.py:413
  59.4 10.5 %collective-permute-start.7 = (f16[64,512]{1,0:T(8,128)(2,1)S(1)}, f16[64,512]{1,0:T(8,128)(2,1)S(1)}, u32[]{:S(2)}, u32[]{:S(2)}) collective-permute-start(f16[64,512]{1,0:T(8,128)(2,1)S(1)} %get-tuple-element.32), channel_id=1, source_target_pairs={{0,4},{4,0},{8,12},{12,8},{16,20},{20,16},{24,28},{28,24},{1,5},{5... | collective-permute-start | bytes 196616 | tf_op jit(solution)/shard_map/ppermute | solution.py:413
  65.5 6.5 %collective-permute-start.11 = (f16[64,512]{1,0:T(8,128)(2,1)S(1)}, f16[64,512]{1,0:T(8,128)(2,1)S(1)}, u32[]{:S(2)}, u32[]{:S(2)}) collective-permute-start(f16[64,512]{1,0:T(8,128)(2,1)S(1)} %get-tuple-element.31), channel_id=1, source_target_pairs={{0,16},{4,20},{8,24},{12,28},{16,0},{20,4},{24,8},{28,12},{1,17},{... | collective-permute-start | bytes 196616 | tf_op jit(solution)/shard_map/ppermute | solution.py:413
  66.2 5.9 %collective-permute-start.13 = (f16[64,512]{1,0:T(8,128)(2,1)S(1)}, f16[64,512]{1,0:T(8,128)(2,1)S(1)}, u32[]{:S(2)}, u32[]{:S(2)}) collective-permute-start(f16[64,512]{1,0:T(8,128)(2,1)S(1)} %get-tuple-element.30), channel_id=1, source_target_pairs={{0,8},{4,12},{8,0},{12,4},{16,24},{20,28},{24,16},{28,20},{1,9},{5... | collective-permute-start | bytes 196616 | tf_op jit(solution)/shard_map/ppermute | solution.py:413
  66.7 6.3 %collective-permute-start.9 = (f16[64,512]{1,0:T(8,128)(2,1)S(1)}, f16[64,512]{1,0:T(8,128)(2,1)S(1)}, u32[]{:S(2)}, u32[]{:S(2)}) collective-permute-start(f16[64,512]{1,0:T(8,128)(2,1)S(1)} %get-tuple-element.29), channel_id=1, source_target_pairs={{0,24},{4,28},{8,16},{12,20},{16,8},{20,12},{24,0},{28,4},{1,25},{... | collective-permute-start | bytes 196616 | tf_op jit(solution)/shard_map/ppermute | solution.py:413
  73.2 5.0 %collective-permute-start.15 = (f16[64,512]{1,0:T(8,128)(2,1)S(1)}, f16[64,512]{1,0:T(8,128)(2,1)S(1)}, u32[]{:S(2)}, u32[]{:S(2)}) collective-permute-start(f16[64,512]{1,0:T(8,128)(2,1)S(1)} %get-tuple-element.28), channel_id=1, source_target_pairs={{0,8},{4,12},{8,0},{12,4},{16,24},{20,28},{24,16},{28,20},{1,9},{5... | collective-permute-start | bytes 196616 | tf_op jit(solution)/shard_map/ppermute | solution.py:413
  74.2 6.3 %collective-permute-start.17 = (f16[64,512]{1,0:T(8,128)(2,1)S(1)}, f16[64,512]{1,0:T(8,128)(2,1)S(1)}, u32[]{:S(2)}, u32[]{:S(2)}) collective-permute-start(f16[64,512]{1,0:T(8,128)(2,1)S(1)} %get-tuple-element.28), channel_id=1, source_target_pairs={{0,16},{4,20},{8,24},{12,28},{16,0},{20,4},{24,8},{28,12},{1,17},{... | collective-permute-start | bytes 196616 | tf_op jit(solution)/shard_map/ppermute | solution.py:413
  76.8 6.1 %collective-permute-start.19 = (f16[64,512]{1,0:T(8,128)(2,1)S(1)}, f16[64,512]{1,0:T(8,128)(2,1)S(1)}, u32[]{:S(2)}, u32[]{:S(2)}) collective-permute-start(f16[64,512]{1,0:T(8,128)(2,1)S(1)} %get-tuple-element.28), channel_id=1, source_target_pairs={{0,24},{4,28},{8,16},{12,20},{16,8},{20,12},{24,0},{28,4},{1,25},{... | collective-permute-start | bytes 196616 | tf_op jit(solution)/shard_map/ppermute | solution.py:413
  77.6 5.8 %collective-permute-start.14 = (f16[64,512]{1,0:T(8,128)(2,1)S(1)}, f16[64,512]{1,0:T(8,128)(2,1)S(1)}, u32[]{:S(2)}, u32[]{:S(2)}) collective-permute-start(f16[64,512]{1,0:T(8,128)(2,1)S(1)} %get-tuple-element.28), channel_id=1, source_target_pairs={{0,4},{4,0},{8,12},{12,8},{16,20},{20,16},{24,28},{28,24},{1,5},{5... | collective-permute-start | bytes 196616 | tf_op jit(solution)/shard_map/ppermute | solution.py:413
  78.2 5.3 %collective-permute-start.16 = (f16[64,512]{1,0:T(8,128)(2,1)S(1)}, f16[64,512]{1,0:T(8,128)(2,1)S(1)}, u32[]{:S(2)}, u32[]{:S(2)}) collective-permute-start(f16[64,512]{1,0:T(8,128)(2,1)S(1)} %collective-permute-done.15), channel_id=1, source_target_pairs={{0,4},{4,0},{8,12},{12,8},{16,20},{20,16},{24,28},{28,24},{1,5},{5... | collective-permute-start | bytes 196616 | tf_op jit(solution)/shard_map/ppermute | solution.py:413
  80.5 4.3 %collective-permute-start.18 = (f16[64,512]{1,0:T(8,128)(2,1)S(1)}, f16[64,512]{1,0:T(8,128)(2,1)S(1)}, u32[]{:S(2)}, u32[]{:S(2)}) collective-permute-start(f16[64,512]{1,0:T(8,128)(2,1)S(1)} %collective-permute-done.17), channel_id=1, source_target_pairs={{0,4},{4,0},{8,12},{12,8},{16,20},{20,16},{24,28},{28,24},{1,5},{5... | collective-permute-start | bytes 196616 | tf_op jit(solution)/shard_map/ppermute | solution.py:413
  82.9 4.3 %collective-permute-start.20 = (f16[64,512]{1,0:T(8,128)(2,1)S(1)}, f16[64,512]{1,0:T(8,128)(2,1)S(1)}, u32[]{:S(2)}, u32[]{:S(2)}) collective-permute-start(f16[64,512]{1,0:T(8,128)(2,1)S(1)} %collective-permute-done.19), channel_id=1, source_target_pairs={{0,4},{4,0},{8,12},{12,8},{16,20},{20,16},{24,28},{28,24},{1,5},{5... | collective-permute-start | bytes 196616 | tf_op jit(solution)/shard_map/ppermute | solution.py:413
  87.2 1.0 %copy-start.8 = (f32[512,512]{1,0:T(8,128)}, f32[512,512]{1,0:T(8,128)S(1)}, u32[]{:S(2)}) copy-start(f32[512,512]{1,0:T(8,128)S(1)} %subtract_dynamic-update-slice_fusion) | copy-start | bytes 3145732

commit v5 on v4

--- a/solution.py
+++ b/solution.py
@@ -49,16 +49,16 @@
 
 
 def partial_kernel(
-    start_ref, values_ref, block_ref, coef_ref, label_ref, slot_ref, out_ref, rest_ref, sem
+    values_ref, block_ref, coef_ref, label_ref, slot_ref, out_ref, held_ref, sem
 ):
     rows = out_ref.shape[1]
     blocks = coef_ref.shape[0]
     shards = values_ref.shape[0] // rows
     copies = [
         pltpu.make_async_copy(
-            values_ref.at[pl.ds((i + 1) * rows, rows)], rest_ref.at[i], sem.at[i]
+            values_ref.at[pl.ds(i * rows, rows)], held_ref.at[i], sem.at[i]
         )
-        for i in range(shards - 1)
+        for i in range(shards)
     ]
     for copy in copies:
         copy.start()
@@ -69,9 +69,8 @@
     for i in range(shards):
         block = block_ref[:, i * rows : (i + 1) * rows]
         column = jnp.broadcast_to(block, (TILE, rows)).T
-        if i > 0:
-            copies[i - 1].wait()
-        values = start_ref[...] if i == 0 else rest_ref[i - 1]
+        copies[i].wait()
+        values = held_ref[i]
         product = dot_nn(values, high) + dot_nn(values, low)
         total = jnp.zeros((rows, TILE), f32)
         for at in range(0, blocks, TILE):
@@ -79,7 +78,7 @@
         out_ref[i : i + 1, :] = jnp.sum(total.T, axis=0, keepdims=True)
 
 
-def partial_scores(start, fixed_values, block_row, fixed_coef, label_row, slot_row):
+def partial_scores(fixed_values, block_row, fixed_coef, label_row, slot_row):
     rows, width = fixed_values.shape
     rows_here = slot_row.shape[1]
     blocks = fixed_coef.shape[0]
@@ -87,12 +86,12 @@
     vmem = pl.BlockSpec(memory_space=pltpu.VMEM)
     return pl.pallas_call(
         partial_kernel,
-        in_specs=[vmem, pl.BlockSpec(memory_space=pltpu.HBM)] + [vmem] * 4,
+        in_specs=[pl.BlockSpec(memory_space=pltpu.HBM)] + [vmem] * 4,
         out_specs=vmem,
         out_shape=jax.ShapeDtypeStruct((shards + 2, rows_here), f32),
         scratch_shapes=[
-            pltpu.VMEM((shards - 1, rows_here, width), bf16),
-            pltpu.SemaphoreType.DMA((shards - 1,)),
+            pltpu.VMEM((shards, rows_here, width), bf16),
+            pltpu.SemaphoreType.DMA((shards,)),
         ],
         cost_estimate=pl.CostEstimate(
             flops=4 * rows * blocks * width,
@@ -101,11 +100,11 @@
         ),
         compiler_params=compiler_params(50),
         name="partial_scores",
-    )(start, fixed_values, block_row, fixed_coef, label_row, slot_row)
+    )(fixed_values, block_row, fixed_coef, label_row, slot_row)
 
 
 def add_blocks(
-    flip, dp_count, values_ref, block_ref, residual_rows, out_ref
+    flip, dp_count, shard_values, block_ref, residual_rows, out_ref
 ):
     kept = out_ref.shape[0]
     chunk = 2 * kept // dp_count
@@ -120,7 +119,7 @@
         high, low = split(residual, 2)
         left_high = jnp.where(mask, high.astype(f32), 0.0).astype(bf16)
         left_low = jnp.where(mask, low.astype(f32), 0.0).astype(bf16)
-        values = values_ref[i * rows : (i + 1) * rows, :]
+        values = shard_values(i)
         total = dot_nn(left_high, values) + dot_nn(left_low, values)
         if i == 0:
             out_ref[...] = total
@@ -130,12 +129,19 @@
 
 def margin_kernel(
     dp_count, returned_ref, fixed_ref, label_ref, slot_ref, values_ref, block_ref,
-    margin_ref, residual_ref, out_ref, held_ref, all_ref, copy_sem,
+    margin_ref, residual_ref, out_ref, keep_ref, all_ref, held_ref, sem,
 ):
-    copy = pltpu.make_async_copy(values_ref, held_ref, copy_sem)
-    copy.start()
+    kept = keep_ref.shape[0]
+    copies = [
+        pltpu.make_async_copy(values_ref.at[pl.ds(0, kept)], keep_ref, sem.at[0]),
+        pltpu.make_async_copy(
+            values_ref.at[pl.ds(kept, held_ref.shape[0])], held_ref, sem.at[1]
+        ),
+    ]
+    for copy in copies:
+        copy.start()
     sources, _, capacity = returned_ref.shape
-    shards, _ = fixed_ref.shape
+    shards, rows = fixed_ref.shape
     pieces = split(returned_ref[...].reshape(sources, capacity), 3)
     table = jnp.concatenate(pieces, axis=0)
     residual_rows = []
@@ -153,13 +159,21 @@
         residual_ref[i : i + 1, :] = residual
         residual_rows.append(residual)
     margin_ref[...] = all_ref[pl.ds(lax.axis_index("feat"), 1), :]
-    copy.wait()
-    add_blocks(1, dp_count, held_ref, block_ref, residual_rows, out_ref)
+    for copy in copies:
+        copy.wait()
+
+    def shard_values(i):
+        if i * rows < kept:
+            return keep_ref[i * rows : (i + 1) * rows, :]
+        return held_ref[i * rows - kept : (i + 1) * rows - kept, :]
+
+    add_blocks(1, dp_count, shard_values, block_ref, residual_rows, out_ref)
 
 
 def margins_and_theirs(returned, fixed, label, slot, fixed_values, block_row, blocks, dp_count):
     shards, rows = fixed.shape
-    width = fixed_values.shape[1]
+    group_rows, width = fixed_values.shape
+    kept = rows * (shards // 2)
 
     def kernel(*refs):
         margin_kernel(dp_count, *refs)
@@ -173,28 +187,61 @@
             jax.ShapeDtypeStruct((1, rows), f32),
             jax.ShapeDtypeStruct((shards, rows), f32),
             jax.ShapeDtypeStruct((blocks // 2, width), f32),
-            jax.ShapeDtypeStruct(fixed_values.shape, fixed_values.dtype),
+            jax.ShapeDtypeStruct((kept, width), bf16),
         ),
-        scratch_shapes=[pltpu.VMEM((shards, rows), f32), pltpu.SemaphoreType.DMA],
+        scratch_shapes=[
+            pltpu.VMEM((shards, rows), f32),
+            pltpu.VMEM((group_rows - kept, width), bf16),
+            pltpu.SemaphoreType.DMA((2,)),
+        ],
         compiler_params=compiler_params(50),
         name="margins_and_theirs",
     )(returned, fixed, label, slot, fixed_values, block_row)
 
 
-def mine_kernel(dp_count, residual_ref, values_ref, block_ref, out_ref):
-    residual_rows = [residual_ref[i : i + 1, :] for i in range(residual_ref.shape[0])]
-    add_blocks(0, dp_count, values_ref, block_ref, residual_rows, out_ref)
-
-
-def gradient_mine(residual, fixed_values, block_row, blocks, dp_count):
+def mine_kernel(
+    dp_count, residual_ref, keep_ref, values_ref, block_ref, out_ref, held_ref, sem
+):
+    shards, rows = residual_ref.shape
+    first = keep_ref.shape[0] // rows
+    copies = [
+        pltpu.make_async_copy(
+            values_ref.at[pl.ds(i * rows, rows)], held_ref.at[i - first], sem.at[i - first]
+        )
+        for i in range(first, shards)
+    ]
+    for copy in copies:
+        copy.start()
+
+    def shard_values(i):
+        if i < first:
+            return keep_ref[i * rows : (i + 1) * rows, :]
+        copies[i - first].wait()
+        return held_ref[i - first]
+
+    residual_rows = [residual_ref[i : i + 1, :] for i in range(shards)]
+    add_blocks(0, dp_count, shard_values, block_ref, residual_rows, out_ref)
+
+
+def gradient_mine(residual, keep, fixed_values, block_row, blocks, dp_count):
     rows, width = fixed_values.shape
+    shards, rows_here = residual.shape
+    copied = shards - keep.shape[0] // rows_here
+    vmem = pl.BlockSpec(memory_space=pltpu.VMEM)
+    hbm = pl.BlockSpec(memory_space=pltpu.HBM)
 
     def kernel(*refs):
         mine_kernel(dp_count, *refs)
 
     return pl.pallas_call(
         kernel,
+        in_specs=[vmem, vmem, hbm, vmem],
+        out_specs=vmem,
         out_shape=jax.ShapeDtypeStruct((blocks // 2, width), f32),
+        scratch_shapes=[
+            pltpu.VMEM((copied, rows_here, width), bf16),
+            pltpu.SemaphoreType.DMA((copied,)),
+        ],
         cost_estimate=pl.CostEstimate(
             flops=2 * rows * blocks * width,
             bytes_accessed=2 * rows * width + 2 * blocks * width,
@@ -202,54 +249,55 @@
         ),
         compiler_params=compiler_params(50),
         name="gradient_mine",
-    )(residual, fixed_values, block_row)
-
-
-def pack_kernel(
-    values_ref, feats_in_ref, slot_in_ref, out_ref, start_ref, feats_ref, slot_ref, sem
-):
-    copies = [
+    )(residual, keep, fixed_values, block_row)
+
+
+def pack_kernel(feats_in_ref, slot_in_ref, out_ref, feats_ref, slot_ref, held_ref, sem):
+    loads = [
         pltpu.make_async_copy(slot_in_ref, slot_ref, sem.at[0]),
         pltpu.make_async_copy(feats_in_ref, feats_ref, sem.at[1]),
-        pltpu.make_async_copy(values_ref.at[pl.ds(0, start_ref.shape[0])], start_ref, sem.at[2]),
     ]
-    for copy in copies:
-        copy.start()
-    copies[0].wait()
-    copies[1].wait()
-    total = out_ref.shape[0]
-    step = min(1024, total)
-    for start in range(0, total, step):
-        mask = (rows_iota((step, slot_ref.shape[1])) + start) == slot_ref[...]
+    for load in loads:
+        load.start()
+    for load in loads:
+        load.wait()
+    pieces, step, _ = held_ref.shape
+    stores = []
+    for i in range(pieces):
+        mask = (rows_iota((step, slot_ref.shape[1])) + i * step) == slot_ref[...]
         one_hot = jnp.where(mask, 1.0, 0.0).astype(bf16)
-        out_ref[start : start + step, :] = dot_nn(one_hot, feats_ref[...]).astype(bf16)
-    copies[2].wait()
-
-
-def pack_feats(fixed_values, member_feats, slot_row, slot_total):
+        held_ref[i] = dot_nn(one_hot, feats_ref[...]).astype(bf16)
+        stores.append(
+            pltpu.make_async_copy(held_ref.at[i], out_ref.at[pl.ds(i * step, step)], sem.at[2 + i])
+        )
+        stores[-1].start()
+    for store in stores:
+        store.wait()
+
+
+def pack_feats(member_feats, slot_row, slot_total):
     rows, width = member_feats.shape
-    vmem = pl.BlockSpec(memory_space=pltpu.VMEM)
+    step = min(512, slot_total)
+    pieces = slot_total // step
+    hbm = pl.BlockSpec(memory_space=pltpu.HBM)
     return pl.pallas_call(
         pack_kernel,
-        in_specs=[pl.BlockSpec(memory_space=pltpu.HBM)] * 3,
-        out_specs=[vmem, vmem],
-        out_shape=(
-            jax.ShapeDtypeStruct((slot_total, width), bf16),
-            jax.ShapeDtypeStruct((rows, fixed_values.shape[1]), bf16),
-        ),
+        in_specs=[hbm, hbm],
+        out_specs=hbm,
+        out_shape=jax.ShapeDtypeStruct((slot_total, width), bf16),
         scratch_shapes=[
             pltpu.VMEM((rows, width), bf16),
             pltpu.VMEM((1, rows), jnp.int32),
-            pltpu.SemaphoreType.DMA((3,)),
+            pltpu.VMEM((pieces, step, width), bf16),
+            pltpu.SemaphoreType.DMA((2 + pieces,)),
         ],
         cost_estimate=pl.CostEstimate(
             flops=2 * rows * slot_total * width,
             bytes_accessed=2 * rows * width + 2 * slot_total * width,
             transcendentals=0,
         ),
-        compiler_params=compiler_params(50),
         name="pack_feats",
-    )(fixed_values, member_feats, slot_row)
+    )(member_feats, slot_row)
 
 
 def message_kernel(pieces, label_ref, slot_ref, fixed_ref, labels_ref, slots_ref, out_ref):
@@ -447,13 +495,24 @@
             kept = kept[: low * chunk] + got.astype(f32)
             low //= 2
         return kept
-    kept = [None] * half
-    for k in reversed(range(half)):
-        at = slice(k * chunk, (k + 1) * chunk)
-        kept[k] = mine[at] + swap(sends[at], "dp", 1).astype(f32)
-    total = kept[0]
-    for k in reversed(range(1, half)):
-        total = total + swap(kept[k].astype(f16), "dp", 2 * k).astype(f32)
+    order = [k for k in (1, 3, 2, 0) if k < half]
+    got = {}
+    for k in order:
+        got[k] = swap(sends[k * chunk : (k + 1) * chunk], "dp", 1)
+    landed = []
+    before = None
+    for k in order:
+        other = got[k]
+        if before is not None:
+            other = lax.optimization_barrier((other, before))[0]
+        kept = mine[k * chunk : (k + 1) * chunk] + other.astype(f32)
+        if k == 0:
+            total = kept
+        else:
+            before = kept.astype(f16)
+            landed.append(swap(before, "dp", 2 * k))
+    for piece in landed:
+        total = total + piece.astype(f32)
     return total
 
 
@@ -479,10 +538,20 @@
             out = put(out, whole[at], k, side)
             out = put(out, other[at], k, 1 - side)
         return out
-    same = [own] + [swap(own, "dp", 2 * k) for k in range(1, half)]
-    for k in range(half):
-        out = put(out, same[k], k, side)
-        out = put(out, swap(same[k], "dp", 1), k, 1 - side)
+    same = {0: own}
+    for k in (1, 3, 2):
+        same[k] = swap(own, "dp", 2 * k)
+    for k in (0,) + (1, 3, 2):
+        other = swap(same[k], "dp", 1)
+        pair = jnp.where(
+            side == 0,
+            jnp.concatenate([same[k], other]),
+            jnp.concatenate([other, same[k]]),
+        )
+        at = (place ^ k) * 2 * rows
+        own_coef = lax.dynamic_slice_in_dim(coef, at, 2 * rows, 0)
+        grad = ridge_fixed * own_coef - pair.astype(f32)
+        out = lax.dynamic_update_slice_in_dim(out, grad, at, 0)
     return out
 
 
@@ -512,7 +581,7 @@
     label_row = labels.reshape(1, rows_here)
     block_row = fixed_blocks.reshape(1, group_rows)
 
-    send_feats, start = pack_feats(fixed_values, member_feats, slot_row, slot_total)
+    send_feats = pack_feats(member_feats, slot_row, slot_total)
     got_feats = lax.all_to_all(
         send_feats.reshape(dp_count, capacity, -1), "dp", 0, 0, tiled=True
     ).reshape(slot_total, -1)
@@ -520,9 +589,7 @@
         member_tiles, tile_source.reshape(1, -1), dp_count, capacity
     )
 
-    own = partial_scores(
-        start, fixed_values, block_row, fixed_coef, label_row, slot_row
-    )
+    own = partial_scores(fixed_values, block_row, fixed_coef, label_row, slot_row)
     pieces = [own] + [swap(own, "feat", k) for k in range(1, feat_count)]
     fixed, label, slot, message = build_message(
         pieces, label_row, slot_row, dp_count, capacity
@@ -541,10 +608,12 @@
             got_feats, got, member_slots, member_coef, feat_count
         )
     returned = lax.all_to_all(new_scores, ("dp", "feat"), 0, 0, tiled=True)
-    margin, residual, theirs, values = margins_and_theirs(
+    margin, residual, theirs, keep = margins_and_theirs(
         returned, fixed, label, slot, fixed_values, block_row, blocks, dp_count
     )
-    mine = gradient_mine(residual, values, block_row, blocks, dp_count)
+    mine = gradient_mine(
+        residual, keep, fixed_values, block_row, blocks, dp_count
+    )
     summed = reduce_chunks(theirs, mine, half).astype(f16)
     fixed_grad = spread_chunks(summed, side, place, half, fixed_coef)
     return (margin.reshape(rows_here), updated_coef, fixed_grad)

time: 88.5 us -> 84.7 us (0.957)
  starting transfers between devices: 33.3 us -> 30.9 us
  local copies, waits for them, and re-layouts: 3.04 us -> 1.23 us
    ppermute x21, starting transfers between devices: 26.1 us -> 23.6 us  [swap(): lax.ppermute(value, axis, [(i, i ^ offset) for i in range(lax.axis_size(a...]
    unnamed x20 -> x16, local copies, waits for them, and re-layouts: 2.81 us -> 1 us
  transfers between devices with their start and end apart: 22 -> 22, of which waited for: 11 -> 13; matrix products, arithmetic and copies ran while one was open for 0% -> 0% of each run, Pallas kernels for 13% -> 13%
where the time goes in v5:
time: 84.7 us; the launch traced here: 84.4 us
  starting transfers between devices  30.9 us (36%)
  Pallas kernels  21.6 us (26%)
  waiting for transfers between devices  19.6 us (23%)
  blocking collectives  9.82 us (12%)
  local copies, waits for them, and re-layouts  1.23 us (1%)
  between operations  0.92 us (1%)
    ppermute x21, starting transfers between devices, swap(): lax.ppermute(value, axis, [(i, i ^ offset) for i in range(lax.axis_size(a...  23.6 us
    ppermute x21, waiting for transfers between devices, swap(): lax.ppermute(value, axis, [(i, i ^ offset) for i in range(lax.axis_size(a...  19.6 us
    all_to_all x1, blocking collectives, body(): returned = lax.all_to_all(new_scores, ('dp', 'feat'), 0, 0, tiled=True)  9.82 us
    all_to_all x1, starting transfers between devices, body(): lax.all_to_all(send_feats.reshape(dp_count, capacity, -1), 'dp', 0, 0, ti...  7.29 us
    pallas_call x1, Pallas kernels, partial_scores(): pl.pallas_call(partial_kernel, in_specs=[pl.BlockSpec(memory_space=pltpu....  6.67 us
    pallas_call x1, Pallas kernels, margins_and_theirs(): pl.pallas_call(kernel, in_specs=[vmem] * 4 + [pl.BlockSpec(memory_space=p...  4.64 us
    pallas_call x1, Pallas kernels, pack_feats(): pl.pallas_call(pack_kernel, in_specs=[hbm, hbm], out_specs=hbm, out_shape...  3.27 us
    pallas_call x1, Pallas kernels, solve_members(): pl.pallas_call(solve_kernel, out_shape=(jax.ShapeDtypeStruct(member_coef....  3.11 us
  transfers between devices with their start and end apart: 22, of which 13 were waited for; matrix products, arithmetic and copies ran while one was open for 0% of the time, Pallas kernels for 13%

profile of v5, /device:TPU:0, one launch (start us, length us, event | category | flops | bytes accessed | tf_op | source)
XLA Modules:
  0.0 84.4 jit_solution(6315528783998460507)
XLA Ops:
  0.7 3.3 %pack_feats.1 = bf16[2048,256]{1,0:T(8,128)(2,1)} custom-call(bf16[1024,256]{1,0:T(8,128)(2,1)} %feats_in_ref.1, s32[1,1024]{1,0:T(1,128)} %bitcast.29), custom_call_target="tpu_custom_call" | custom-call | flops 1073741824 | bytes 1572864 | tf_op jit(solution)/shard_map/pack_feats/pallas_call | solution.py:283
  4.0 7.3 %all-to-all-start = ((bf16[8,256,256]{2,1,0:T(8,128)(2,1)}), bf16[8,256,256]{2,1,0:T(8,128)(2,1)S(1)}, u32[]{:S(2)}, u32[]{:S(2)}) async-start(bf16[8,256,256]{2,1,0:T(8,128)(2,1)} %bitcast.34), calls=%async_computation | async-start | bytes 2097152 | tf_op jit(solution)/shard_map/all_to_all | solution.py:585
  11.3 6.7 %partial_scores.1.refs_0_ = f32[6,1024]{1,0:T(8,128)S(1)} custom-call(bf16[4096,512]{1,0:T(8,128)(2,1)} %refs_2_.1, s32[1,4096]{1,0:T(1,128)S(1)} %bitcast.25, f32[512,512]{1,0:T(8,128)S(1)} %copy-done, s32[1,1024]{1,0:T(1,128)S(1)} %bitcast.32, s32[1,1024]{1,0:T(1,128)S(1)} %bitcast.30), custom_call_target="tpu_custom_call" | custom-call | flops 4294967296 | bytes 5242880 | tf_op jit(solution)/shard_map/partial_scores/pallas_call | solution.py:87
  18.1 1.6 %collective-permute-start.1 = (f32[6,1024]{1,0:T(8,128)S(1)}, f32[6,1024]{1,0:T(8,128)S(1)}, u32[]{:S(2)}, u32[]{:S(2)}) collective-permute-start(f32[6,1024]{1,0:T(8,128)S(1)} %partial_scores.1.refs_0_), channel_id=1, source_target_pairs={{0,2},{1,3},{2,0},{3,1},{4,6},{5,7},{6,4},{7,5},{8,10},{9,11},{10,... | collective-permute-start | bytes 73736 | tf_op jit(solution)/shard_map/ppermute | solution.py:461
  19.9 2.1 %collective-permute-done.1.refs_2_ = f32[6,1024]{1,0:T(8,128)S(1)} collective-permute-done((f32[6,1024]{1,0:T(8,128)S(1)}, f32[6,1024]{1,0:T(8,128)S(1)}, u32[]{:S(2)}, u32[]{:S(2)}) %collective-permute-start.1) | collective-permute-done | bytes 24608 | tf_op jit(solution)/shard_map/ppermute | solution.py:461
  22.1 1.0 %collective-permute-done.2.refs_3_ = f32[6,1024]{1,0:T(8,128)S(1)} collective-permute-done((f32[6,1024]{1,0:T(8,128)S(1)}, f32[6,1024]{1,0:T(8,128)S(1)}, u32[]{:S(2)}, u32[]{:S(2)}) %collective-permute-start.2) | collective-permute-done | bytes 24608 | tf_op jit(solution)/shard_map/ppermute | solution.py:461
  23.3 2.1 %collective-permute-start.3 = (f32[4,2,256]{2,1,0:T(2,128)S(1)}, f32[4,2,256]{2,1,0:T(2,128)S(1)}, u32[]{:S(2)}, u32[]{:S(2)}) collective-permute-start(f32[4,2,256]{2,1,0:T(2,128)S(1)} %get-tuple-element.38), channel_id=1, source_target_pairs={{0,4},{4,0},{8,12},{12,8},{16,20},{20,16},{24,28},{28,24},{1,5},{5... | collective-permute-start | bytes 24584 | tf_op jit(solution)/shard_map/ppermute | solution.py:461
  25.4 1.7 %collective-permute-done.3 = f32[4,2,256]{2,1,0:T(2,128)S(1)} collective-permute-done((f32[4,2,256]{2,1,0:T(2,128)S(1)}, f32[4,2,256]{2,1,0:T(2,128)S(1)}, u32[]{:S(2)}, u32[]{:S(2)}) %collective-permute-start.3) | collective-permute-done | bytes 8224 | tf_op jit(solution)/shard_map/ppermute | solution.py:461
  27.2 2.3 %collective-permute-start.4 = (f32[2,2,256]{2,1,0:T(2,128)S(1)}, f32[2,2,256]{2,1,0:T(2,128)S(1)}, u32[]{:S(2)}, u32[]{:S(2)}) collective-permute-start(f32[2,2,256]{2,1,0:T(2,128)S(1)} %get-tuple-element.35), channel_id=1, source_target_pairs={{0,8},{4,12},{8,0},{12,4},{16,24},{20,28},{24,16},{28,20},{1,9},{5... | collective-permute-start | bytes 12296 | tf_op jit(solution)/shard_map/ppermute | solution.py:461
  29.5 1.0 %slot_members.1.member_ref = f32[8,256]{1,0:T(8,128)S(1)} custom-call(s32[4]{0:T(128)S(1)} %copy-done.5, s32[1,2432]{1,0:T(1,128)S(1)} %reshape.40.source_ref), custom_call_target="tpu_custom_call" | custom-call | tf_op jit(solution)/shard_map/slot_members/pallas_call | solution.py:360
  30.4 2.4 %collective-permute-start.5 = (f32[2,2,256]{2,1,0:T(2,128)S(1)}, f32[2,2,256]{2,1,0:T(2,128)S(1)}, u32[]{:S(2)}, u32[]{:S(2)}) collective-permute-start(f32[2,2,256]{2,1,0:T(2,128)S(1)} %get-tuple-element.34), channel_id=1, source_target_pairs={{0,16},{4,20},{8,24},{12,28},{16,0},{20,4},{24,8},{28,12},{1,17},{... | collective-permute-start | bytes 12296 | tf_op jit(solution)/shard_map/ppermute | solution.py:461
  32.9 4.4 %collective-permute-done.5 = f32[2,2,256]{2,1,0:T(2,128)S(1)} collective-permute-done((f32[2,2,256]{2,1,0:T(2,128)S(1)}, f32[2,2,256]{2,1,0:T(2,128)S(1)}, u32[]{:S(2)}, u32[]{:S(2)}) %collective-permute-start.5) | collective-permute-done | bytes 4128 | tf_op jit(solution)/shard_map/ppermute | solution.py:461
  37.3 0.9 %collective-permute-done.6 = f32[2,2,256]{2,1,0:T(2,128)S(1)} collective-permute-done((f32[2,2,256]{2,1,0:T(2,128)S(1)}, f32[2,2,256]{2,1,0:T(2,128)S(1)}, u32[]{:S(2)}, u32[]{:S(2)}) %collective-permute-start.6) | collective-permute-done | bytes 4128 | tf_op jit(solution)/shard_map/ppermute | solution.py:461
  38.2 3.1 %solve_members.1 = (f32[4,256]{1,0:T(4,128)}, f32[32,1,256]{2,1,0:T(1,128)S(1)}) custom-call(bf16[2048,256]{1,0:T(8,128)(2,1)S(1)} %bitcast.23, f32[8,2,256]{2,1,0:T(2,128)S(1)} %bitcast.24, f32[8,256]{1,0:T(8,128)S(1)} %slot_members.1.member_ref, f32[4,256]{1,0:T(4,128)S(1)} %copy-done.2), custom_call_target="tpu_custom_call" | custom-call | tf_op jit(solution)/shard_map/solve_members/pallas_call | solution.py:449
  41.3 9.8 %all_to_all.10.refs_0_ = f32[32,1,256]{2,1,0:T(1,128)S(1)} all-to-all(f32[32,1,256]{2,1,0:T(1,128)S(1)} %get-tuple-element.17), channel_id=1, replica_groups=mesh['dp'=8,'feat'=4] {'dp','feat'}, dimensions={0} | all-to-all | bytes 65536 | tf_op jit(solution)/shard_map/all_to_all | solution.py:610
  51.2 4.6 %margins_and_theirs.1 = (f32[1,1024]{1,0:T(1,128)}, f32[4,1024]{1,0:T(4,128)S(1)}, f32[256,512]{1,0:T(8,128)S(1)}, bf16[2048,512]{1,0:T(8,128)(2,1)S(1)}) custom-call(f32[32,1,256]{2,1,0:T(1,128)S(1)} %all_to_all.10.refs_0_, f32[4,1024]{1,0:T(4,128)S(1)} %get-tuple-element.18.refs_1_, f32[4,1024]{1,0:T(4,128)S(1)} %get-tuple-element.19.refs_2_, ...), custom_call_target="tpu_custom_call" | custom-call | tf_op jit(solution)/shard_map/margins_and_theirs/pallas_call | solution.py:182
  56.6 1.4 %collective-permute-start.9 = (f16[64,512]{1,0:T(8,128)(2,1)S(1)}, f16[64,512]{1,0:T(8,128)(2,1)S(1)}, u32[]{:S(2)}, u32[]{:S(2)}) collective-permute-start(f16[64,512]{1,0:T(8,128)(2,1)S(1)} %get-tuple-element.31), channel_id=1, source_target_pairs={{0,4},{4,0},{8,12},{12,8},{16,20},{20,16},{24,28},{28,24},{1,5},{5... | collective-permute-start | bytes 196616 | tf_op jit(solution)/shard_map/ppermute | solution.py:461
  58.6 1.4 %collective-permute-start.7 = (f16[64,512]{1,0:T(8,128)(2,1)S(1)}, f16[64,512]{1,0:T(8,128)(2,1)S(1)}, u32[]{:S(2)}, u32[]{:S(2)}) collective-permute-start(f16[64,512]{1,0:T(8,128)(2,1)S(1)} %get-tuple-element.29), channel_id=1, source_target_pairs={{0,4},{4,0},{8,12},{12,8},{16,20},{20,16},{24,28},{28,24},{1,5},{5... | collective-permute-start | bytes 196616 | tf_op jit(solution)/shard_map/ppermute | solution.py:461
  60.0 2.6 %gradient_mine.1 = f32[256,512]{1,0:T(8,128)S(1)} custom-call(f32[4,1024]{1,0:T(4,128)S(1)} %get-tuple-element.23.refs_0_, bf16[2048,512]{1,0:T(8,128)(2,1)S(1)} %get-tuple-element.24.refs_1_, bf16[4096,512]{1,0:T(8,128)(2,1)} %refs_2_.1, s32[1,4096]{1,0:T(1,128)S(1)} %bitcast.27), custom_call_target="tpu_custom_call" | custom-call | flops 2147483648 | bytes 4718592 | tf_op jit(solution)/shard_map/gradient_mine/pallas_call | solution.py:236
  62.8 0.8 collective-permute-done.8
  63.9 2.3 %collective-permute-start.12 = (f16[64,512]{1,0:T(8,128)(2,1)S(1)}, f16[64,512]{1,0:T(8,128)(2,1)S(1)}, u32[]{:S(2)}, u32[]{:S(2)}) collective-permute-start(f16[64,512]{1,0:T(8,128)(2,1)S(1)} %fusion.1), channel_id=1, source_target_pairs={{0,24},{4,28},{8,16},{12,20},{16,8},{20,12},{24,0},{28,4},{1,25},{... | collective-permute-start | bytes 196616 | tf_op jit(solution)/shard_map/ppermute | solution.py:461
  66.2 1.0 %collective-permute-start.11 = (f16[64,512]{1,0:T(8,128)(2,1)S(1)}, f16[64,512]{1,0:T(8,128)(2,1)S(1)}, u32[]{:S(2)}, u32[]{:S(2)}) collective-permute-start(f16[64,512]{1,0:T(8,128)(2,1)S(1)} %fusion), channel_id=1, source_target_pairs={{0,8},{4,12},{8,0},{12,4},{16,24},{20,28},{24,16},{28,20},{1,9},{5... | collective-permute-start | bytes 196616 | tf_op jit(solution)/shard_map/ppermute | solution.py:461
  67.2 2.9 %collective-permute-done.13 = f16[64,512]{1,0:T(8,128)(2,1)S(1)} collective-permute-done((f16[64,512]{1,0:T(8,128)(2,1)S(1)}, f16[64,512]{1,0:T(8,128)(2,1)S(1)}, u32[]{:S(2)}, u32[]{:S(2)}) %collective-permute-start.13) | collective-permute-done | bytes 65568 | tf_op jit(solution)/shard_map/ppermute | solution.py:461
  70.1 1.0 %collective-permute-done.11 = f16[64,512]{1,0:T(8,128)(2,1)S(1)} collective-permute-done((f16[64,512]{1,0:T(8,128)(2,1)S(1)}, f16[64,512]{1,0:T(8,128)(2,1)S(1)}, u32[]{:S(2)}, u32[]{:S(2)}) %collective-permute-start.11) | collective-permute-done | bytes 65568 | tf_op jit(solution)/shard_map/ppermute | solution.py:461
  71.6 1.7 %collective-permute-start.17 = (f16[64,512]{1,0:T(8,128)(2,1)S(1)}, f16[64,512]{1,0:T(8,128)(2,1)S(1)}, u32[]{:S(2)}, u32[]{:S(2)}) collective-permute-start(f16[64,512]{1,0:T(8,128)(2,1)S(1)} %fusion.6), channel_id=1, source_target_pairs={{0,24},{4,28},{8,16},{12,20},{16,8},{20,12},{24,0},{28,4},{1,25},{... | collective-permute-start | bytes 196616 | tf_op jit(solution)/shard_map/ppermute | solution.py:461
  73.3 1.5 %collective-permute-start.19 = (f16[64,512]{1,0:T(8,128)(2,1)S(1)}, f16[64,512]{1,0:T(8,128)(2,1)S(1)}, u32[]{:S(2)}, u32[]{:S(2)}) collective-permute-start(f16[64,512]{1,0:T(8,128)(2,1)S(1)} %fusion.6), channel_id=1, source_target_pairs={{0,16},{4,20},{8,24},{12,28},{16,0},{20,4},{24,8},{28,12},{1,17},{... | collective-permute-start | bytes 196616 | tf_op jit(solution)/shard_map/ppermute | solution.py:461
  76.0 1.0 %collective-permute-start.16 = (f16[64,512]{1,0:T(8,128)(2,1)S(1)}, f16[64,512]{1,0:T(8,128)(2,1)S(1)}, u32[]{:S(2)}, u32[]{:S(2)}) collective-permute-start(f16[64,512]{1,0:T(8,128)(2,1)S(1)} %collective-permute-done.15), channel_id=1, source_target_pairs={{0,4},{4,0},{8,12},{12,8},{16,20},{20,16},{24,28},{28,24},{1,5},{5... | collective-permute-start | bytes 196616 | tf_op jit(solution)/shard_map/ppermute | solution.py:461
  77.7 1.0 %collective-permute-start.18 = (f16[64,512]{1,0:T(8,128)(2,1)S(1)}, f16[64,512]{1,0:T(8,128)(2,1)S(1)}, u32[]{:S(2)}, u32[]{:S(2)}) collective-permute-start(f16[64,512]{1,0:T(8,128)(2,1)S(1)} %collective-permute-done.17), channel_id=1, source_target_pairs={{0,4},{4,0},{8,12},{12,8},{16,20},{20,16},{24,28},{28,24},{1,5},{5... | collective-permute-start | bytes 196616 | tf_op jit(solution)/shard_map/ppermute | solution.py:461
  79.1 0.9 %collective-permute-start.20 = (f16[64,512]{1,0:T(8,128)(2,1)S(1)}, f16[64,512]{1,0:T(8,128)(2,1)S(1)}, u32[]{:S(2)}, u32[]{:S(2)}) collective-permute-start(f16[64,512]{1,0:T(8,128)(2,1)S(1)} %collective-permute-done.19), channel_id=1, source_target_pairs={{0,4},{4,0},{8,12},{12,8},{16,20},{20,16},{24,28},{28,24},{1,5},{5... | collective-permute-start | bytes 196616 | tf_op jit(solution)/shard_map/ppermute | solution.py:461
  80.3 1.6 %collective-permute-done.18 = f16[64,512]{1,0:T(8,128)(2,1)S(1)} collective-permute-done((f16[64,512]{1,0:T(8,128)(2,1)S(1)}, f16[64,512]{1,0:T(8,128)(2,1)S(1)}, u32[]{:S(2)}, u32[]{:S(2)}) %collective-permute-start.18) | collective-permute-done | bytes 65568 | tf_op jit(solution)/shard_map/ppermute | solution.py:461
  82.0 1.4 %collective-permute-done.20 = f16[64,512]{1,0:T(8,128)(2,1)S(1)} collective-permute-done((f16[64,512]{1,0:T(8,128)(2,1)S(1)}, f16[64,512]{1,0:T(8,128)(2,1)S(1)}, u32[]{:S(2)}, u32[]{:S(2)}) %collective-permute-start.20) | collective-permute-done | bytes 65568 | tf_op jit(solution)/shard_map/ppermute | solution.py:461
  83.5 1.0 %copy-done.6 = f32[512,512]{1,0:T(8,128)} copy-done((f32[512,512]{1,0:T(8,128)}, f32[512,512]{1,0:T(8,128)S(1)}, u32[]{:S(2)}) %copy-start.6) | copy-done | bytes 1048600
  (55 shorter events, 5.6 us)
Async XLA Ops:
  0.6 10.6 %copy-start.3 = (s32[1024]{0:T(1024)S(1)}, s32[1024]{0:T(1024)}, u32[]{:S(2)}) copy-start(s32[1024]{0:T(1024)} %param.15) | copy-start | bytes 12292
  0.6 10.6 %copy-start.1 = (s32[4096,1]{0,1:T(1,128)S(1)}, s32[4096,1]{0,1:T(1,128)}, u32[]{:S(2)}) copy-start(s32[4096,1]{0,1:T(1,128)} %param.12) | copy-start | bytes 49156
  0.7 10.6 %copy-start.4 = (s32[1024]{0:T(1024)S(1)}, s32[1024]{0:T(1024)}, u32[]{:S(2)}) copy-start(s32[1024]{0:T(1024)} %param.10) | copy-start | bytes 12292
  0.7 10.6 %copy-start = (f32[512,512]{1,0:T(8,128)S(1)}, f32[512,512]{1,0:T(8,128)}, u32[]{:S(2)}) copy-start(f32[512,512]{1,0:T(8,128)} %coef_ref.2) | copy-start | bytes 3145732
  4.0 34.3 %all-to-all-start = ((bf16[8,256,256]{2,1,0:T(8,128)(2,1)}), bf16[8,256,256]{2,1,0:T(8,128)(2,1)S(1)}, u32[]{:S(2)}, u32[]{:S(2)}) async-start(bf16[8,256,256]{2,1,0:T(8,128)(2,1)} %bitcast.34), calls=%async_computation | async-start | bytes 2097152 | tf_op jit(solution)/shard_map/all_to_all | solution.py:585
  11.3 18.2 %copy-start.7 = (s32[2432]{0:T(1024)S(1)}, s32[2432]{0:T(1024)}, u32[]{:S(2)}) copy-start(s32[2432]{0:T(1024)} %param.16) | copy-start | bytes 29188
  11.3 18.2 %copy-start.5 = (s32[4]{0:T(128)S(1)}, s32[4]{0:T(128)}, u32[]{:S(2)}) copy-start(s32[4]{0:T(128)} %tiles_ref.1) | copy-start | bytes 52
  11.3 26.9 %copy-start.2 = (f32[4,256]{1,0:T(4,128)S(1)}, f32[4,256]{1,0:T(4,128)}, u32[]{:S(2)}) copy-start(f32[4,256]{1,0:T(4,128)} %coef_ref.3) | copy-start | bytes 12292
  18.0 1.9 %collective-permute-start = (f32[6,1024]{1,0:T(8,128)S(1)}, f32[6,1024]{1,0:T(8,128)S(1)}, u32[]{:S(2)}, u32[]{:S(2)}) collective-permute-start(f32[6,1024]{1,0:T(8,128)S(1)} %partial_scores.1.refs_0_), channel_id=1, source_target_pairs={{0,1},{1,0},{2,3},{3,2},{4,5},{5,4},{6,7},{7,6},{8,9},{9,8},{10,11... | collective-permute-start | bytes 73736 | tf_op jit(solution)/shard_map/ppermute | solution.py:461
  18.1 4.0 %collective-permute-start.1 = (f32[6,1024]{1,0:T(8,128)S(1)}, f32[6,1024]{1,0:T(8,128)S(1)}, u32[]{:S(2)}, u32[]{:S(2)}) collective-permute-start(f32[6,1024]{1,0:T(8,128)S(1)} %partial_scores.1.refs_0_), channel_id=1, source_target_pairs={{0,2},{1,3},{2,0},{3,1},{4,6},{5,7},{6,4},{7,5},{8,10},{9,11},{10,... | collective-permute-start | bytes 73736 | tf_op jit(solution)/shard_map/ppermute | solution.py:461
  19.7 3.4 %collective-permute-start.2 = (f32[6,1024]{1,0:T(8,128)S(1)}, f32[6,1024]{1,0:T(8,128)S(1)}, u32[]{:S(2)}, u32[]{:S(2)}) collective-permute-start(f32[6,1024]{1,0:T(8,128)S(1)} %partial_scores.1.refs_0_), channel_id=1, source_target_pairs={{0,3},{1,2},{2,1},{3,0},{4,7},{5,6},{6,5},{7,4},{8,11},{9,10},{10,... | collective-permute-start | bytes 73736 | tf_op jit(solution)/shard_map/ppermute | solution.py:461
  23.3 3.8 %collective-permute-start.3 = (f32[4,2,256]{2,1,0:T(2,128)S(1)}, f32[4,2,256]{2,1,0:T(2,128)S(1)}, u32[]{:S(2)}, u32[]{:S(2)}) collective-permute-start(f32[4,2,256]{2,1,0:T(2,128)S(1)} %get-tuple-element.38), channel_id=1, source_target_pairs={{0,4},{4,0},{8,12},{12,8},{16,20},{20,16},{24,28},{28,24},{1,5},{5... | collective-permute-start | bytes 24584 | tf_op jit(solution)/shard_map/ppermute | solution.py:461
  27.2 5.7 %collective-permute-start.4 = (f32[2,2,256]{2,1,0:T(2,128)S(1)}, f32[2,2,256]{2,1,0:T(2,128)S(1)}, u32[]{:S(2)}, u32[]{:S(2)}) collective-permute-start(f32[2,2,256]{2,1,0:T(2,128)S(1)} %get-tuple-element.35), channel_id=1, source_target_pairs={{0,8},{4,12},{8,0},{12,4},{16,24},{20,28},{24,16},{28,20},{1,9},{5... | collective-permute-start | bytes 12296 | tf_op jit(solution)/shard_map/ppermute | solution.py:461
  30.4 6.8 %collective-permute-start.5 = (f32[2,2,256]{2,1,0:T(2,128)S(1)}, f32[2,2,256]{2,1,0:T(2,128)S(1)}, u32[]{:S(2)}, u32[]{:S(2)}) collective-permute-start(f32[2,2,256]{2,1,0:T(2,128)S(1)} %get-tuple-element.34), channel_id=1, source_target_pairs={{0,16},{4,20},{8,24},{12,28},{16,0},{20,4},{24,8},{28,12},{1,17},{... | collective-permute-start | bytes 12296 | tf_op jit(solution)/shard_map/ppermute | solution.py:461
  32.8 5.4 %collective-permute-start.6 = (f32[2,2,256]{2,1,0:T(2,128)S(1)}, f32[2,2,256]{2,1,0:T(2,128)S(1)}, u32[]{:S(2)}, u32[]{:S(2)}) collective-permute-start(f32[2,2,256]{2,1,0:T(2,128)S(1)} %get-tuple-element.33), channel_id=1, source_target_pairs={{0,24},{4,28},{8,16},{12,20},{16,8},{20,12},{24,0},{28,4},{1,25},{... | collective-permute-start | bytes 12296 | tf_op jit(solution)/shard_map/ppermute | solution.py:461
  55.9 6.8 %collective-permute-start.10 = (f16[64,512]{1,0:T(8,128)(2,1)S(1)}, f16[64,512]{1,0:T(8,128)(2,1)S(1)}, u32[]{:S(2)}, u32[]{:S(2)}) collective-permute-start(f16[64,512]{1,0:T(8,128)(2,1)S(1)} %get-tuple-element.30), channel_id=1, source_target_pairs={{0,4},{4,0},{8,12},{12,8},{16,20},{20,16},{24,28},{28,24},{1,5},{5... | collective-permute-start | bytes 196616 | tf_op jit(solution)/shard_map/ppermute | solution.py:461
  56.6 6.2 %collective-permute-start.9 = (f16[64,512]{1,0:T(8,128)(2,1)S(1)}, f16[64,512]{1,0:T(8,128)(2,1)S(1)}, u32[]{:S(2)}, u32[]{:S(2)}) collective-permute-start(f16[64,512]{1,0:T(8,128)(2,1)S(1)} %get-tuple-element.31), channel_id=1, source_target_pairs={{0,4},{4,0},{8,12},{12,8},{16,20},{20,16},{24,28},{28,24},{1,5},{5... | collective-permute-start | bytes 196616 | tf_op jit(solution)/shard_map/ppermute | solution.py:461
  58.0 5.6 %collective-permute-start.8 = (f16[64,512]{1,0:T(8,128)(2,1)S(1)}, f16[64,512]{1,0:T(8,128)(2,1)S(1)}, u32[]{:S(2)}, u32[]{:S(2)}) collective-permute-start(f16[64,512]{1,0:T(8,128)(2,1)S(1)} %get-tuple-element.32), channel_id=1, source_target_pairs={{0,4},{4,0},{8,12},{12,8},{16,20},{20,16},{24,28},{28,24},{1,5},{5... | collective-permute-start | bytes 196616 | tf_op jit(solution)/shard_map/ppermute | solution.py:461
  58.6 8.6 %collective-permute-start.7 = (f16[64,512]{1,0:T(8,128)(2,1)S(1)}, f16[64,512]{1,0:T(8,128)(2,1)S(1)}, u32[]{:S(2)}, u32[]{:S(2)}) collective-permute-start(f16[64,512]{1,0:T(8,128)(2,1)S(1)} %get-tuple-element.29), channel_id=1, source_target_pairs={{0,4},{4,0},{8,12},{12,8},{16,20},{20,16},{24,28},{28,24},{1,5},{5... | collective-permute-start | bytes 196616 | tf_op jit(solution)/shard_map/ppermute | solution.py:461
  63.6 6.5 %collective-permute-start.13 = (f16[64,512]{1,0:T(8,128)(2,1)S(1)}, f16[64,512]{1,0:T(8,128)(2,1)S(1)}, u32[]{:S(2)}, u32[]{:S(2)}) collective-permute-start(f16[64,512]{1,0:T(8,128)(2,1)S(1)} %fusion.2), channel_id=1, source_target_pairs={{0,16},{4,20},{8,24},{12,28},{16,0},{20,4},{24,8},{28,12},{1,17},{... | collective-permute-start | bytes 196616 | tf_op jit(solution)/shard_map/ppermute | solution.py:461
  63.9 6.2 %collective-permute-start.12 = (f16[64,512]{1,0:T(8,128)(2,1)S(1)}, f16[64,512]{1,0:T(8,128)(2,1)S(1)}, u32[]{:S(2)}, u32[]{:S(2)}) collective-permute-start(f16[64,512]{1,0:T(8,128)(2,1)S(1)} %fusion.1), channel_id=1, source_target_pairs={{0,24},{4,28},{8,16},{12,20},{16,8},{20,12},{24,0},{28,4},{1,25},{... | collective-permute-start | bytes 196616 | tf_op jit(solution)/shard_map/ppermute | solution.py:461
  66.2 4.9 %collective-permute-start.11 = (f16[64,512]{1,0:T(8,128)(2,1)S(1)}, f16[64,512]{1,0:T(8,128)(2,1)S(1)}, u32[]{:S(2)}, u32[]{:S(2)}) collective-permute-start(f16[64,512]{1,0:T(8,128)(2,1)S(1)} %fusion), channel_id=1, source_target_pairs={{0,8},{4,12},{8,0},{12,4},{16,24},{20,28},{24,16},{28,20},{1,9},{5... | collective-permute-start | bytes 196616 | tf_op jit(solution)/shard_map/ppermute | solution.py:461
  71.2 4.8 %collective-permute-start.15 = (f16[64,512]{1,0:T(8,128)(2,1)S(1)}, f16[64,512]{1,0:T(8,128)(2,1)S(1)}, u32[]{:S(2)}, u32[]{:S(2)}) collective-permute-start(f16[64,512]{1,0:T(8,128)(2,1)S(1)} %fusion.6), channel_id=1, source_target_pairs={{0,8},{4,12},{8,0},{12,4},{16,24},{20,28},{24,16},{28,20},{1,9},{5... | collective-permute-start | bytes 196616 | tf_op jit(solution)/shard_map/ppermute | solution.py:461
  71.6 6.1 %collective-permute-start.17 = (f16[64,512]{1,0:T(8,128)(2,1)S(1)}, f16[64,512]{1,0:T(8,128)(2,1)S(1)}, u32[]{:S(2)}, u32[]{:S(2)}) collective-permute-start(f16[64,512]{1,0:T(8,128)(2,1)S(1)} %fusion.6), channel_id=1, source_target_pairs={{0,24},{4,28},{8,16},{12,20},{16,8},{20,12},{24,0},{28,4},{1,25},{... | collective-permute-start | bytes 196616 | tf_op jit(solution)/shard_map/ppermute | solution.py:461
  73.3 5.9 %collective-permute-start.19 = (f16[64,512]{1,0:T(8,128)(2,1)S(1)}, f16[64,512]{1,0:T(8,128)(2,1)S(1)}, u32[]{:S(2)}, u32[]{:S(2)}) collective-permute-start(f16[64,512]{1,0:T(8,128)(2,1)S(1)} %fusion.6), channel_id=1, source_target_pairs={{0,16},{4,20},{8,24},{12,28},{16,0},{20,4},{24,8},{28,12},{1,17},{... | collective-permute-start | bytes 196616 | tf_op jit(solution)/shard_map/ppermute | solution.py:461
  74.7 5.3 %collective-permute-start.14 = (f16[64,512]{1,0:T(8,128)(2,1)S(1)}, f16[64,512]{1,0:T(8,128)(2,1)S(1)}, u32[]{:S(2)}, u32[]{:S(2)}) collective-permute-start(f16[64,512]{1,0:T(8,128)(2,1)S(1)} %fusion.6), channel_id=1, source_target_pairs={{0,4},{4,0},{8,12},{12,8},{16,20},{20,16},{24,28},{28,24},{1,5},{5... | collective-permute-start | bytes 196616 | tf_op jit(solution)/shard_map/ppermute | solution.py:461
  76.0 4.3 %collective-permute-start.16 = (f16[64,512]{1,0:T(8,128)(2,1)S(1)}, f16[64,512]{1,0:T(8,128)(2,1)S(1)}, u32[]{:S(2)}, u32[]{:S(2)}) collective-permute-start(f16[64,512]{1,0:T(8,128)(2,1)S(1)} %collective-permute-done.15), channel_id=1, source_target_pairs={{0,4},{4,0},{8,12},{12,8},{16,20},{20,16},{24,28},{28,24},{1,5},{5... | collective-permute-start | bytes 196616 | tf_op jit(solution)/shard_map/ppermute | solution.py:461
  77.7 4.3 %collective-permute-start.18 = (f16[64,512]{1,0:T(8,128)(2,1)S(1)}, f16[64,512]{1,0:T(8,128)(2,1)S(1)}, u32[]{:S(2)}, u32[]{:S(2)}) collective-permute-start(f16[64,512]{1,0:T(8,128)(2,1)S(1)} %collective-permute-done.17), channel_id=1, source_target_pairs={{0,4},{4,0},{8,12},{12,8},{16,20},{20,16},{24,28},{28,24},{1,5},{5... | collective-permute-start | bytes 196616 | tf_op jit(solution)/shard_map/ppermute | solution.py:461
  79.1 4.3 %collective-permute-start.20 = (f16[64,512]{1,0:T(8,128)(2,1)S(1)}, f16[64,512]{1,0:T(8,128)(2,1)S(1)}, u32[]{:S(2)}, u32[]{:S(2)}) collective-permute-start(f16[64,512]{1,0:T(8,128)(2,1)S(1)} %collective-permute-done.19), channel_id=1, source_target_pairs={{0,4},{4,0},{8,12},{12,8},{16,20},{20,16},{24,28},{28,24},{1,5},{5... | collective-permute-start | bytes 196616 | tf_op jit(solution)/shard_map/ppermute | solution.py:461
  83.5 1.0 %copy-start.6 = (f32[512,512]{1,0:T(8,128)}, f32[512,512]{1,0:T(8,128)S(1)}, u32[]{:S(2)}) copy-start(f32[512,512]{1,0:T(8,128)S(1)} %subtract_dynamic-update-slice_fusion) | copy-start | bytes 3145732

commit v6 on v5

--- a/solution.py
+++ b/solution.py
@@ -49,14 +49,17 @@
 
 
 def partial_kernel(
-    values_ref, block_ref, coef_ref, label_ref, slot_ref, out_ref, held_ref, sem
+    values_ref, block_ref, coef_ref, label_ref, slot_ref, out_ref, keep_ref, held_ref, sem
 ):
     rows = out_ref.shape[1]
     blocks = coef_ref.shape[0]
     shards = values_ref.shape[0] // rows
+    first = keep_ref.shape[0] // rows
     copies = [
         pltpu.make_async_copy(
-            values_ref.at[pl.ds(i * rows, rows)], held_ref.at[i], sem.at[i]
+            values_ref.at[pl.ds(i * rows, rows)],
+            keep_ref.at[pl.ds(i * rows, rows)] if i < first else held_ref.at[i - first],
+            sem.at[i],
         )
         for i in range(shards)
     ]
@@ -70,7 +73,7 @@
         block = block_ref[:, i * rows : (i + 1) * rows]
         column = jnp.broadcast_to(block, (TILE, rows)).T
         copies[i].wait()
-        values = held_ref[i]
+        values = keep_ref[i * rows : (i + 1) * rows, :] if i < first else held_ref[i - first]
         product = dot_nn(values, high) + dot_nn(values, low)
         total = jnp.zeros((rows, TILE), f32)
         for at in range(0, blocks, TILE):
@@ -83,14 +86,18 @@
     rows_here = slot_row.shape[1]
     blocks = fixed_coef.shape[0]
     shards = rows // rows_here
+    first = shards // 2
     vmem = pl.BlockSpec(memory_space=pltpu.VMEM)
     return pl.pallas_call(
         partial_kernel,
         in_specs=[pl.BlockSpec(memory_space=pltpu.HBM)] + [vmem] * 4,
-        out_specs=vmem,
-        out_shape=jax.ShapeDtypeStruct((shards + 2, rows_here), f32),
+        out_specs=[vmem, vmem],
+        out_shape=(
+            jax.ShapeDtypeStruct((shards + 2, rows_here), f32),
+            jax.ShapeDtypeStruct((first * rows_here, width), bf16),
+        ),
         scratch_shapes=[
-            pltpu.VMEM((shards, rows_here, width), bf16),
+            pltpu.VMEM((shards - first, rows_here, width), bf16),
             pltpu.SemaphoreType.DMA((shards,)),
         ],
         cost_estimate=pl.CostEstimate(
@@ -127,42 +134,59 @@
             out_ref[...] += total
 
 
+def lookup_products(returned_ref, slot, shards, shard):
+    sources, _, capacity = returned_ref.shape
+    table = jnp.concatenate(split(returned_ref[...].reshape(sources, capacity), 3), axis=0)
+    owner = slot // capacity
+    place_hot = jnp.where(hot(slot - owner * capacity, capacity), 1.0, 0.0).astype(bf16)
+    found = dot_nn(table, place_hot)
+    found = found[:sources] + (found[sources : 2 * sources] + found[2 * sources :])
+    owner_hot = hot(owner * shards + shard, sources)
+    return jnp.sum(jnp.where(owner_hot, found, 0.0), axis=0, keepdims=True)
+
+
+def lookup_lanes(returned_ref, slot, shards, shard):
+    sources, _, capacity = returned_ref.shape
+    rows = slot.shape[1]
+    folds = rows // TILE
+    slot = jnp.concatenate([slot[:, i * TILE : (i + 1) * TILE] for i in range(folds)], axis=0)
+    block = slot // TILE
+    lane = slot % TILE
+    score = jnp.zeros(slot.shape, f32)
+    per_owner = capacity // TILE
+    for owner in range(sources // shards):
+        for part in range(per_owner):
+            piece = returned_ref[owner * shards + shard, :, part * TILE : (part + 1) * TILE]
+            spread = jnp.broadcast_to(piece, slot.shape)
+            found = jnp.take_along_axis(spread, lane, axis=1)
+            score = jnp.where(block == owner * per_owner + part, found, score)
+    return jnp.concatenate([score[i : i + 1] for i in range(folds)], axis=1)
+
+
 def margin_kernel(
-    dp_count, returned_ref, fixed_ref, label_ref, slot_ref, values_ref, block_ref,
-    margin_ref, residual_ref, out_ref, keep_ref, all_ref, held_ref, sem,
+    dp_count, returned_ref, fixed_ref, label_ref, slot_ref, keep_ref, values_ref, block_ref,
+    margin_ref, residual_ref, out_ref, all_ref, held_ref, sem,
 ):
     kept = keep_ref.shape[0]
-    copies = [
-        pltpu.make_async_copy(values_ref.at[pl.ds(0, kept)], keep_ref, sem.at[0]),
-        pltpu.make_async_copy(
-            values_ref.at[pl.ds(kept, held_ref.shape[0])], held_ref, sem.at[1]
-        ),
-    ]
-    for copy in copies:
-        copy.start()
-    sources, _, capacity = returned_ref.shape
+    copy = pltpu.make_async_copy(values_ref.at[pl.ds(kept, held_ref.shape[0])], held_ref, sem)
+    copy.start()
+    capacity = returned_ref.shape[2]
     shards, rows = fixed_ref.shape
-    pieces = split(returned_ref[...].reshape(sources, capacity), 3)
-    table = jnp.concatenate(pieces, axis=0)
+    lookup = lookup_lanes if capacity % TILE == 0 else lookup_products
     residual_rows = []
     for i in range(shards):
         slot = slot_ref[i : i + 1, :].astype(jnp.int32)
-        owner = slot // capacity
-        place_hot = jnp.where(hot(slot - owner * capacity, capacity), 1.0, 0.0).astype(bf16)
-        found = dot_nn(table, place_hot)
-        found = found[:sources] + (found[sources : 2 * sources] + found[2 * sources :])
-        owner_hot = hot(owner * shards + i, sources)
-        score = jnp.sum(jnp.where(owner_hot, found, 0.0), axis=0, keepdims=True)
+        score = lookup(returned_ref, slot, shards, i)
         margin = fixed_ref[i : i + 1, :] + score
         all_ref[i : i + 1, :] = margin
         residual = (label_ref[i : i + 1, :] - sigmoid(margin)) * (1.0 / dp_count)
         residual_ref[i : i + 1, :] = residual
         residual_rows.append(residual)
     margin_ref[...] = all_ref[pl.ds(lax.axis_index("feat"), 1), :]
-    for copy in copies:
-        copy.wait()
 
     def shard_values(i):
+        if i * rows == kept:
+            copy.wait()
         if i * rows < kept:
             return keep_ref[i * rows : (i + 1) * rows, :]
         return held_ref[i * rows - kept : (i + 1) * rows - kept, :]
@@ -170,10 +194,12 @@
     add_blocks(1, dp_count, shard_values, block_ref, residual_rows, out_ref)
 
 
-def margins_and_theirs(returned, fixed, label, slot, fixed_values, block_row, blocks, dp_count):
+def margins_and_theirs(
+    returned, fixed, label, slot, keep, fixed_values, block_row, blocks, dp_count
+):
     shards, rows = fixed.shape
     group_rows, width = fixed_values.shape
-    kept = rows * (shards // 2)
+    kept = keep.shape[0]
 
     def kernel(*refs):
         margin_kernel(dp_count, *refs)
@@ -181,22 +207,21 @@
     vmem = pl.BlockSpec(memory_space=pltpu.VMEM)
     return pl.pallas_call(
         kernel,
-        in_specs=[vmem] * 4 + [pl.BlockSpec(memory_space=pltpu.HBM), vmem],
-        out_specs=[vmem] * 4,
+        in_specs=[vmem] * 5 + [pl.BlockSpec(memory_space=pltpu.HBM), vmem],
+        out_specs=[vmem] * 3,
         out_shape=(
             jax.ShapeDtypeStruct((1, rows), f32),
             jax.ShapeDtypeStruct((shards, rows), f32),
             jax.ShapeDtypeStruct((blocks // 2, width), f32),
-            jax.ShapeDtypeStruct((kept, width), bf16),
         ),
         scratch_shapes=[
             pltpu.VMEM((shards, rows), f32),
             pltpu.VMEM((group_rows - kept, width), bf16),
-            pltpu.SemaphoreType.DMA((2,)),
+            pltpu.SemaphoreType.DMA,
         ],
         compiler_params=compiler_params(50),
         name="margins_and_theirs",
-    )(returned, fixed, label, slot, fixed_values, block_row)
+    )(returned, fixed, label, slot, keep, fixed_values, block_row)
 
 
 def mine_kernel(
@@ -589,7 +614,7 @@
         member_tiles, tile_source.reshape(1, -1), dp_count, capacity
     )
 
-    own = partial_scores(fixed_values, block_row, fixed_coef, label_row, slot_row)
+    own, keep = partial_scores(fixed_values, block_row, fixed_coef, label_row, slot_row)
     pieces = [own] + [swap(own, "feat", k) for k in range(1, feat_count)]
     fixed, label, slot, message = build_message(
         pieces, label_row, slot_row, dp_count, capacity
@@ -608,8 +633,8 @@
             got_feats, got, member_slots, member_coef, feat_count
         )
     returned = lax.all_to_all(new_scores, ("dp", "feat"), 0, 0, tiled=True)
-    margin, residual, theirs, keep = margins_and_theirs(
-        returned, fixed, label, slot, fixed_values, block_row, blocks, dp_count
+    margin, residual, theirs = margins_and_theirs(
+        returned, fixed, label, slot, keep, fixed_values, block_row, blocks, dp_count
     )
     mine = gradient_mine(
         residual, keep, fixed_values, block_row, blocks, dp_count

time: 84.7 us -> 85.8 us (1.013)
  Pallas kernels: 21.6 us -> 20.1 us
  local copies, waits for them, and re-layouts: 1.23 us -> 2.45 us
  waiting for transfers between devices: 19.6 us -> 20.8 us
  starting transfers between devices: 30.9 us -> 31.8 us
    pallas_call x1, Pallas kernels: 4.64 us -> 3.1 us  [margins_and_theirs(): pl.pallas_call(kernel, in_specs=[vmem] * 5 + [pl.BlockSpec(memory_space=p...]
    unnamed x16 -> x18, local copies, waits for them, and re-layouts: 1 us -> 2.21 us
    ppermute x21, waiting for transfers between devices: 19.6 us -> 20.8 us  [swap(): lax.ppermute(value, axis, [(i, i ^ offset) for i in range(lax.axis_size(a...]
    ppermute x21, starting transfers between devices: 23.6 us -> 24.5 us  [swap(): lax.ppermute(value, axis, [(i, i ^ offset) for i in range(lax.axis_size(a...]
  transfers between devices with their start and end apart: 22 -> 22, of which waited for: 13 -> 12; matrix products, arithmetic and copies ran while one was open for 0% -> 0% of each run, Pallas kernels for 13% -> 13%
where the time goes in v6:
time: 85.8 us; the launch traced here: 85.5 us
  starting transfers between devices  31.8 us (37%)
  waiting for transfers between devices  20.8 us (24%)
  Pallas kernels  20.1 us (23%)
  blocking collectives  9.16 us (11%)
  local copies, waits for them, and re-layouts  2.45 us (3%)
  between operations  0.89 us (1%)
    ppermute x21, starting transfers between devices, swap(): lax.ppermute(value, axis, [(i, i ^ offset) for i in range(lax.axis_size(a...  24.5 us
    ppermute x21, waiting for transfers between devices, swap(): lax.ppermute(value, axis, [(i, i ^ offset) for i in range(lax.axis_size(a...  20.8 us
    all_to_all x1, blocking collectives, body(): returned = lax.all_to_all(new_scores, ('dp', 'feat'), 0, 0, tiled=True)  9.16 us
    all_to_all x1, starting transfers between devices, body(): lax.all_to_all(send_feats.reshape(dp_count, capacity, -1), 'dp', 0, 0, ti...  7.3 us
    pallas_call x1, Pallas kernels, partial_scores(): pl.pallas_call(partial_kernel, in_specs=[pl.BlockSpec(memory_space=pltpu....  6.7 us
    pallas_call x1, Pallas kernels, pack_feats(): pl.pallas_call(pack_kernel, in_specs=[hbm, hbm], out_specs=hbm, out_shape...  3.2 us
    pallas_call x1, Pallas kernels, solve_members(): pl.pallas_call(solve_kernel, out_shape=(jax.ShapeDtypeStruct(member_coef....  3.11 us
    pallas_call x1, Pallas kernels, margins_and_theirs(): pl.pallas_call(kernel, in_specs=[vmem] * 5 + [pl.BlockSpec(memory_space=p...  3.1 us
  transfers between devices with their start and end apart: 22, of which 12 were waited for; matrix products, arithmetic and copies ran while one was open for 0% of the time, Pallas kernels for 13%

profile of v6, /device:TPU:0, one launch (start us, length us, event | category | flops | bytes accessed | tf_op | source)
XLA Modules:
  0.0 85.5 jit_solution(2438510700117682868)
XLA Ops:
  0.7 3.2 %pack_feats.1 = bf16[2048,256]{1,0:T(8,128)(2,1)} custom-call(bf16[1024,256]{1,0:T(8,128)(2,1)} %feats_in_ref.1, s32[1,1024]{1,0:T(1,128)} %bitcast.29), custom_call_target="tpu_custom_call" | custom-call | flops 1073741824 | bytes 1572864 | tf_op jit(solution)/shard_map/pack_feats/pallas_call | solution.py:308
  3.9 7.3 %all-to-all-start = ((bf16[8,256,256]{2,1,0:T(8,128)(2,1)}), bf16[8,256,256]{2,1,0:T(8,128)(2,1)S(1)}, u32[]{:S(2)}, u32[]{:S(2)}) async-start(bf16[8,256,256]{2,1,0:T(8,128)(2,1)} %bitcast.34), calls=%async_computation | async-start | bytes 2097152 | tf_op jit(solution)/shard_map/all_to_all | solution.py:610
  11.2 1.2 %copy-done = f32[512,512]{1,0:T(8,128)S(1)} copy-done((f32[512,512]{1,0:T(8,128)S(1)}, f32[512,512]{1,0:T(8,128)}, u32[]{:S(2)}) %copy-start) | copy-done | bytes 1048600
  12.4 6.7 %partial_scores.1 = (f32[6,1024]{1,0:T(8,128)S(1)}, bf16[2048,512]{1,0:T(8,128)(2,1)S(1)}) custom-call(bf16[4096,512]{1,0:T(8,128)(2,1)} %refs_2_.1, s32[1,4096]{1,0:T(1,128)S(1)} %bitcast.25, f32[512,512]{1,0:T(8,128)S(1)} %copy-done, s32[1,1024]{1,0:T(1,128)S(1)} %bitcast.32, s32[1,1024]{1,0:T(1,128)S(1)} %bitcast.30), custom_call_target="tpu_custom_call" | custom-call | flops 4294967296 | bytes 5242880 | tf_op jit(solution)/shard_map/partial_scores/pallas_call | solution.py:91
  19.2 1.6 %collective-permute-start.1 = (f32[6,1024]{1,0:T(8,128)S(1)}, f32[6,1024]{1,0:T(8,128)S(1)}, u32[]{:S(2)}, u32[]{:S(2)}) collective-permute-start(f32[6,1024]{1,0:T(8,128)S(1)} %get-tuple-element.17.refs_0_), channel_id=1, source_target_pairs={{0,2},{1,3},{2,0},{3,1},{4,6},{5,7},{6,4},{7,5},{8,10},{9,11},{10,... | collective-permute-start | bytes 73736 | tf_op jit(solution)/shard_map/ppermute | solution.py:486
  21.1 2.1 %collective-permute-done.1.refs_2_ = f32[6,1024]{1,0:T(8,128)S(1)} collective-permute-done((f32[6,1024]{1,0:T(8,128)S(1)}, f32[6,1024]{1,0:T(8,128)S(1)}, u32[]{:S(2)}, u32[]{:S(2)}) %collective-permute-start.1) | collective-permute-done | bytes 24608 | tf_op jit(solution)/shard_map/ppermute | solution.py:486
  23.2 1.0 %collective-permute-done.2.refs_3_ = f32[6,1024]{1,0:T(8,128)S(1)} collective-permute-done((f32[6,1024]{1,0:T(8,128)S(1)}, f32[6,1024]{1,0:T(8,128)S(1)}, u32[]{:S(2)}, u32[]{:S(2)}) %collective-permute-start.2) | collective-permute-done | bytes 24608 | tf_op jit(solution)/shard_map/ppermute | solution.py:486
  24.5 2.1 %collective-permute-start.3 = (f32[4,2,256]{2,1,0:T(2,128)S(1)}, f32[4,2,256]{2,1,0:T(2,128)S(1)}, u32[]{:S(2)}, u32[]{:S(2)}) collective-permute-start(f32[4,2,256]{2,1,0:T(2,128)S(1)} %get-tuple-element.40), channel_id=1, source_target_pairs={{0,4},{4,0},{8,12},{12,8},{16,20},{20,16},{24,28},{28,24},{1,5},{5... | collective-permute-start | bytes 24584 | tf_op jit(solution)/shard_map/ppermute | solution.py:486
  26.6 1.7 %collective-permute-done.3 = f32[4,2,256]{2,1,0:T(2,128)S(1)} collective-permute-done((f32[4,2,256]{2,1,0:T(2,128)S(1)}, f32[4,2,256]{2,1,0:T(2,128)S(1)}, u32[]{:S(2)}, u32[]{:S(2)}) %collective-permute-start.3) | collective-permute-done | bytes 8224 | tf_op jit(solution)/shard_map/ppermute | solution.py:486
  28.3 2.1 %collective-permute-start.4 = (f32[2,2,256]{2,1,0:T(2,128)S(1)}, f32[2,2,256]{2,1,0:T(2,128)S(1)}, u32[]{:S(2)}, u32[]{:S(2)}) collective-permute-start(f32[2,2,256]{2,1,0:T(2,128)S(1)} %get-tuple-element.37), channel_id=1, source_target_pairs={{0,8},{4,12},{8,0},{12,4},{16,24},{20,28},{24,16},{28,20},{1,9},{5... | collective-permute-start | bytes 12296 | tf_op jit(solution)/shard_map/ppermute | solution.py:486
  30.4 1.0 %slot_members.1.member_ref = f32[8,256]{1,0:T(8,128)S(1)} custom-call(s32[4]{0:T(128)S(1)} %copy-done.6, s32[1,2432]{1,0:T(1,128)S(1)} %reshape.40.source_ref), custom_call_target="tpu_custom_call" | custom-call | tf_op jit(solution)/shard_map/slot_members/pallas_call | solution.py:385
  31.4 2.3 %collective-permute-start.5 = (f32[2,2,256]{2,1,0:T(2,128)S(1)}, f32[2,2,256]{2,1,0:T(2,128)S(1)}, u32[]{:S(2)}, u32[]{:S(2)}) collective-permute-start(f32[2,2,256]{2,1,0:T(2,128)S(1)} %get-tuple-element.36), channel_id=1, source_target_pairs={{0,16},{4,20},{8,24},{12,28},{16,0},{20,4},{24,8},{28,12},{1,17},{... | collective-permute-start | bytes 12296 | tf_op jit(solution)/shard_map/ppermute | solution.py:486
  33.8 3.3 %collective-permute-done.5 = f32[2,2,256]{2,1,0:T(2,128)S(1)} collective-permute-done((f32[2,2,256]{2,1,0:T(2,128)S(1)}, f32[2,2,256]{2,1,0:T(2,128)S(1)}, u32[]{:S(2)}, u32[]{:S(2)}) %collective-permute-start.5) | collective-permute-done | bytes 4128 | tf_op jit(solution)/shard_map/ppermute | solution.py:486
  37.2 1.9 %collective-permute-done.6 = f32[2,2,256]{2,1,0:T(2,128)S(1)} collective-permute-done((f32[2,2,256]{2,1,0:T(2,128)S(1)}, f32[2,2,256]{2,1,0:T(2,128)S(1)}, u32[]{:S(2)}, u32[]{:S(2)}) %collective-permute-start.6) | collective-permute-done | bytes 4128 | tf_op jit(solution)/shard_map/ppermute | solution.py:486
  39.1 3.1 %solve_members.1 = (f32[4,256]{1,0:T(4,128)}, f32[32,1,256]{2,1,0:T(1,128)S(1)}) custom-call(bf16[2048,256]{1,0:T(8,128)(2,1)S(1)} %bitcast.23, f32[8,2,256]{2,1,0:T(2,128)S(1)} %bitcast.24, f32[8,256]{1,0:T(8,128)S(1)} %slot_members.1.member_ref, f32[4,256]{1,0:T(4,128)S(1)} %copy-done.3), custom_call_target="tpu_custom_call" | custom-call | tf_op jit(solution)/shard_map/solve_members/pallas_call | solution.py:474
  42.3 9.2 %all_to_all.10.refs_0_ = f32[32,1,256]{2,1,0:T(1,128)S(1)} all-to-all(f32[32,1,256]{2,1,0:T(1,128)S(1)} %get-tuple-element.19), channel_id=1, replica_groups=mesh['dp'=8,'feat'=4] {'dp','feat'}, dimensions={0} | all-to-all | bytes 65536 | tf_op jit(solution)/shard_map/all_to_all | solution.py:635
  51.4 3.1 %margins_and_theirs.1 = (f32[1,1024]{1,0:T(1,128)}, f32[4,1024]{1,0:T(4,128)S(1)}, f32[256,512]{1,0:T(8,128)S(1)}) custom-call(f32[32,1,256]{2,1,0:T(1,128)S(1)} %all_to_all.10.refs_0_, f32[4,1024]{1,0:T(4,128)S(1)} %get-tuple-element.20.refs_1_, f32[4,1024]{1,0:T(4,128)S(1)} %get-tuple-element.21.refs_2_, f32[4,1024]{1,0:T(4,128)S(1)} %get-tuple-element.22.refs_3_, ...), custom_call_target="tpu_custom_call" | custom-call | tf_op jit(solution)/shard_map/margins_and_theirs/pallas_call | solution.py:208
  55.3 2.7 %gradient_mine.1 = f32[256,512]{1,0:T(8,128)S(1)} custom-call(f32[4,1024]{1,0:T(4,128)S(1)} %get-tuple-element.26.refs_0_, bf16[2048,512]{1,0:T(8,128)(2,1)S(1)} %get-tuple-element.23.refs_4_.refs_1_, bf16[4096,512]{1,0:T(8,128)(2,1)} %refs_2_.1, s32[1,4096]{1,0:T(1,128)S(1)} %bitcast.27), custom_call_target="tpu_custom_call" | custom-call | flops 2147483648 | bytes 4718592 | tf_op jit(solution)/shard_map/gradient_mine/pallas_call | solution.py:261
  58.0 1.5 %collective-permute-start.8 = (f16[64,512]{1,0:T(8,128)(2,1)S(1)}, f16[64,512]{1,0:T(8,128)(2,1)S(1)}, u32[]{:S(2)}, u32[]{:S(2)}) collective-permute-start(f16[64,512]{1,0:T(8,128)(2,1)S(1)} %get-tuple-element.34), channel_id=1, source_target_pairs={{0,4},{4,0},{8,12},{12,8},{16,20},{20,16},{24,28},{28,24},{1,5},{5... | collective-permute-start | bytes 196616 | tf_op jit(solution)/shard_map/ppermute | solution.py:486
  60.1 1.4 %collective-permute-start.7 = (f16[64,512]{1,0:T(8,128)(2,1)S(1)}, f16[64,512]{1,0:T(8,128)(2,1)S(1)}, u32[]{:S(2)}, u32[]{:S(2)}) collective-permute-start(f16[64,512]{1,0:T(8,128)(2,1)S(1)} %get-tuple-element.31), channel_id=1, source_target_pairs={{0,4},{4,0},{8,12},{12,8},{16,20},{20,16},{24,28},{28,24},{1,5},{5... | collective-permute-start | bytes 196616 | tf_op jit(solution)/shard_map/ppermute | solution.py:486
  61.6 2.9 %collective-permute-done.9 = f16[64,512]{1,0:T(8,128)(2,1)S(1)} collective-permute-done((f16[64,512]{1,0:T(8,128)(2,1)S(1)}, f16[64,512]{1,0:T(8,128)(2,1)S(1)}, u32[]{:S(2)}, u32[]{:S(2)}) %collective-permute-start.9) | collective-permute-done | bytes 65568 | tf_op jit(solution)/shard_map/ppermute | solution.py:486
  64.8 2.3 %collective-permute-start.12 = (f16[64,512]{1,0:T(8,128)(2,1)S(1)}, f16[64,512]{1,0:T(8,128)(2,1)S(1)}, u32[]{:S(2)}, u32[]{:S(2)}) collective-permute-start(f16[64,512]{1,0:T(8,128)(2,1)S(1)} %fusion.1), channel_id=1, source_target_pairs={{0,24},{4,28},{8,16},{12,20},{16,8},{20,12},{24,0},{28,4},{1,25},{... | collective-permute-start | bytes 196616 | tf_op jit(solution)/shard_map/ppermute | solution.py:486
  67.1 1.0 %collective-permute-start.11 = (f16[64,512]{1,0:T(8,128)(2,1)S(1)}, f16[64,512]{1,0:T(8,128)(2,1)S(1)}, u32[]{:S(2)}, u32[]{:S(2)}) collective-permute-start(f16[64,512]{1,0:T(8,128)(2,1)S(1)} %fusion), channel_id=1, source_target_pairs={{0,8},{4,12},{8,0},{12,4},{16,24},{20,28},{24,16},{28,20},{1,9},{5... | collective-permute-start | bytes 196616 | tf_op jit(solution)/shard_map/ppermute | solution.py:486
  68.1 2.9 %collective-permute-done.13 = f16[64,512]{1,0:T(8,128)(2,1)S(1)} collective-permute-done((f16[64,512]{1,0:T(8,128)(2,1)S(1)}, f16[64,512]{1,0:T(8,128)(2,1)S(1)}, u32[]{:S(2)}, u32[]{:S(2)}) %collective-permute-start.13) | collective-permute-done | bytes 65568 | tf_op jit(solution)/shard_map/ppermute | solution.py:486
  72.5 1.8 %collective-permute-start.17 = (f16[64,512]{1,0:T(8,128)(2,1)S(1)}, f16[64,512]{1,0:T(8,128)(2,1)S(1)}, u32[]{:S(2)}, u32[]{:S(2)}) collective-permute-start(f16[64,512]{1,0:T(8,128)(2,1)S(1)} %fusion.6), channel_id=1, source_target_pairs={{0,24},{4,28},{8,16},{12,20},{16,8},{20,12},{24,0},{28,4},{1,25},{... | collective-permute-start | bytes 196616 | tf_op jit(solution)/shard_map/ppermute | solution.py:486
  74.3 1.3 %collective-permute-start.19 = (f16[64,512]{1,0:T(8,128)(2,1)S(1)}, f16[64,512]{1,0:T(8,128)(2,1)S(1)}, u32[]{:S(2)}, u32[]{:S(2)}) collective-permute-start(f16[64,512]{1,0:T(8,128)(2,1)S(1)} %fusion.6), channel_id=1, source_target_pairs={{0,16},{4,20},{8,24},{12,28},{16,0},{20,4},{24,8},{28,12},{1,17},{... | collective-permute-start | bytes 196616 | tf_op jit(solution)/shard_map/ppermute | solution.py:486
  75.6 1.4 %collective-permute-start.14 = (f16[64,512]{1,0:T(8,128)(2,1)S(1)}, f16[64,512]{1,0:T(8,128)(2,1)S(1)}, u32[]{:S(2)}, u32[]{:S(2)}) collective-permute-start(f16[64,512]{1,0:T(8,128)(2,1)S(1)} %fusion.6), channel_id=1, source_target_pairs={{0,4},{4,0},{8,12},{12,8},{16,20},{20,16},{24,28},{28,24},{1,5},{5... | collective-permute-start | bytes 196616 | tf_op jit(solution)/shard_map/ppermute | solution.py:486
  78.5 1.2 %collective-permute-start.18 = (f16[64,512]{1,0:T(8,128)(2,1)S(1)}, f16[64,512]{1,0:T(8,128)(2,1)S(1)}, u32[]{:S(2)}, u32[]{:S(2)}) collective-permute-start(f16[64,512]{1,0:T(8,128)(2,1)S(1)} %collective-permute-done.17), channel_id=1, source_target_pairs={{0,4},{4,0},{8,12},{12,8},{16,20},{20,16},{24,28},{28,24},{1,5},{5... | collective-permute-start | bytes 196616 | tf_op jit(solution)/shard_map/ppermute | solution.py:486
  80.2 1.1 %collective-permute-start.20 = (f16[64,512]{1,0:T(8,128)(2,1)S(1)}, f16[64,512]{1,0:T(8,128)(2,1)S(1)}, u32[]{:S(2)}, u32[]{:S(2)}) collective-permute-start(f16[64,512]{1,0:T(8,128)(2,1)S(1)} %collective-permute-done.19), channel_id=1, source_target_pairs={{0,4},{4,0},{8,12},{12,8},{16,20},{20,16},{24,28},{28,24},{1,5},{5... | collective-permute-start | bytes 196616 | tf_op jit(solution)/shard_map/ppermute | solution.py:486
  81.6 1.2 %collective-permute-done.18 = f16[64,512]{1,0:T(8,128)(2,1)S(1)} collective-permute-done((f16[64,512]{1,0:T(8,128)(2,1)S(1)}, f16[64,512]{1,0:T(8,128)(2,1)S(1)}, u32[]{:S(2)}, u32[]{:S(2)}) %collective-permute-start.18) | collective-permute-done | bytes 65568 | tf_op jit(solution)/shard_map/ppermute | solution.py:486
  82.8 1.6 %collective-permute-done.20 = f16[64,512]{1,0:T(8,128)(2,1)S(1)} collective-permute-done((f16[64,512]{1,0:T(8,128)(2,1)S(1)}, f16[64,512]{1,0:T(8,128)(2,1)S(1)}, u32[]{:S(2)}, u32[]{:S(2)}) %collective-permute-start.20) | collective-permute-done | bytes 65568 | tf_op jit(solution)/shard_map/ppermute | solution.py:486
  84.5 1.0 %copy-done.7 = f32[512,512]{1,0:T(8,128)} copy-done((f32[512,512]{1,0:T(8,128)}, f32[512,512]{1,0:T(8,128)S(1)}, u32[]{:S(2)}) %copy-start.7) | copy-done | bytes 1048600
  (57 shorter events, 6.2 us)
Async XLA Ops:
  0.6 10.5 %copy-start.4 = (s32[1024]{0:T(1024)S(1)}, s32[1024]{0:T(1024)}, u32[]{:S(2)}) copy-start(s32[1024]{0:T(1024)} %param.15) | copy-start | bytes 12292
  0.6 10.5 %copy-start.2 = (s32[4096,1]{0,1:T(1,128)S(1)}, s32[4096,1]{0,1:T(1,128)}, u32[]{:S(2)}) copy-start(s32[4096,1]{0,1:T(1,128)} %param.12) | copy-start | bytes 49156
  0.7 10.5 %copy-start.5 = (s32[1024]{0:T(1024)S(1)}, s32[1024]{0:T(1024)}, u32[]{:S(2)}) copy-start(s32[1024]{0:T(1024)} %param.10) | copy-start | bytes 12292
  3.9 35.3 %all-to-all-start = ((bf16[8,256,256]{2,1,0:T(8,128)(2,1)}), bf16[8,256,256]{2,1,0:T(8,128)(2,1)S(1)}, u32[]{:S(2)}, u32[]{:S(2)}) async-start(bf16[8,256,256]{2,1,0:T(8,128)(2,1)} %bitcast.34), calls=%async_computation | async-start | bytes 2097152 | tf_op jit(solution)/shard_map/all_to_all | solution.py:610
  11.2 1.2 %copy-start = (f32[512,512]{1,0:T(8,128)S(1)}, f32[512,512]{1,0:T(8,128)}, u32[]{:S(2)}) copy-start(f32[512,512]{1,0:T(8,128)} %coef_ref.2) | copy-start | bytes 3145732
  12.4 18.0 %copy-start.8 = (s32[2432]{0:T(1024)S(1)}, s32[2432]{0:T(1024)}, u32[]{:S(2)}) copy-start(s32[2432]{0:T(1024)} %param.16) | copy-start | bytes 29188
  12.4 18.0 %copy-start.6 = (s32[4]{0:T(128)S(1)}, s32[4]{0:T(128)}, u32[]{:S(2)}) copy-start(s32[4]{0:T(128)} %tiles_ref.1) | copy-start | bytes 52
  12.4 26.7 %copy-start.3 = (f32[4,256]{1,0:T(4,128)S(1)}, f32[4,256]{1,0:T(4,128)}, u32[]{:S(2)}) copy-start(f32[4,256]{1,0:T(4,128)} %coef_ref.3) | copy-start | bytes 12292
  19.1 1.9 %collective-permute-start = (f32[6,1024]{1,0:T(8,128)S(1)}, f32[6,1024]{1,0:T(8,128)S(1)}, u32[]{:S(2)}, u32[]{:S(2)}) collective-permute-start(f32[6,1024]{1,0:T(8,128)S(1)} %get-tuple-element.17.refs_0_), channel_id=1, source_target_pairs={{0,1},{1,0},{2,3},{3,2},{4,5},{5,4},{6,7},{7,6},{8,9},{9,8},{10,11... | collective-permute-start | bytes 73736 | tf_op jit(solution)/shard_map/ppermute | solution.py:486
  19.2 4.0 %collective-permute-start.1 = (f32[6,1024]{1,0:T(8,128)S(1)}, f32[6,1024]{1,0:T(8,128)S(1)}, u32[]{:S(2)}, u32[]{:S(2)}) collective-permute-start(f32[6,1024]{1,0:T(8,128)S(1)} %get-tuple-element.17.refs_0_), channel_id=1, source_target_pairs={{0,2},{1,3},{2,0},{3,1},{4,6},{5,7},{6,4},{7,5},{8,10},{9,11},{10,... | collective-permute-start | bytes 73736 | tf_op jit(solution)/shard_map/ppermute | solution.py:486
  20.8 3.4 %collective-permute-start.2 = (f32[6,1024]{1,0:T(8,128)S(1)}, f32[6,1024]{1,0:T(8,128)S(1)}, u32[]{:S(2)}, u32[]{:S(2)}) collective-permute-start(f32[6,1024]{1,0:T(8,128)S(1)} %get-tuple-element.17.refs_0_), channel_id=1, source_target_pairs={{0,3},{1,2},{2,1},{3,0},{4,7},{5,6},{6,5},{7,4},{8,11},{9,10},{10,... | collective-permute-start | bytes 73736 | tf_op jit(solution)/shard_map/ppermute | solution.py:486
  24.5 3.8 %collective-permute-start.3 = (f32[4,2,256]{2,1,0:T(2,128)S(1)}, f32[4,2,256]{2,1,0:T(2,128)S(1)}, u32[]{:S(2)}, u32[]{:S(2)}) collective-permute-start(f32[4,2,256]{2,1,0:T(2,128)S(1)} %get-tuple-element.40), channel_id=1, source_target_pairs={{0,4},{4,0},{8,12},{12,8},{16,20},{20,16},{24,28},{28,24},{1,5},{5... | collective-permute-start | bytes 24584 | tf_op jit(solution)/shard_map/ppermute | solution.py:486
  28.3 5.5 %collective-permute-start.4 = (f32[2,2,256]{2,1,0:T(2,128)S(1)}, f32[2,2,256]{2,1,0:T(2,128)S(1)}, u32[]{:S(2)}, u32[]{:S(2)}) collective-permute-start(f32[2,2,256]{2,1,0:T(2,128)S(1)} %get-tuple-element.37), channel_id=1, source_target_pairs={{0,8},{4,12},{8,0},{12,4},{16,24},{20,28},{24,16},{28,20},{1,9},{5... | collective-permute-start | bytes 12296 | tf_op jit(solution)/shard_map/ppermute | solution.py:486
  31.4 5.8 %collective-permute-start.5 = (f32[2,2,256]{2,1,0:T(2,128)S(1)}, f32[2,2,256]{2,1,0:T(2,128)S(1)}, u32[]{:S(2)}, u32[]{:S(2)}) collective-permute-start(f32[2,2,256]{2,1,0:T(2,128)S(1)} %get-tuple-element.36), channel_id=1, source_target_pairs={{0,16},{4,20},{8,24},{12,28},{16,0},{20,4},{24,8},{28,12},{1,17},{... | collective-permute-start | bytes 12296 | tf_op jit(solution)/shard_map/ppermute | solution.py:486
  33.7 5.4 %collective-permute-start.6 = (f32[2,2,256]{2,1,0:T(2,128)S(1)}, f32[2,2,256]{2,1,0:T(2,128)S(1)}, u32[]{:S(2)}, u32[]{:S(2)}) collective-permute-start(f32[2,2,256]{2,1,0:T(2,128)S(1)} %get-tuple-element.35), channel_id=1, source_target_pairs={{0,24},{4,28},{8,16},{12,20},{16,8},{20,12},{24,0},{28,4},{1,25},{... | collective-permute-start | bytes 12296 | tf_op jit(solution)/shard_map/ppermute | solution.py:486
  54.6 6.9 %collective-permute-start.10 = (f16[64,512]{1,0:T(8,128)(2,1)S(1)}, f16[64,512]{1,0:T(8,128)(2,1)S(1)}, u32[]{:S(2)}, u32[]{:S(2)}) collective-permute-start(f16[64,512]{1,0:T(8,128)(2,1)S(1)} %get-tuple-element.32), channel_id=1, source_target_pairs={{0,4},{4,0},{8,12},{12,8},{16,20},{20,16},{24,28},{28,24},{1,5},{5... | collective-permute-start | bytes 196616 | tf_op jit(solution)/shard_map/ppermute | solution.py:486
  55.3 26.2 %copy-start.1 = (f32[512,512]{1,0:T(8,128)S(1)}, f32[512,512]{1,0:T(8,128)}, u32[]{:S(2)}) copy-start(f32[512,512]{1,0:T(8,128)} %coef_ref.2) | copy-start | bytes 3145732
  58.0 6.5 %collective-permute-start.8 = (f16[64,512]{1,0:T(8,128)(2,1)S(1)}, f16[64,512]{1,0:T(8,128)(2,1)S(1)}, u32[]{:S(2)}, u32[]{:S(2)}) collective-permute-start(f16[64,512]{1,0:T(8,128)(2,1)S(1)} %get-tuple-element.34), channel_id=1, source_target_pairs={{0,4},{4,0},{8,12},{12,8},{16,20},{20,16},{24,28},{28,24},{1,5},{5... | collective-permute-start | bytes 196616 | tf_op jit(solution)/shard_map/ppermute | solution.py:486
  59.5 4.9 %collective-permute-start.9 = (f16[64,512]{1,0:T(8,128)(2,1)S(1)}, f16[64,512]{1,0:T(8,128)(2,1)S(1)}, u32[]{:S(2)}, u32[]{:S(2)}) collective-permute-start(f16[64,512]{1,0:T(8,128)(2,1)S(1)} %get-tuple-element.33), channel_id=1, source_target_pairs={{0,4},{4,0},{8,12},{12,8},{16,20},{20,16},{24,28},{28,24},{1,5},{5... | collective-permute-start | bytes 196616 | tf_op jit(solution)/shard_map/ppermute | solution.py:486
  60.1 8.0 %collective-permute-start.7 = (f16[64,512]{1,0:T(8,128)(2,1)S(1)}, f16[64,512]{1,0:T(8,128)(2,1)S(1)}, u32[]{:S(2)}, u32[]{:S(2)}) collective-permute-start(f16[64,512]{1,0:T(8,128)(2,1)S(1)} %get-tuple-element.31), channel_id=1, source_target_pairs={{0,4},{4,0},{8,12},{12,8},{16,20},{20,16},{24,28},{28,24},{1,5},{5... | collective-permute-start | bytes 196616 | tf_op jit(solution)/shard_map/ppermute | solution.py:486
  64.5 6.5 %collective-permute-start.13 = (f16[64,512]{1,0:T(8,128)(2,1)S(1)}, f16[64,512]{1,0:T(8,128)(2,1)S(1)}, u32[]{:S(2)}, u32[]{:S(2)}) collective-permute-start(f16[64,512]{1,0:T(8,128)(2,1)S(1)} %fusion.2), channel_id=1, source_target_pairs={{0,16},{4,20},{8,24},{12,28},{16,0},{20,4},{24,8},{28,12},{1,17},{... | collective-permute-start | bytes 196616 | tf_op jit(solution)/shard_map/ppermute | solution.py:486
  64.8 6.2 %collective-permute-start.12 = (f16[64,512]{1,0:T(8,128)(2,1)S(1)}, f16[64,512]{1,0:T(8,128)(2,1)S(1)}, u32[]{:S(2)}, u32[]{:S(2)}) collective-permute-start(f16[64,512]{1,0:T(8,128)(2,1)S(1)} %fusion.1), channel_id=1, source_target_pairs={{0,24},{4,28},{8,16},{12,20},{16,8},{20,12},{24,0},{28,4},{1,25},{... | collective-permute-start | bytes 196616 | tf_op jit(solution)/shard_map/ppermute | solution.py:486
  67.1 4.9 %collective-permute-start.11 = (f16[64,512]{1,0:T(8,128)(2,1)S(1)}, f16[64,512]{1,0:T(8,128)(2,1)S(1)}, u32[]{:S(2)}, u32[]{:S(2)}) collective-permute-start(f16[64,512]{1,0:T(8,128)(2,1)S(1)} %fusion), channel_id=1, source_target_pairs={{0,8},{4,12},{8,0},{12,4},{16,24},{20,28},{24,16},{28,20},{1,9},{5... | collective-permute-start | bytes 196616 | tf_op jit(solution)/shard_map/ppermute | solution.py:486
  72.0 5.0 %collective-permute-start.15 = (f16[64,512]{1,0:T(8,128)(2,1)S(1)}, f16[64,512]{1,0:T(8,128)(2,1)S(1)}, u32[]{:S(2)}, u32[]{:S(2)}) collective-permute-start(f16[64,512]{1,0:T(8,128)(2,1)S(1)} %fusion.6), channel_id=1, source_target_pairs={{0,8},{4,12},{8,0},{12,4},{16,24},{20,28},{24,16},{28,20},{1,9},{5... | collective-permute-start | bytes 196616 | tf_op jit(solution)/shard_map/ppermute | solution.py:486
  72.5 6.1 %collective-permute-start.17 = (f16[64,512]{1,0:T(8,128)(2,1)S(1)}, f16[64,512]{1,0:T(8,128)(2,1)S(1)}, u32[]{:S(2)}, u32[]{:S(2)}) collective-permute-start(f16[64,512]{1,0:T(8,128)(2,1)S(1)} %fusion.6), channel_id=1, source_target_pairs={{0,24},{4,28},{8,16},{12,20},{16,8},{20,12},{24,0},{28,4},{1,25},{... | collective-permute-start | bytes 196616 | tf_op jit(solution)/shard_map/ppermute | solution.py:486
  74.3 5.9 %collective-permute-start.19 = (f16[64,512]{1,0:T(8,128)(2,1)S(1)}, f16[64,512]{1,0:T(8,128)(2,1)S(1)}, u32[]{:S(2)}, u32[]{:S(2)}) collective-permute-start(f16[64,512]{1,0:T(8,128)(2,1)S(1)} %fusion.6), channel_id=1, source_target_pairs={{0,16},{4,20},{8,24},{12,28},{16,0},{20,4},{24,8},{28,12},{1,17},{... | collective-permute-start | bytes 196616 | tf_op jit(solution)/shard_map/ppermute | solution.py:486
  75.6 5.8 %collective-permute-start.14 = (f16[64,512]{1,0:T(8,128)(2,1)S(1)}, f16[64,512]{1,0:T(8,128)(2,1)S(1)}, u32[]{:S(2)}, u32[]{:S(2)}) collective-permute-start(f16[64,512]{1,0:T(8,128)(2,1)S(1)} %fusion.6), channel_id=1, source_target_pairs={{0,4},{4,0},{8,12},{12,8},{16,20},{20,16},{24,28},{28,24},{1,5},{5... | collective-permute-start | bytes 196616 | tf_op jit(solution)/shard_map/ppermute | solution.py:486
  77.0 4.5 %collective-permute-start.16 = (f16[64,512]{1,0:T(8,128)(2,1)S(1)}, f16[64,512]{1,0:T(8,128)(2,1)S(1)}, u32[]{:S(2)}, u32[]{:S(2)}) collective-permute-start(f16[64,512]{1,0:T(8,128)(2,1)S(1)} %collective-permute-done.15), channel_id=1, source_target_pairs={{0,4},{4,0},{8,12},{12,8},{16,20},{20,16},{24,28},{28,24},{1,5},{5... | collective-permute-start | bytes 196616 | tf_op jit(solution)/shard_map/ppermute | solution.py:486
  78.5 4.3 %collective-permute-start.18 = (f16[64,512]{1,0:T(8,128)(2,1)S(1)}, f16[64,512]{1,0:T(8,128)(2,1)S(1)}, u32[]{:S(2)}, u32[]{:S(2)}) collective-permute-start(f16[64,512]{1,0:T(8,128)(2,1)S(1)} %collective-permute-done.17), channel_id=1, source_target_pairs={{0,4},{4,0},{8,12},{12,8},{16,20},{20,16},{24,28},{28,24},{1,5},{5... | collective-permute-start | bytes 196616 | tf_op jit(solution)/shard_map/ppermute | solution.py:486
  80.2 4.3 %collective-permute-start.20 = (f16[64,512]{1,0:T(8,128)(2,1)S(1)}, f16[64,512]{1,0:T(8,128)(2,1)S(1)}, u32[]{:S(2)}, u32[]{:S(2)}) collective-permute-start(f16[64,512]{1,0:T(8,128)(2,1)S(1)} %collective-permute-done.19), channel_id=1, source_target_pairs={{0,4},{4,0},{8,12},{12,8},{16,20},{20,16},{24,28},{28,24},{1,5},{5... | collective-permute-start | bytes 196616 | tf_op jit(solution)/shard_map/ppermute | solution.py:486
  84.5 1.0 %copy-start.7 = (f32[512,512]{1,0:T(8,128)}, f32[512,512]{1,0:T(8,128)S(1)}, u32[]{:S(2)}) copy-start(f32[512,512]{1,0:T(8,128)S(1)} %subtract_dynamic-update-slice_fusion) | copy-start | bytes 3145732

commit v7 on v6

--- a/solution.py
+++ b/solution.py
@@ -179,7 +179,7 @@
         score = lookup(returned_ref, slot, shards, i)
         margin = fixed_ref[i : i + 1, :] + score
         all_ref[i : i + 1, :] = margin
-        residual = (label_ref[i : i + 1, :] - sigmoid(margin)) * (1.0 / dp_count)
+        residual = (label_ref[i : i + 1, :] - sigmoid(margin)) * (2.0 / dp_count)
         residual_ref[i : i + 1, :] = residual
         residual_rows.append(residual)
     margin_ref[...] = all_ref[pl.ds(lax.axis_index("feat"), 1), :]
@@ -548,7 +548,7 @@
     def put(out, got, k, parity):
         at = ((place ^ k) * 2 + parity) * rows
         own_coef = lax.dynamic_slice_in_dim(coef, at, rows, 0)
-        grad = ridge_fixed * own_coef - got.astype(f32)
+        grad = ridge_fixed * own_coef - 0.5 * got.astype(f32)
         return lax.dynamic_update_slice_in_dim(out, grad, at, 0)
 
     if half > 4:
@@ -564,9 +564,10 @@
             out = put(out, other[at], k, 1 - side)
         return out
     same = {0: own}
-    for k in (1, 3, 2):
+    order = [k for k in (1, 3, 2) if k < half]
+    for k in order:
         same[k] = swap(own, "dp", 2 * k)
-    for k in (0,) + (1, 3, 2):
+    for k in (0, *order):
         other = swap(same[k], "dp", 1)
         pair = jnp.where(
             side == 0,
@@ -575,7 +576,7 @@
         )
         at = (place ^ k) * 2 * rows
         own_coef = lax.dynamic_slice_in_dim(coef, at, 2 * rows, 0)
-        grad = ridge_fixed * own_coef - pair.astype(f32)
+        grad = ridge_fixed * own_coef - 0.5 * pair.astype(f32)
         out = lax.dynamic_update_slice_in_dim(out, grad, at, 0)
     return out
 

time: 85.8 us -> 85.8 us (level)
  transfers between devices with their start and end apart: 22 -> 22, of which waited for: 12 -> 12; matrix products, arithmetic and copies ran while one was open for 0% -> 1% of each run, Pallas kernels for 13% -> 13%
where the time goes in v7:
time: 85.8 us; the launch traced here: 85.5 us
  starting transfers between devices  31.8 us (37%)
  waiting for transfers between devices  20.7 us (24%)
  Pallas kernels  20.1 us (23%)
  blocking collectives  9.16 us (11%)
  local copies, waits for them, and re-layouts  2.45 us (3%)
  between operations  0.89 us (1%)
    ppermute x21, starting transfers between devices, swap(): lax.ppermute(value, axis, [(i, i ^ offset) for i in range(lax.axis_size(a...  24.5 us
    ppermute x21, waiting for transfers between devices, swap(): lax.ppermute(value, axis, [(i, i ^ offset) for i in range(lax.axis_size(a...  20.7 us
    all_to_all x1, blocking collectives, body(): returned = lax.all_to_all(new_scores, ('dp', 'feat'), 0, 0, tiled=True)  9.16 us
    all_to_all x1, starting transfers between devices, body(): lax.all_to_all(send_feats.reshape(dp_count, capacity, -1), 'dp', 0, 0, ti...  7.3 us
    pallas_call x1, Pallas kernels, partial_scores(): pl.pallas_call(partial_kernel, in_specs=[pl.BlockSpec(memory_space=pltpu....  6.7 us
    pallas_call x1, Pallas kernels, pack_feats(): pl.pallas_call(pack_kernel, in_specs=[hbm, hbm], out_specs=hbm, out_shape...  3.2 us
    pallas_call x1, Pallas kernels, solve_members(): pl.pallas_call(solve_kernel, out_shape=(jax.ShapeDtypeStruct(member_coef....  3.11 us
    pallas_call x1, Pallas kernels, margins_and_theirs(): pl.pallas_call(kernel, in_specs=[vmem] * 5 + [pl.BlockSpec(memory_space=p...  3.1 us
  transfers between devices with their start and end apart: 22, of which 12 were waited for; matrix products, arithmetic and copies ran while one was open for 1% of the time, Pallas kernels for 13%

profile of v7, /device:TPU:0, one launch (start us, length us, event | category | flops | bytes accessed | tf_op | source)
XLA Modules:
  0.0 85.5 jit_solution(50791598121478608)
XLA Ops:
  0.7 3.2 %pack_feats.1 = bf16[2048,256]{1,0:T(8,128)(2,1)} custom-call(bf16[1024,256]{1,0:T(8,128)(2,1)} %feats_in_ref.1, s32[1,1024]{1,0:T(1,128)} %bitcast.29), custom_call_target="tpu_custom_call" | custom-call | flops 1073741824 | bytes 1572864 | tf_op jit(solution)/shard_map/pack_feats/pallas_call | solution.py:308
  3.9 7.3 %all-to-all-start = ((bf16[8,256,256]{2,1,0:T(8,128)(2,1)}), bf16[8,256,256]{2,1,0:T(8,128)(2,1)S(1)}, u32[]{:S(2)}, u32[]{:S(2)}) async-start(bf16[8,256,256]{2,1,0:T(8,128)(2,1)} %bitcast.34), calls=%async_computation | async-start | bytes 2097152 | tf_op jit(solution)/shard_map/all_to_all | solution.py:611
  11.2 1.2 %copy-done = f32[512,512]{1,0:T(8,128)S(1)} copy-done((f32[512,512]{1,0:T(8,128)S(1)}, f32[512,512]{1,0:T(8,128)}, u32[]{:S(2)}) %copy-start) | copy-done | bytes 1048600
  12.4 6.7 %partial_scores.1 = (f32[6,1024]{1,0:T(8,128)S(1)}, bf16[2048,512]{1,0:T(8,128)(2,1)S(1)}) custom-call(bf16[4096,512]{1,0:T(8,128)(2,1)} %refs_2_.1, s32[1,4096]{1,0:T(1,128)S(1)} %bitcast.25, f32[512,512]{1,0:T(8,128)S(1)} %copy-done, s32[1,1024]{1,0:T(1,128)S(1)} %bitcast.32, s32[1,1024]{1,0:T(1,128)S(1)} %bitcast.30), custom_call_target="tpu_custom_call" | custom-call | flops 4294967296 | bytes 5242880 | tf_op jit(solution)/shard_map/partial_scores/pallas_call | solution.py:91
  19.2 1.6 %collective-permute-start.1 = (f32[6,1024]{1,0:T(8,128)S(1)}, f32[6,1024]{1,0:T(8,128)S(1)}, u32[]{:S(2)}, u32[]{:S(2)}) collective-permute-start(f32[6,1024]{1,0:T(8,128)S(1)} %get-tuple-element.17.refs_0_), channel_id=1, source_target_pairs={{0,2},{1,3},{2,0},{3,1},{4,6},{5,7},{6,4},{7,5},{8,10},{9,11},{10,... | collective-permute-start | bytes 73736 | tf_op jit(solution)/shard_map/ppermute | solution.py:486
  21.1 2.1 %collective-permute-done.1.refs_2_ = f32[6,1024]{1,0:T(8,128)S(1)} collective-permute-done((f32[6,1024]{1,0:T(8,128)S(1)}, f32[6,1024]{1,0:T(8,128)S(1)}, u32[]{:S(2)}, u32[]{:S(2)}) %collective-permute-start.1) | collective-permute-done | bytes 24608 | tf_op jit(solution)/shard_map/ppermute | solution.py:486
  23.2 1.0 %collective-permute-done.2.refs_3_ = f32[6,1024]{1,0:T(8,128)S(1)} collective-permute-done((f32[6,1024]{1,0:T(8,128)S(1)}, f32[6,1024]{1,0:T(8,128)S(1)}, u32[]{:S(2)}, u32[]{:S(2)}) %collective-permute-start.2) | collective-permute-done | bytes 24608 | tf_op jit(solution)/shard_map/ppermute | solution.py:486
  24.5 2.1 %collective-permute-start.3 = (f32[4,2,256]{2,1,0:T(2,128)S(1)}, f32[4,2,256]{2,1,0:T(2,128)S(1)}, u32[]{:S(2)}, u32[]{:S(2)}) collective-permute-start(f32[4,2,256]{2,1,0:T(2,128)S(1)} %get-tuple-element.40), channel_id=1, source_target_pairs={{0,4},{4,0},{8,12},{12,8},{16,20},{20,16},{24,28},{28,24},{1,5},{5... | collective-permute-start | bytes 24584 | tf_op jit(solution)/shard_map/ppermute | solution.py:486
  26.6 1.7 %collective-permute-done.3 = f32[4,2,256]{2,1,0:T(2,128)S(1)} collective-permute-done((f32[4,2,256]{2,1,0:T(2,128)S(1)}, f32[4,2,256]{2,1,0:T(2,128)S(1)}, u32[]{:S(2)}, u32[]{:S(2)}) %collective-permute-start.3) | collective-permute-done | bytes 8224 | tf_op jit(solution)/shard_map/ppermute | solution.py:486
  28.3 2.1 %collective-permute-start.4 = (f32[2,2,256]{2,1,0:T(2,128)S(1)}, f32[2,2,256]{2,1,0:T(2,128)S(1)}, u32[]{:S(2)}, u32[]{:S(2)}) collective-permute-start(f32[2,2,256]{2,1,0:T(2,128)S(1)} %get-tuple-element.37), channel_id=1, source_target_pairs={{0,8},{4,12},{8,0},{12,4},{16,24},{20,28},{24,16},{28,20},{1,9},{5... | collective-permute-start | bytes 12296 | tf_op jit(solution)/shard_map/ppermute | solution.py:486
  30.4 1.0 %slot_members.1.member_ref = f32[8,256]{1,0:T(8,128)S(1)} custom-call(s32[4]{0:T(128)S(1)} %copy-done.6, s32[1,2432]{1,0:T(1,128)S(1)} %reshape.40.source_ref), custom_call_target="tpu_custom_call" | custom-call | tf_op jit(solution)/shard_map/slot_members/pallas_call | solution.py:385
  31.4 2.3 %collective-permute-start.5 = (f32[2,2,256]{2,1,0:T(2,128)S(1)}, f32[2,2,256]{2,1,0:T(2,128)S(1)}, u32[]{:S(2)}, u32[]{:S(2)}) collective-permute-start(f32[2,2,256]{2,1,0:T(2,128)S(1)} %get-tuple-element.36), channel_id=1, source_target_pairs={{0,16},{4,20},{8,24},{12,28},{16,0},{20,4},{24,8},{28,12},{1,17},{... | collective-permute-start | bytes 12296 | tf_op jit(solution)/shard_map/ppermute | solution.py:486
  33.8 3.3 %collective-permute-done.5 = f32[2,2,256]{2,1,0:T(2,128)S(1)} collective-permute-done((f32[2,2,256]{2,1,0:T(2,128)S(1)}, f32[2,2,256]{2,1,0:T(2,128)S(1)}, u32[]{:S(2)}, u32[]{:S(2)}) %collective-permute-start.5) | collective-permute-done | bytes 4128 | tf_op jit(solution)/shard_map/ppermute | solution.py:486
  37.2 1.9 %collective-permute-done.6 = f32[2,2,256]{2,1,0:T(2,128)S(1)} collective-permute-done((f32[2,2,256]{2,1,0:T(2,128)S(1)}, f32[2,2,256]{2,1,0:T(2,128)S(1)}, u32[]{:S(2)}, u32[]{:S(2)}) %collective-permute-start.6) | collective-permute-done | bytes 4128 | tf_op jit(solution)/shard_map/ppermute | solution.py:486
  39.1 3.1 %solve_members.1 = (f32[4,256]{1,0:T(4,128)}, f32[32,1,256]{2,1,0:T(1,128)S(1)}) custom-call(bf16[2048,256]{1,0:T(8,128)(2,1)S(1)} %bitcast.23, f32[8,2,256]{2,1,0:T(2,128)S(1)} %bitcast.24, f32[8,256]{1,0:T(8,128)S(1)} %slot_members.1.member_ref, f32[4,256]{1,0:T(4,128)S(1)} %copy-done.3), custom_call_target="tpu_custom_call" | custom-call | tf_op jit(solution)/shard_map/solve_members/pallas_call | solution.py:474
  42.3 9.2 %all_to_all.10.refs_0_ = f32[32,1,256]{2,1,0:T(1,128)S(1)} all-to-all(f32[32,1,256]{2,1,0:T(1,128)S(1)} %get-tuple-element.19), channel_id=1, replica_groups=mesh['dp'=8,'feat'=4] {'dp','feat'}, dimensions={0} | all-to-all | bytes 65536 | tf_op jit(solution)/shard_map/all_to_all | solution.py:636
  51.4 3.1 %margins_and_theirs.1 = (f32[1,1024]{1,0:T(1,128)}, f32[4,1024]{1,0:T(4,128)S(1)}, f32[256,512]{1,0:T(8,128)S(1)}) custom-call(f32[32,1,256]{2,1,0:T(1,128)S(1)} %all_to_all.10.refs_0_, f32[4,1024]{1,0:T(4,128)S(1)} %get-tuple-element.20.refs_1_, f32[4,1024]{1,0:T(4,128)S(1)} %get-tuple-element.21.refs_2_, f32[4,1024]{1,0:T(4,128)S(1)} %get-tuple-element.22.refs_3_, ...), custom_call_target="tpu_custom_call" | custom-call | tf_op jit(solution)/shard_map/margins_and_theirs/pallas_call | solution.py:208
  55.3 2.7 %gradient_mine.1 = f32[256,512]{1,0:T(8,128)S(1)} custom-call(f32[4,1024]{1,0:T(4,128)S(1)} %get-tuple-element.26.refs_0_, bf16[2048,512]{1,0:T(8,128)(2,1)S(1)} %get-tuple-element.23.refs_4_.refs_1_, bf16[4096,512]{1,0:T(8,128)(2,1)} %refs_2_.1, s32[1,4096]{1,0:T(1,128)S(1)} %bitcast.27), custom_call_target="tpu_custom_call" | custom-call | flops 2147483648 | bytes 4718592 | tf_op jit(solution)/shard_map/gradient_mine/pallas_call | solution.py:261
  58.0 1.5 %collective-permute-start.8 = (f16[64,512]{1,0:T(8,128)(2,1)S(1)}, f16[64,512]{1,0:T(8,128)(2,1)S(1)}, u32[]{:S(2)}, u32[]{:S(2)}) collective-permute-start(f16[64,512]{1,0:T(8,128)(2,1)S(1)} %get-tuple-element.34), channel_id=1, source_target_pairs={{0,4},{4,0},{8,12},{12,8},{16,20},{20,16},{24,28},{28,24},{1,5},{5... | collective-permute-start | bytes 196616 | tf_op jit(solution)/shard_map/ppermute | solution.py:486
  60.1 1.4 %collective-permute-start.7 = (f16[64,512]{1,0:T(8,128)(2,1)S(1)}, f16[64,512]{1,0:T(8,128)(2,1)S(1)}, u32[]{:S(2)}, u32[]{:S(2)}) collective-permute-start(f16[64,512]{1,0:T(8,128)(2,1)S(1)} %get-tuple-element.31), channel_id=1, source_target_pairs={{0,4},{4,0},{8,12},{12,8},{16,20},{20,16},{24,28},{28,24},{1,5},{5... | collective-permute-start | bytes 196616 | tf_op jit(solution)/shard_map/ppermute | solution.py:486
  61.6 2.9 %collective-permute-done.9 = f16[64,512]{1,0:T(8,128)(2,1)S(1)} collective-permute-done((f16[64,512]{1,0:T(8,128)(2,1)S(1)}, f16[64,512]{1,0:T(8,128)(2,1)S(1)}, u32[]{:S(2)}, u32[]{:S(2)}) %collective-permute-start.9) | collective-permute-done | bytes 65568 | tf_op jit(solution)/shard_map/ppermute | solution.py:486
  64.8 2.3 %collective-permute-start.12 = (f16[64,512]{1,0:T(8,128)(2,1)S(1)}, f16[64,512]{1,0:T(8,128)(2,1)S(1)}, u32[]{:S(2)}, u32[]{:S(2)}) collective-permute-start(f16[64,512]{1,0:T(8,128)(2,1)S(1)} %fusion.1), channel_id=1, source_target_pairs={{0,24},{4,28},{8,16},{12,20},{16,8},{20,12},{24,0},{28,4},{1,25},{... | collective-permute-start | bytes 196616 | tf_op jit(solution)/shard_map/ppermute | solution.py:486
  67.1 1.0 %collective-permute-start.11 = (f16[64,512]{1,0:T(8,128)(2,1)S(1)}, f16[64,512]{1,0:T(8,128)(2,1)S(1)}, u32[]{:S(2)}, u32[]{:S(2)}) collective-permute-start(f16[64,512]{1,0:T(8,128)(2,1)S(1)} %fusion), channel_id=1, source_target_pairs={{0,8},{4,12},{8,0},{12,4},{16,24},{20,28},{24,16},{28,20},{1,9},{5... | collective-permute-start | bytes 196616 | tf_op jit(solution)/shard_map/ppermute | solution.py:486
  68.1 2.9 %collective-permute-done.13 = f16[64,512]{1,0:T(8,128)(2,1)S(1)} collective-permute-done((f16[64,512]{1,0:T(8,128)(2,1)S(1)}, f16[64,512]{1,0:T(8,128)(2,1)S(1)}, u32[]{:S(2)}, u32[]{:S(2)}) %collective-permute-start.13) | collective-permute-done | bytes 65568 | tf_op jit(solution)/shard_map/ppermute | solution.py:486
  72.5 1.8 %collective-permute-start.17 = (f16[64,512]{1,0:T(8,128)(2,1)S(1)}, f16[64,512]{1,0:T(8,128)(2,1)S(1)}, u32[]{:S(2)}, u32[]{:S(2)}) collective-permute-start(f16[64,512]{1,0:T(8,128)(2,1)S(1)} %fusion.6), channel_id=1, source_target_pairs={{0,24},{4,28},{8,16},{12,20},{16,8},{20,12},{24,0},{28,4},{1,25},{... | collective-permute-start | bytes 196616 | tf_op jit(solution)/shard_map/ppermute | solution.py:486
  74.3 1.3 %collective-permute-start.19 = (f16[64,512]{1,0:T(8,128)(2,1)S(1)}, f16[64,512]{1,0:T(8,128)(2,1)S(1)}, u32[]{:S(2)}, u32[]{:S(2)}) collective-permute-start(f16[64,512]{1,0:T(8,128)(2,1)S(1)} %fusion.6), channel_id=1, source_target_pairs={{0,16},{4,20},{8,24},{12,28},{16,0},{20,4},{24,8},{28,12},{1,17},{... | collective-permute-start | bytes 196616 | tf_op jit(solution)/shard_map/ppermute | solution.py:486
  75.6 1.4 %collective-permute-start.14 = (f16[64,512]{1,0:T(8,128)(2,1)S(1)}, f16[64,512]{1,0:T(8,128)(2,1)S(1)}, u32[]{:S(2)}, u32[]{:S(2)}) collective-permute-start(f16[64,512]{1,0:T(8,128)(2,1)S(1)} %fusion.6), channel_id=1, source_target_pairs={{0,4},{4,0},{8,12},{12,8},{16,20},{20,16},{24,28},{28,24},{1,5},{5... | collective-permute-start | bytes 196616 | tf_op jit(solution)/shard_map/ppermute | solution.py:486
  78.5 1.2 %collective-permute-start.18 = (f16[64,512]{1,0:T(8,128)(2,1)S(1)}, f16[64,512]{1,0:T(8,128)(2,1)S(1)}, u32[]{:S(2)}, u32[]{:S(2)}) collective-permute-start(f16[64,512]{1,0:T(8,128)(2,1)S(1)} %collective-permute-done.17), channel_id=1, source_target_pairs={{0,4},{4,0},{8,12},{12,8},{16,20},{20,16},{24,28},{28,24},{1,5},{5... | collective-permute-start | bytes 196616 | tf_op jit(solution)/shard_map/ppermute | solution.py:486
  80.2 1.1 %collective-permute-start.20 = (f16[64,512]{1,0:T(8,128)(2,1)S(1)}, f16[64,512]{1,0:T(8,128)(2,1)S(1)}, u32[]{:S(2)}, u32[]{:S(2)}) collective-permute-start(f16[64,512]{1,0:T(8,128)(2,1)S(1)} %collective-permute-done.19), channel_id=1, source_target_pairs={{0,4},{4,0},{8,12},{12,8},{16,20},{20,16},{24,28},{28,24},{1,5},{5... | collective-permute-start | bytes 196616 | tf_op jit(solution)/shard_map/ppermute | solution.py:486
  81.6 1.2 %collective-permute-done.18 = f16[64,512]{1,0:T(8,128)(2,1)S(1)} collective-permute-done((f16[64,512]{1,0:T(8,128)(2,1)S(1)}, f16[64,512]{1,0:T(8,128)(2,1)S(1)}, u32[]{:S(2)}, u32[]{:S(2)}) %collective-permute-start.18) | collective-permute-done | bytes 65568 | tf_op jit(solution)/shard_map/ppermute | solution.py:486
  82.8 1.6 %collective-permute-done.20 = f16[64,512]{1,0:T(8,128)(2,1)S(1)} collective-permute-done((f16[64,512]{1,0:T(8,128)(2,1)S(1)}, f16[64,512]{1,0:T(8,128)(2,1)S(1)}, u32[]{:S(2)}, u32[]{:S(2)}) %collective-permute-start.20) | collective-permute-done | bytes 65568 | tf_op jit(solution)/shard_map/ppermute | solution.py:486
  84.5 1.0 %copy-done.7 = f32[512,512]{1,0:T(8,128)} copy-done((f32[512,512]{1,0:T(8,128)}, f32[512,512]{1,0:T(8,128)S(1)}, u32[]{:S(2)}) %copy-start.7) | copy-done | bytes 1048600
  (57 shorter events, 6.3 us)
Async XLA Ops:
  0.6 10.5 %copy-start.4 = (s32[1024]{0:T(1024)S(1)}, s32[1024]{0:T(1024)}, u32[]{:S(2)}) copy-start(s32[1024]{0:T(1024)} %param.15) | copy-start | bytes 12292
  0.6 10.5 %copy-start.2 = (s32[4096,1]{0,1:T(1,128)S(1)}, s32[4096,1]{0,1:T(1,128)}, u32[]{:S(2)}) copy-start(s32[4096,1]{0,1:T(1,128)} %param.12) | copy-start | bytes 49156
  0.7 10.5 %copy-start.5 = (s32[1024]{0:T(1024)S(1)}, s32[1024]{0:T(1024)}, u32[]{:S(2)}) copy-start(s32[1024]{0:T(1024)} %param.10) | copy-start | bytes 12292
  3.9 35.3 %all-to-all-start = ((bf16[8,256,256]{2,1,0:T(8,128)(2,1)}), bf16[8,256,256]{2,1,0:T(8,128)(2,1)S(1)}, u32[]{:S(2)}, u32[]{:S(2)}) async-start(bf16[8,256,256]{2,1,0:T(8,128)(2,1)} %bitcast.34), calls=%async_computation | async-start | bytes 2097152 | tf_op jit(solution)/shard_map/all_to_all | solution.py:611
  11.2 1.2 %copy-start = (f32[512,512]{1,0:T(8,128)S(1)}, f32[512,512]{1,0:T(8,128)}, u32[]{:S(2)}) copy-start(f32[512,512]{1,0:T(8,128)} %coef_ref.2) | copy-start | bytes 3145732
  12.4 18.0 %copy-start.8 = (s32[2432]{0:T(1024)S(1)}, s32[2432]{0:T(1024)}, u32[]{:S(2)}) copy-start(s32[2432]{0:T(1024)} %param.16) | copy-start | bytes 29188
  12.4 18.0 %copy-start.6 = (s32[4]{0:T(128)S(1)}, s32[4]{0:T(128)}, u32[]{:S(2)}) copy-start(s32[4]{0:T(128)} %tiles_ref.1) | copy-start | bytes 52
  12.4 26.7 %copy-start.3 = (f32[4,256]{1,0:T(4,128)S(1)}, f32[4,256]{1,0:T(4,128)}, u32[]{:S(2)}) copy-start(f32[4,256]{1,0:T(4,128)} %coef_ref.3) | copy-start | bytes 12292
  19.1 1.9 %collective-permute-start = (f32[6,1024]{1,0:T(8,128)S(1)}, f32[6,1024]{1,0:T(8,128)S(1)}, u32[]{:S(2)}, u32[]{:S(2)}) collective-permute-start(f32[6,1024]{1,0:T(8,128)S(1)} %get-tuple-element.17.refs_0_), channel_id=1, source_target_pairs={{0,1},{1,0},{2,3},{3,2},{4,5},{5,4},{6,7},{7,6},{8,9},{9,8},{10,11... | collective-permute-start | bytes 73736 | tf_op jit(solution)/shard_map/ppermute | solution.py:486
  19.2 4.0 %collective-permute-start.1 = (f32[6,1024]{1,0:T(8,128)S(1)}, f32[6,1024]{1,0:T(8,128)S(1)}, u32[]{:S(2)}, u32[]{:S(2)}) collective-permute-start(f32[6,1024]{1,0:T(8,128)S(1)} %get-tuple-element.17.refs_0_), channel_id=1, source_target_pairs={{0,2},{1,3},{2,0},{3,1},{4,6},{5,7},{6,4},{7,5},{8,10},{9,11},{10,... | collective-permute-start | bytes 73736 | tf_op jit(solution)/shard_map/ppermute | solution.py:486
  20.8 3.4 %collective-permute-start.2 = (f32[6,1024]{1,0:T(8,128)S(1)}, f32[6,1024]{1,0:T(8,128)S(1)}, u32[]{:S(2)}, u32[]{:S(2)}) collective-permute-start(f32[6,1024]{1,0:T(8,128)S(1)} %get-tuple-element.17.refs_0_), channel_id=1, source_target_pairs={{0,3},{1,2},{2,1},{3,0},{4,7},{5,6},{6,5},{7,4},{8,11},{9,10},{10,... | collective-permute-start | bytes 73736 | tf_op jit(solution)/shard_map/ppermute | solution.py:486
  24.5 3.8 %collective-permute-start.3 = (f32[4,2,256]{2,1,0:T(2,128)S(1)}, f32[4,2,256]{2,1,0:T(2,128)S(1)}, u32[]{:S(2)}, u32[]{:S(2)}) collective-permute-start(f32[4,2,256]{2,1,0:T(2,128)S(1)} %get-tuple-element.40), channel_id=1, source_target_pairs={{0,4},{4,0},{8,12},{12,8},{16,20},{20,16},{24,28},{28,24},{1,5},{5... | collective-permute-start | bytes 24584 | tf_op jit(solution)/shard_map/ppermute | solution.py:486
  28.3 5.5 %collective-permute-start.4 = (f32[2,2,256]{2,1,0:T(2,128)S(1)}, f32[2,2,256]{2,1,0:T(2,128)S(1)}, u32[]{:S(2)}, u32[]{:S(2)}) collective-permute-start(f32[2,2,256]{2,1,0:T(2,128)S(1)} %get-tuple-element.37), channel_id=1, source_target_pairs={{0,8},{4,12},{8,0},{12,4},{16,24},{20,28},{24,16},{28,20},{1,9},{5... | collective-permute-start | bytes 12296 | tf_op jit(solution)/shard_map/ppermute | solution.py:486
  31.4 5.8 %collective-permute-start.5 = (f32[2,2,256]{2,1,0:T(2,128)S(1)}, f32[2,2,256]{2,1,0:T(2,128)S(1)}, u32[]{:S(2)}, u32[]{:S(2)}) collective-permute-start(f32[2,2,256]{2,1,0:T(2,128)S(1)} %get-tuple-element.36), channel_id=1, source_target_pairs={{0,16},{4,20},{8,24},{12,28},{16,0},{20,4},{24,8},{28,12},{1,17},{... | collective-permute-start | bytes 12296 | tf_op jit(solution)/shard_map/ppermute | solution.py:486
  33.7 5.4 %collective-permute-start.6 = (f32[2,2,256]{2,1,0:T(2,128)S(1)}, f32[2,2,256]{2,1,0:T(2,128)S(1)}, u32[]{:S(2)}, u32[]{:S(2)}) collective-permute-start(f32[2,2,256]{2,1,0:T(2,128)S(1)} %get-tuple-element.35), channel_id=1, source_target_pairs={{0,24},{4,28},{8,16},{12,20},{16,8},{20,12},{24,0},{28,4},{1,25},{... | collective-permute-start | bytes 12296 | tf_op jit(solution)/shard_map/ppermute | solution.py:486
  54.6 6.9 %collective-permute-start.10 = (f16[64,512]{1,0:T(8,128)(2,1)S(1)}, f16[64,512]{1,0:T(8,128)(2,1)S(1)}, u32[]{:S(2)}, u32[]{:S(2)}) collective-permute-start(f16[64,512]{1,0:T(8,128)(2,1)S(1)} %get-tuple-element.32), channel_id=1, source_target_pairs={{0,4},{4,0},{8,12},{12,8},{16,20},{20,16},{24,28},{28,24},{1,5},{5... | collective-permute-start | bytes 196616 | tf_op jit(solution)/shard_map/ppermute | solution.py:486
  55.3 26.2 %copy-start.1 = (f32[512,512]{1,0:T(8,128)S(1)}, f32[512,512]{1,0:T(8,128)}, u32[]{:S(2)}) copy-start(f32[512,512]{1,0:T(8,128)} %coef_ref.2) | copy-start | bytes 3145732
  58.0 6.5 %collective-permute-start.8 = (f16[64,512]{1,0:T(8,128)(2,1)S(1)}, f16[64,512]{1,0:T(8,128)(2,1)S(1)}, u32[]{:S(2)}, u32[]{:S(2)}) collective-permute-start(f16[64,512]{1,0:T(8,128)(2,1)S(1)} %get-tuple-element.34), channel_id=1, source_target_pairs={{0,4},{4,0},{8,12},{12,8},{16,20},{20,16},{24,28},{28,24},{1,5},{5... | collective-permute-start | bytes 196616 | tf_op jit(solution)/shard_map/ppermute | solution.py:486
  59.5 4.9 %collective-permute-start.9 = (f16[64,512]{1,0:T(8,128)(2,1)S(1)}, f16[64,512]{1,0:T(8,128)(2,1)S(1)}, u32[]{:S(2)}, u32[]{:S(2)}) collective-permute-start(f16[64,512]{1,0:T(8,128)(2,1)S(1)} %get-tuple-element.33), channel_id=1, source_target_pairs={{0,4},{4,0},{8,12},{12,8},{16,20},{20,16},{24,28},{28,24},{1,5},{5... | collective-permute-start | bytes 196616 | tf_op jit(solution)/shard_map/ppermute | solution.py:486
  60.1 8.0 %collective-permute-start.7 = (f16[64,512]{1,0:T(8,128)(2,1)S(1)}, f16[64,512]{1,0:T(8,128)(2,1)S(1)}, u32[]{:S(2)}, u32[]{:S(2)}) collective-permute-start(f16[64,512]{1,0:T(8,128)(2,1)S(1)} %get-tuple-element.31), channel_id=1, source_target_pairs={{0,4},{4,0},{8,12},{12,8},{16,20},{20,16},{24,28},{28,24},{1,5},{5... | collective-permute-start | bytes 196616 | tf_op jit(solution)/shard_map/ppermute | solution.py:486
  64.5 6.5 %collective-permute-start.13 = (f16[64,512]{1,0:T(8,128)(2,1)S(1)}, f16[64,512]{1,0:T(8,128)(2,1)S(1)}, u32[]{:S(2)}, u32[]{:S(2)}) collective-permute-start(f16[64,512]{1,0:T(8,128)(2,1)S(1)} %fusion.2), channel_id=1, source_target_pairs={{0,16},{4,20},{8,24},{12,28},{16,0},{20,4},{24,8},{28,12},{1,17},{... | collective-permute-start | bytes 196616 | tf_op jit(solution)/shard_map/ppermute | solution.py:486
  64.8 6.2 %collective-permute-start.12 = (f16[64,512]{1,0:T(8,128)(2,1)S(1)}, f16[64,512]{1,0:T(8,128)(2,1)S(1)}, u32[]{:S(2)}, u32[]{:S(2)}) collective-permute-start(f16[64,512]{1,0:T(8,128)(2,1)S(1)} %fusion.1), channel_id=1, source_target_pairs={{0,24},{4,28},{8,16},{12,20},{16,8},{20,12},{24,0},{28,4},{1,25},{... | collective-permute-start | bytes 196616 | tf_op jit(solution)/shard_map/ppermute | solution.py:486
  67.1 4.9 %collective-permute-start.11 = (f16[64,512]{1,0:T(8,128)(2,1)S(1)}, f16[64,512]{1,0:T(8,128)(2,1)S(1)}, u32[]{:S(2)}, u32[]{:S(2)}) collective-permute-start(f16[64,512]{1,0:T(8,128)(2,1)S(1)} %fusion), channel_id=1, source_target_pairs={{0,8},{4,12},{8,0},{12,4},{16,24},{20,28},{24,16},{28,20},{1,9},{5... | collective-permute-start | bytes 196616 | tf_op jit(solution)/shard_map/ppermute | solution.py:486
  72.0 5.0 %collective-permute-start.15 = (f16[64,512]{1,0:T(8,128)(2,1)S(1)}, f16[64,512]{1,0:T(8,128)(2,1)S(1)}, u32[]{:S(2)}, u32[]{:S(2)}) collective-permute-start(f16[64,512]{1,0:T(8,128)(2,1)S(1)} %fusion.6), channel_id=1, source_target_pairs={{0,8},{4,12},{8,0},{12,4},{16,24},{20,28},{24,16},{28,20},{1,9},{5... | collective-permute-start | bytes 196616 | tf_op jit(solution)/shard_map/ppermute | solution.py:486
  72.5 6.1 %collective-permute-start.17 = (f16[64,512]{1,0:T(8,128)(2,1)S(1)}, f16[64,512]{1,0:T(8,128)(2,1)S(1)}, u32[]{:S(2)}, u32[]{:S(2)}) collective-permute-start(f16[64,512]{1,0:T(8,128)(2,1)S(1)} %fusion.6), channel_id=1, source_target_pairs={{0,24},{4,28},{8,16},{12,20},{16,8},{20,12},{24,0},{28,4},{1,25},{... | collective-permute-start | bytes 196616 | tf_op jit(solution)/shard_map/ppermute | solution.py:486
  74.3 5.9 %collective-permute-start.19 = (f16[64,512]{1,0:T(8,128)(2,1)S(1)}, f16[64,512]{1,0:T(8,128)(2,1)S(1)}, u32[]{:S(2)}, u32[]{:S(2)}) collective-permute-start(f16[64,512]{1,0:T(8,128)(2,1)S(1)} %fusion.6), channel_id=1, source_target_pairs={{0,16},{4,20},{8,24},{12,28},{16,0},{20,4},{24,8},{28,12},{1,17},{... | collective-permute-start | bytes 196616 | tf_op jit(solution)/shard_map/ppermute | solution.py:486
  75.6 5.8 %collective-permute-start.14 = (f16[64,512]{1,0:T(8,128)(2,1)S(1)}, f16[64,512]{1,0:T(8,128)(2,1)S(1)}, u32[]{:S(2)}, u32[]{:S(2)}) collective-permute-start(f16[64,512]{1,0:T(8,128)(2,1)S(1)} %fusion.6), channel_id=1, source_target_pairs={{0,4},{4,0},{8,12},{12,8},{16,20},{20,16},{24,28},{28,24},{1,5},{5... | collective-permute-start | bytes 196616 | tf_op jit(solution)/shard_map/ppermute | solution.py:486
  77.0 4.5 %collective-permute-start.16 = (f16[64,512]{1,0:T(8,128)(2,1)S(1)}, f16[64,512]{1,0:T(8,128)(2,1)S(1)}, u32[]{:S(2)}, u32[]{:S(2)}) collective-permute-start(f16[64,512]{1,0:T(8,128)(2,1)S(1)} %collective-permute-done.15), channel_id=1, source_target_pairs={{0,4},{4,0},{8,12},{12,8},{16,20},{20,16},{24,28},{28,24},{1,5},{5... | collective-permute-start | bytes 196616 | tf_op jit(solution)/shard_map/ppermute | solution.py:486
  78.5 4.3 %collective-permute-start.18 = (f16[64,512]{1,0:T(8,128)(2,1)S(1)}, f16[64,512]{1,0:T(8,128)(2,1)S(1)}, u32[]{:S(2)}, u32[]{:S(2)}) collective-permute-start(f16[64,512]{1,0:T(8,128)(2,1)S(1)} %collective-permute-done.17), channel_id=1, source_target_pairs={{0,4},{4,0},{8,12},{12,8},{16,20},{20,16},{24,28},{28,24},{1,5},{5... | collective-permute-start | bytes 196616 | tf_op jit(solution)/shard_map/ppermute | solution.py:486
  80.2 4.3 %collective-permute-start.20 = (f16[64,512]{1,0:T(8,128)(2,1)S(1)}, f16[64,512]{1,0:T(8,128)(2,1)S(1)}, u32[]{:S(2)}, u32[]{:S(2)}) collective-permute-start(f16[64,512]{1,0:T(8,128)(2,1)S(1)} %collective-permute-done.19), channel_id=1, source_target_pairs={{0,4},{4,0},{8,12},{12,8},{16,20},{20,16},{24,28},{28,24},{1,5},{5... | collective-permute-start | bytes 196616 | tf_op jit(solution)/shard_map/ppermute | solution.py:486
  84.5 1.0 %copy-start.7 = (f32[512,512]{1,0:T(8,128)}, f32[512,512]{1,0:T(8,128)S(1)}, u32[]{:S(2)}) copy-start(f32[512,512]{1,0:T(8,128)S(1)} %subtract_dynamic-update-slice_fusion) | copy-start | bytes 3145732
